TPU v7x, 256 devices: a whole 4x4x8 slice. The times are simulated.
256 devices in a mesh: tp: 8 (over x, core), ad: 32 (over y, z).
Axes of the slice: x: 4, y: 4, z: 8, core: 2. Of those that a mesh axis runs over, the one named last changes fastest.
Arguments:
- hidden: bfloat16 [14336, 8192], P('ad'), may hold values from -6 to 6
- gain: bfloat16 [8192], replicated, may hold values from 0.25 to 1.75
- key_value_weight: bfloat16 [8192, 2, 1024], P(None, None, 'tp'), may hold values from -0.0625 to 0.0625
- adapter_down_weight: bfloat16 [64, 8192, 128], P('ad', 'tp'), may hold values from -0.0625 to 0.0625
- adapter_up_weight: bfloat16 [64, 2, 64, 1024], P('ad', None, None, 'tp'), may hold values from -0.75 to 0.75
- language_pair_index: int32 [14336], P('ad'), may hold values from 0 to 63, as said below
- adapter_row_index: int32 [64], replicated, may hold values from 0 to 63, as said below
Outputs:
- kv_out: bfloat16 [14336, 2, 1024], P('ad', None, 'tp')
Inputs may be any that keep to these rules, and one draw needn't show every extreme that they name: A row's owner is adapter_row_index[language_pair_index] // 2. Among the rows of one device, one owner, the same for every device, has exactly 56 rows; every other owner has at most 28, and one other owner, the same for every device, exactly 28. `adapter_row_index`: each adapter's row in adapter_down_weight and adapter_up_weight; every row appears once.
All inputs are finite; a program needn't handle non-finite values.
Results may differ from a plain program's by a relative error of at most 0.0053.
Values may be sent and summed in bfloat16 or wider, within the bound.
No kernel may reach another device: no remote copies, remote signals or barrier semaphores. Data moves between devices by JAX's collectives and lax.ppermute only.
A program may use at most 128 MiB of HBM per device.

v0:
```python
import jax
import jax.numpy as jnp
from jax import lax
from jax.sharding import PartitionSpec as P

epsilon = 1e-05
adapter_scale = 0.5


def down_local(rows_in, row_ids, down_table):
    adapter_total = down_table.shape[0]
    labels = jnp.arange(adapter_total, dtype=jnp.int32)
    row_mask = row_ids[:, None] == labels[None, :]
    every_low = jnp.einsum("rc,acm->ram", rows_in, down_table, preferred_element_type=jnp.float32)
    partial_low = jnp.sum(jnp.where(row_mask[:, :, None], every_low, jnp.float32(0.0)), axis=1)
    return (partial_low, row_mask)


def upward_delta(summed_low, row_mask, up_table):
    narrow = summed_low.astype(jnp.bfloat16)
    row_total = narrow.shape[0]
    adapter_total = up_table.shape[0]
    rank_width = up_table.shape[2]
    widened = jnp.where(row_mask[:, :, None], narrow[:, None, :], jnp.zeros((), jnp.bfloat16))
    widened = widened.reshape(row_total, adapter_total, 2, rank_width)
    values = jnp.einsum("racq,acqh->rch", widened, up_table, preferred_element_type=jnp.float32)
    return values.astype(jnp.bfloat16)


def on_device(
    hidden,
    gain,
    key_value_weight,
    adapter_down_weight,
    adapter_up_weight,
    language_pair_index,
    adapter_row_index,
):
    tok_count = hidden.shape[0]
    model_width = hidden.shape[1]
    owner_count = lax.axis_size("ad")
    by_holder = adapter_down_weight.shape[0]
    column_portion = adapter_down_weight.shape[1]
    head_cols = key_value_weight.shape[2]
    row_quota = tok_count // owner_count
    wide_hidden = hidden.astype(jnp.float32)
    inv_rms = lax.rsqrt(jnp.mean(wide_hidden * wide_hidden, axis=-1, keepdims=True) + epsilon)
    normed = (wide_hidden * inv_rms * gain.astype(jnp.float32)).astype(jnp.bfloat16)
    base_projection = jnp.dot(
        normed,
        key_value_weight.reshape(model_width, 2 * head_cols),
        preferred_element_type=jnp.float32,
    ).reshape(tok_count, 2, head_cols)
    own_cols = lax.dynamic_slice_in_dim(
        normed, lax.axis_index("tp") * column_portion, column_portion, 1
    )
    slot_ids = adapter_row_index[language_pair_index]
    owner_ids = slot_ids // by_holder
    local_ids = slot_ids % by_holder
    owner_labels = jnp.arange(owner_count, dtype=jnp.int32)
    capacity = 4 * row_quota
    onehot = (owner_ids[:, None] == owner_labels[None, :]).astype(jnp.int32)
    before = jnp.cumsum(onehot, axis=0) - onehot
    bucket_pos = jnp.sum(before * onehot, axis=1)
    total_slots = owner_count * capacity
    dest_slot = jnp.where(owner_ids < owner_count, owner_ids * capacity + bucket_pos, total_slots)
    slot_labels = jnp.arange(total_slots, dtype=jnp.int32)
    selector = slot_labels[:, None] == dest_slot[None, :]
    selector_bf = selector.astype(jnp.bfloat16)
    send_rows = jnp.dot(selector_bf, own_cols, preferred_element_type=jnp.float32).astype(
        jnp.bfloat16
    )
    send_rows = send_rows.reshape(owner_count, capacity, column_portion)
    filled = jnp.any(selector, axis=1)
    picked_ids = jnp.sum(jnp.where(selector, local_ids[None, :], 0), axis=1)
    send_ids = jnp.where(filled, picked_ids, by_holder).reshape(owner_count, capacity)
    received_rows = lax.all_to_all(send_rows, "ad", split_axis=0, concat_axis=0, tiled=True)
    got_ids = lax.all_to_all(send_ids, "ad", split_axis=0, concat_axis=0, tiled=True)
    source_count = got_ids.shape[0]
    element_count = got_ids.shape[1]
    flat_ids = got_ids.reshape(source_count * element_count)
    partial_low, row_mask = down_local(
        received_rows.reshape(source_count * element_count, column_portion),
        flat_ids,
        adapter_down_weight,
    )
    summed_output = lax.psum(partial_low, "tp")
    delta_rows = upward_delta(summed_output, row_mask, adapter_up_weight).reshape(
        source_count, element_count, 2, head_cols
    )
    returned = lax.all_to_all(delta_rows, "ad", split_axis=0, concat_axis=0, tiled=True)
    flat_back = returned.reshape(total_slots, 2 * head_cols)
    back_rows = jnp.einsum("st,sc->tc", selector_bf, flat_back, preferred_element_type=jnp.float32)
    delta_by_row = back_rows.astype(jnp.bfloat16).reshape(tok_count, 2, head_cols)
    return (base_projection + adapter_scale * delta_by_row.astype(jnp.float32)).astype(jnp.bfloat16)


def solution(mesh):
    return jax.shard_map(
        on_device,
        mesh=mesh,
        in_specs=(
            P("ad", None),
            P(),
            P(None, None, "tp"),
            P("ad", "tp", None),
            P("ad", None, None, "tp"),
            P("ad"),
            P(),
        ),
        out_specs=P("ad", None, "tp"),
        check_vma=False,
    )
```

profile of v0, /device:TPU:6, one launch (start us, length us, event | category | flops | bytes accessed | tf_op | source)
XLA Modules:
  0.0 251.6 jit_solution(11058479754245148850)
XLA Ops:
  0.0 2.1 fusion.34
  2.1 2.1 fusion.35
  4.1 2.1 fusion.36
  6.2 1.6 fusion.37
  7.8 40.5 %add_select_fusion = (s32[448]{0:T(512)S(1)}, s32[448]{0:T(512)S(1)}) fusion(s32[]{:T(128)} %bitcast.66, s32[]{:T(128)} %bitcast.65, s32[]{:T(128)} %bitcast.64, s32[]{:T(128)} %bitcast.63, s32[]{:T(128)} %bitcast.62, s32[]{:T(128)} %bitcast.61, s32[]{:T(128)} %bitcast.60, s32[]{:T(128)} %bitcast.59, s32[]{:T(128)} %bitcast.58, s32[]{:T(128)} %bitcast.57, ...), kind=kLoop, calls=%fused_computation.46 | loop fusion | flops 62720 | bytes 5632 | tf_op jit(solution)/shard_map/jit(remainder)/select_n | solution.py:59
  48.4 1.2 reduce-window.6
  51.7 11.5 %all-to-all-start = ((s32[32,1,56]{2,1,0:T(1,128)}), s32[32,1,56]{2,1,0:T(1,128)S(1)}, u32[]{:S(2)}, u32[]{:S(2)}) async-start(s32[32,1,56]{2,1,0:T(1,128)} %select_n.72), calls=%async_computation | async-start | bytes 32768 | tf_op jit(solution)/shard_map/all_to_all | solution.py:78
  63.2 0.7 convert_element_type.37
  63.9 4.6 %fusion = f32[448]{0:T(512)S(1)} fusion(bf16[448,8192]{1,0:T(8,128)(2,1)} %param.7), kind=kLoop, calls=%fused_computation.2 | loop fusion | flops 11009600 | bytes 7341824 | tf_op jit(solution)/shard_map/reduce_sum | solution.py:47
  68.5 5.5 %fusion.2 = bf16[448,8192]{1,0:T(8,128)(2,1)S(1)} fusion(bf16[448,8192]{1,0:T(8,128)(2,1)} %param.7, f32[8192]{0:T(1024)S(1)} %convert_element_type.37, f32[448]{0:T(512)S(1)} %add_rsqrt_fusion), kind=kLoop, calls=%fused_computation.4 | loop fusion | flops 14680064 | bytes 14714624 | tf_op jit(solution)/shard_map/convert_element_type | solution.py:48
  74.1 3.0 %copy-done.1 = bf16[448,8192]{1,0:T(8,128)(2,1)} copy-done((bf16[448,8192]{1,0:T(8,128)(2,1)}, bf16[448,8192]{1,0:T(8,128)(2,1)S(1)}, u32[]{:S(2)}) %copy-start.1) | copy-done | bytes 7340056
  77.0 4.1 %convolution_convert_fusion = bf16[1792,1024]{1,0:T(8,128)(2,1)} fusion(s32[448]{0:T(512)S(1)} %add_select_fusion.2, bf16[448,8192]{1,0:T(8,128)(2,1)S(1)} %fusion.2, s32[]{:T(128)S(6)} %select_n.73), kind=kOutput, calls=%fused_computation.8 | convolution fusion | flops 1646804992 | bytes 4589572 | tf_op jit(solution)/shard_map/dot_general | solution.py:70
  81.2 9.9 %all-to-all-start.1 = ((bf16[32,56,1024]{2,1,0:T(8,128)(2,1)}), bf16[32,56,1024]{2,1,0:T(8,128)(2,1)}, u32[]{:S(2)}, u32[]{:S(2)}) async-start(bf16[32,56,1024]{2,1,0:T(8,128)(2,1)} %bitcast.119), calls=%async_computation.1 | async-start | bytes 7340032 | tf_op jit(solution)/shard_map/all_to_all | solution.py:77
  92.4 84.1 %all-to-all-done.1 = bf16[32,56,1024]{2,1,0:T(8,128)(2,1)} async-done(((bf16[32,56,1024]{2,1,0:T(8,128)(2,1)}), bf16[32,56,1024]{2,1,0:T(8,128)(2,1)}, u32[]{:S(2)}, u32[]{:S(2)}) %all-to-all-start.1) | async-done | bytes 3670048 | tf_op jit(solution)/shard_map/all_to_all | solution.py:77
  176.5 3.2 %fusion.10 = f32[1792,128]{1,0:T(8,128)S(1)} fusion(bf16[1792,1024,1]{1,0,2:T(8,128)(2,1)} %bitcast.70, bf16[2,1024,128]{2,1,0:T(8,128)(2,1)S(1)} %copy-done, pred[1792,2]{0,1:T(4,128)(4,1)S(1)} %iota_compare_fusion.13), kind=kOutput, calls=%fused_computation.18 | convolution fusion | flops 940212224 | bytes 5115392 | tf_op jit(solution)/shard_map/rc,acm->ram/dot_general | solution.py:14
  179.7 28.7 %all-reduce.2 = bf16[1792,128]{1,0:T(8,128)(2,1)S(1)} all-reduce(f32[1792,128]{1,0:T(8,128)S(1)} %fusion.10), channel_id=1, replica_groups=mesh['tp'=8,'ad'=32] {'tp'}, use_global_device_ids=true, to_apply=%region_7.8 | all-reduce | flops 229376 | bytes 1376256 | tf_op jit(solution)/shard_map/psum | solution.py:87
  209.1 1.9 copy.39
  211.0 6.2 %all-to-all-start.2 = ((bf16[32,56,2,128]{3,2,1,0:T(2,128)(2,1)}), bf16[32,56,2,128]{3,2,1,0:T(2,128)(2,1)S(1)}, u32[]{:S(2)}, u32[]{:S(2)}) async-start(bf16[32,56,2,128]{3,2,1,0:T(2,128)(2,1)} %copy.39), calls=%async_computation.2 | async-start | bytes 1835008 | tf_op jit(solution)/shard_map/all_to_all | solution.py:91
  217.2 4.8 %copy.58 = bf16[1024,8,2,128]{3,1,2,0:T(8,128)(2,1)} copy(bf16[1024,8,2,128]{3,2,1,0:T(2,128)(2,1)} %bitcast.117) | data formatting | bytes 8388608
  222.0 6.4 %copy.34 = bf16[256,8192]{1,0:T(8,128)(2,1)} copy(bf16[256,8192]{0,1:T(8,128)(2,1)} %bitcast.116) | data formatting | bytes 8388608 | tf_op jit(solution)/shard_map/dot_general | solution.py:49
  228.4 15.2 %all-to-all-done.2 = bf16[32,56,2,128]{3,2,1,0:T(2,128)(2,1)S(1)} async-done(((bf16[32,56,2,128]{3,2,1,0:T(2,128)(2,1)}), bf16[32,56,2,128]{3,2,1,0:T(2,128)(2,1)S(1)}, u32[]{:S(2)}, u32[]{:S(2)}) %all-to-all-start.2) | async-done | bytes 917536 | tf_op jit(solution)/shard_map/all_to_all | solution.py:91
  243.5 0.7 fusion.17
  244.3 6.4 %fusion.18 = bf16[448,2,128]{2,0,1:T(8,128)(2,1)S(1)} fusion(bf16[2,128,8192]{2,1,0:T(8,128)(2,1)} %bitcast.118, bf16[448,8192]{1,0:T(8,128)(2,1)} %copy-done.1, f32[56,2,8,128]{3,2,1,0:T(8,128)S(1)} %fusion.17), kind=kOutput, calls=%fused_computation.24 | convolution fusion | flops 1879277568 | bytes 12222464 | tf_op jit(solution)/shard_map/dot_general | solution.py:49
  250.7 0.9 copy.41
  (26 shorter events, 4.1 us)
Async XLA Ops:
  0.0 176.5 %copy-start = (bf16[2,1024,128]{2,1,0:T(8,128)(2,1)S(1)}, bf16[2,1024,128]{2,1,0:T(8,128)(2,1)}, u32[]{:S(2)}) copy-start(bf16[2,1024,128]{2,1,0:T(8,128)(2,1)} %param.10) | copy-start | bytes 1572868
  51.7 29.5 %all-to-all-start = ((s32[32,1,56]{2,1,0:T(1,128)}), s32[32,1,56]{2,1,0:T(1,128)S(1)}, u32[]{:S(2)}, u32[]{:S(2)}) async-start(s32[32,1,56]{2,1,0:T(1,128)} %select_n.72), calls=%async_computation | async-start | bytes 32768 | tf_op jit(solution)/shard_map/all_to_all | solution.py:78
  74.1 3.0 %copy-start.1 = (bf16[448,8192]{1,0:T(8,128)(2,1)}, bf16[448,8192]{1,0:T(8,128)(2,1)S(1)}, u32[]{:S(2)}) copy-start(bf16[448,8192]{1,0:T(8,128)(2,1)S(1)} %fusion.2) | copy-start | bytes 22020100
  81.2 95.3 %all-to-all-start.1 = ((bf16[32,56,1024]{2,1,0:T(8,128)(2,1)}), bf16[32,56,1024]{2,1,0:T(8,128)(2,1)}, u32[]{:S(2)}, u32[]{:S(2)}) async-start(bf16[32,56,1024]{2,1,0:T(8,128)(2,1)} %bitcast.119), calls=%async_computation.1 | async-start | bytes 7340032 | tf_op jit(solution)/shard_map/all_to_all | solution.py:77
  176.5 32.1 %copy-start.2 = (bf16[2,2,64,128]{3,2,1,0:T(8,128)(2,1)S(1)}, bf16[2,2,64,128]{3,2,1,0:T(8,128)(2,1)}, u32[]{:S(2)}) copy-start(bf16[2,2,64,128]{3,2,1,0:T(8,128)(2,1)} %param.11) | copy-start | bytes 196612
  211.0 32.6 %all-to-all-start.2 = ((bf16[32,56,2,128]{3,2,1,0:T(2,128)(2,1)}), bf16[32,56,2,128]{3,2,1,0:T(2,128)(2,1)S(1)}, u32[]{:S(2)}, u32[]{:S(2)}) async-start(bf16[32,56,2,128]{3,2,1,0:T(2,128)(2,1)} %copy.39), calls=%async_computation.2 | async-start | bytes 1835008 | tf_op jit(solution)/shard_map/all_to_all | solution.py:91
where the time goes:
time: 253 us; the launch traced here: 252 us
  waiting for transfers between devices  99.2 us (39%)
  other arithmetic  54.5 us (22%)
  blocking collectives  28.7 us (11%)
  starting transfers between devices  27.6 us (11%)
  local copies, waits for them, and re-layouts  26.5 us (10%)
  matrix products  14.9 us (6%)
    all_to_all x1, waiting for transfers between devices, on_device(): lax.all_to_all(send_rows, 'ad', split_axis=0, concat_axis=0, tiled=True)  84.1 us
    select_n x1, other arithmetic, on_device(): local_ids = slot_ids % by_holder  40.5 us
    psum x1, blocking collectives, on_device(): summed_output = lax.psum(partial_low, 'tp')  28.7 us
    all_to_all x1, waiting for transfers between devices, on_device(): lax.all_to_all(delta_rows, 'ad', split_axis=0, concat_axis=0, tiled=True)  15.2 us
    all_to_all x1, starting transfers between devices, on_device(): lax.all_to_all(send_ids, 'ad', split_axis=0, concat_axis=0, tiled=True)  11.5 us
    all_to_all x1, starting transfers between devices, on_device(): lax.all_to_all(send_rows, 'ad', split_axis=0, concat_axis=0, tiled=True)  9.9 us
    gather x4, local copies, waits for them, and re-layouts, on_device(): slot_ids = adapter_row_index[language_pair_index]  7.79 us
    unnamed x7, local copies, waits for them, and re-layouts  7.74 us
  transfers between devices with their start and end apart: 3, of which 2 were waited for; matrix products, arithmetic and copies ran while one was open for 11% of the time, Pallas kernels for 0%

commit v1 on v0

v1 whole, which is shorter than its diff:
```python
import jax
import jax.numpy as jnp
from jax import lax
from jax.experimental import pallas as pl
from jax.experimental.pallas import tpu as pltpu
from jax.sharding import Mesh, PartitionSpec as P


epsilon = 1e-05
adapter_scale = 0.5
F32 = jnp.float32
BF16 = jnp.bfloat16

TOK = 448
DIM = 8192
COLS = 1024
CAP = 28
BLOCK = 32
NZ = 8
NY = 4
BUCKETS = NZ + 1
SLOTS = BUCKETS * BLOCK
EARLY = 7
LATE = BUCKETS - EARLY
ORDER = (0, 7, 1, 6, 2, 5, 3, 4)
RANK2 = 128
VMEM_LIMIT = 24 * 1024 * 1024


def iota(shape, axis):
    return lax.broadcasted_iota(jnp.int32, shape, axis).astype(F32)


def to_column(row, count):
    same = iota((count, count), 0) == iota((count, count), 1)
    return jnp.sum(jnp.where(same, row, 0.0), axis=1, keepdims=True)


def params():
    return pltpu.CompilerParams(vmem_limit_bytes=VMEM_LIMIT)


def whole():
    return pl.BlockSpec(memory_space=pltpu.VMEM)


def scalars():
    return pl.BlockSpec(memory_space=pltpu.SMEM)


def gain_row(gain):
    wide = gain.astype(F32)
    return jnp.concatenate([wide[i : i + 1] for i in range(8)], axis=1)


def dispatch_kernel(place_ref, hidden_ref, gain_ref, pair_ref, table_ref, *outs):
    sends = outs[:NY]
    dst_ref, hot_ref = outs[NY:]
    own = (hidden_ref[...].astype(F32) * gain_row(gain_ref[...])).astype(BF16)
    y_me = place_ref[1].astype(F32)
    z_me = place_ref[2].astype(F32)
    count = table_ref.shape[1]
    pair = pair_ref[...].astype(F32)
    table = to_column(table_ref[...].astype(F32), count)
    slot = jnp.sum(jnp.where(iota((count, TOK), 0) == pair, table, 0.0), axis=0, keepdims=True)
    owner = jnp.floor(slot * 0.5)
    local = slot - 2.0 * owner
    same = to_column(owner, TOK) == owner
    before = iota((TOK, TOK), 0) < iota((TOK, TOK), 1)
    pos = jnp.sum(jnp.where(same & before, 1.0, 0.0), axis=0, keepdims=True)
    y_to = jnp.floor(owner * (1.0 / NZ))
    dy = y_to - y_me
    dy = jnp.where(dy < 0, dy + NY, dy)
    dz = owner - NZ * y_to - z_me
    dz = jnp.where(dz < 0, dz + NZ, dz)
    rank = jnp.where(dz == 4, 7.0, jnp.where(dz < 4, 2.0 * dz, 15.0 - 2.0 * dz))
    over = pos >= CAP
    bucket = dy * BUCKETS + jnp.where(over, float(NZ), rank)
    place = jnp.where(over, pos - CAP, pos)
    dst = bucket * BLOCK + place
    dst_ref[...] = jnp.broadcast_to(to_column(dst, TOK), (TOK, 128))
    hot_ref[0] = jnp.max(jnp.where(over, rank, -1.0)).astype(jnp.int32)
    spot = jnp.where(iota((TOK, 128), 1) == to_column(place, TOK), 1.0, 0.0).astype(BF16)
    for part in range(NY):
        pick = jnp.where(iota((SLOTS, TOK), 0) + part * SLOTS == dst, 1.0, 0.0).astype(BF16)
        rows = jnp.dot(pick, own, preferred_element_type=F32).astype(BF16)
        sends[part][...] = rows.reshape(BUCKETS, BLOCK, COLS)
        marks = jnp.where(iota((16, TOK), 0) + part * BUCKETS == bucket, local, 0.0).astype(BF16)
        ids = jnp.dot(marks, spot, preferred_element_type=F32)
        for b in range(BUCKETS):
            head = rows[b * BLOCK : (b + 1) * BLOCK, :128].astype(F32)
            head = jnp.where(iota((BLOCK, 128), 0) == CAP, ids[b : b + 1], head)
            sends[part][b, :, pl.ds(0, 128)] = head.astype(BF16)


def dispatch(place, hidden, gain, pair, table):
    message = jax.ShapeDtypeStruct((BUCKETS, BLOCK, COLS), BF16)
    out = pl.pallas_call(
        dispatch_kernel,
        grid_spec=pltpu.PrefetchScalarGridSpec(
            num_scalar_prefetch=1,
            grid=(1,),
            in_specs=[
                pl.BlockSpec((TOK, COLS), lambda i, p: (0, p[0])),
                pl.BlockSpec((8, 128), lambda i, p: (p[0], 0)),
                pl.BlockSpec((1, TOK), lambda i, p: (0, 0)),
                pl.BlockSpec((1, table.shape[1]), lambda i, p: (0, 0)),
            ],
            out_specs=[pl.BlockSpec((BUCKETS, BLOCK, COLS), lambda i, p: (0, 0, 0))] * NY
            + [pl.BlockSpec((TOK, 128), lambda i, p: (0, 0)), scalars()],
        ),
        out_shape=[message] * NY
        + [jax.ShapeDtypeStruct((TOK, 128), F32), jax.ShapeDtypeStruct((1,), jnp.int32)],
        cost_estimate=pl.CostEstimate(
            flops=2 * NY * SLOTS * TOK * COLS, bytes_accessed=4_000_000, transcendentals=0
        ),
        name="dispatch",
    )(place, hidden, gain, pair, table)
    return out[:NY], out[NY], out[NY + 1]


def base_kernel(hidden_ref, gain_ref, weight_ref, out_ref, inv_ref, square_ref):
    step = pl.program_id(0)
    wide = hidden_ref[...].astype(F32)
    scaled = (wide * gain_row(gain_ref[...])).astype(BF16)
    weight = jnp.concatenate([weight_ref[0], weight_ref[1]], axis=1)
    term = jnp.dot(scaled, weight, preferred_element_type=F32)
    lanes = sum(
        wide[:, c : c + 128] * wide[:, c : c + 128] for c in range(0, wide.shape[1], 128)
    )

    @pl.when(step == 0)
    def _():
        out_ref[...] = term
        square_ref[...] = lanes

    @pl.when(step > 0)
    def _():
        out_ref[...] += term
        square_ref[...] += lanes

    @pl.when(step == pl.num_programs(0) - 1)
    def _():
        mean = jnp.sum(square_ref[...], axis=1, keepdims=True) * (1.0 / DIM)
        inv = lax.rsqrt(mean + epsilon)
        out_ref[...] = out_ref[...] * inv
        inv_ref[...] = jnp.broadcast_to(inv, (TOK, 128))


def base_projection(hidden, gain, weight):
    tile = 1024
    return pl.pallas_call(
        base_kernel,
        grid=(DIM // tile,),
        in_specs=[
            pl.BlockSpec((TOK, tile), lambda k: (0, k)),
            pl.BlockSpec((8, 128), lambda k: (k, 0)),
            pl.BlockSpec((2, tile, 128), lambda k: (0, k, 0)),
        ],
        out_specs=[
            pl.BlockSpec((TOK, 256), lambda k: (0, 0)),
            pl.BlockSpec((TOK, 128), lambda k: (0, 0)),
        ],
        out_shape=[
            jax.ShapeDtypeStruct((TOK, 256), F32),
            jax.ShapeDtypeStruct((TOK, 128), F32),
        ],
        scratch_shapes=[pltpu.VMEM((TOK, 128), F32)],
        cost_estimate=pl.CostEstimate(
            flops=2 * TOK * DIM * 256, bytes_accessed=12_000_000, transcendentals=0
        ),
        name="base",
    )(hidden, gain, weight)


def local_column(head):
    row = head[CAP : CAP + 1, :].astype(F32)
    same = iota((BLOCK, 128), 0) == iota((BLOCK, 128), 1)
    return jnp.sum(jnp.where(same, row, 0.0), axis=1, keepdims=True)


def bucket_rows(received, b):
    rows = jnp.concatenate([r[b] for r in received], axis=0)
    local = jnp.concatenate([local_column(r[b, :, :128]) for r in received], axis=0)
    return rows, local


def project(rows, local, weight):
    both = jnp.dot(rows, weight, preferred_element_type=F32)
    return jnp.where(local < 0.5, both[:, :RANK2], both[:, RANK2:])


def down_early_kernel(place_ref, hot_ref, *refs):
    received = refs[:NY]
    chunks = refs[NY : NY + EARLY]
    mine_ref, other_ref, more_ref, low_ref = refs[NY + EARLY :]
    more_ref[...] = jnp.zeros_like(more_ref)
    for k in range(EARLY):
        c = chunks[k]
        weight = jnp.concatenate([c[0, :COLS], c[1, :COLS]], axis=1)
        rows, local = bucket_rows(received, k)
        low_ref[k * NY * BLOCK : (k + 1) * NY * BLOCK] = project(rows, local, weight).astype(BF16)

        @pl.when(hot_ref[0] == k)
        def _():
            rows, local = bucket_rows(received, NZ)
            more_ref[...] = project(rows, local, weight).astype(BF16)

    size = EARLY * NY * BLOCK // 2
    first = pl.multiple_of(place_ref[3] * size, size)
    second = pl.multiple_of(size - place_ref[3] * size, size)
    mine_ref[...] = low_ref[pl.ds(first, size), :]
    other_ref[...] = low_ref[pl.ds(second, size), :]


def down_early(place, hot, received, chunks):
    size = EARLY * NY * BLOCK // 2
    return pl.pallas_call(
        down_early_kernel,
        in_specs=[scalars(), scalars()] + [whole()] * (NY + EARLY),
        out_specs=[whole()] * 3,
        out_shape=[
            jax.ShapeDtypeStruct((size, RANK2), BF16),
            jax.ShapeDtypeStruct((size, RANK2), BF16),
            jax.ShapeDtypeStruct((NY * BLOCK, RANK2), BF16),
        ],
        scratch_shapes=[pltpu.VMEM((2 * size, RANK2), BF16)],
        compiler_params=params(),
        cost_estimate=pl.CostEstimate(
            flops=2 * EARLY * 128 * 1024 * 256, bytes_accessed=6_000_000, transcendentals=0
        ),
        name="down_early",
    )(place, hot, *received, *chunks)


def down_late_kernel(hot_ref, *refs):
    received = refs[:NY]
    zero, one, more_ref, low_ref = refs[NY:]
    weight = jnp.concatenate([zero[0, :COLS], one[0, :COLS]], axis=1)
    rows, local = bucket_rows(received, EARLY)
    low_ref[0] = project(rows, local, weight).astype(BF16)
    low_ref[1] = more_ref[...]

    @pl.when(hot_ref[0] == EARLY)
    def _():
        rows, local = bucket_rows(received, NZ)
        low_ref[1] = project(rows, local, weight).astype(BF16)


def down_late(hot, received, chunks, more):
    return pl.pallas_call(
        down_late_kernel,
        in_specs=[scalars()] + [whole()] * (NY + 3),
        out_specs=whole(),
        out_shape=jax.ShapeDtypeStruct((LATE, NY * BLOCK, RANK2), BF16),
        compiler_params=params(),
        cost_estimate=pl.CostEstimate(
            flops=2 * 256 * 1024 * 256, bytes_accessed=1_000_000, transcendentals=0
        ),
        name="down_late",
    )(hot, *received, *chunks, more)


def spread(low, local):
    zero = jnp.zeros_like(low)
    return jnp.concatenate(
        [jnp.where(local < 0.5, low, zero), jnp.where(local < 0.5, zero, low)], axis=1
    ).astype(BF16)


def up_matrix(up):
    key_row = (lax.broadcasted_iota(jnp.int32, (2 * RANK2, 128), 0) % RANK2) < RANK2 // 2
    up = up.astype(F32)
    return jnp.concatenate(
        [jnp.where(key_row, up, 0.0), jnp.where(key_row, 0.0, up)], axis=1
    ).astype(BF16)


def up_rows(chunk):
    return jnp.concatenate([chunk[0, COLS:], chunk[1, COLS:]], axis=0)


def up_early_kernel(place_ref, half_ref, theirs_ref, *refs):
    received = refs[:NY]
    chunks = refs[NY : NY + EARLY]
    outs = refs[NY + EARLY : -1]
    low_ref = refs[-1]
    size = EARLY * NY * BLOCK // 2
    first = pl.multiple_of(place_ref[3] * size, size)
    second = pl.multiple_of(size - place_ref[3] * size, size)
    low_ref[pl.ds(first, size), :] = half_ref[...]
    low_ref[pl.ds(second, size), :] = theirs_ref[...]
    for k in range(EARLY):
        local = jnp.concatenate([local_column(r[k, :, :128]) for r in received], axis=0)
        low = low_ref[k * NY * BLOCK : (k + 1) * NY * BLOCK, :].astype(F32)
        delta = jnp.dot(
            spread(low, local), up_matrix(up_rows(chunks[k])), preferred_element_type=F32
        ).astype(BF16)
        for s in range(NY):
            outs[s][k] = delta[s * BLOCK : (s + 1) * BLOCK]


def up_early(place, half, theirs, received, chunks):
    return pl.pallas_call(
        up_early_kernel,
        in_specs=[scalars()] + [whole()] * (2 + NY + EARLY),
        out_specs=[whole()] * NY,
        out_shape=[jax.ShapeDtypeStruct((EARLY, BLOCK, 256), BF16)] * NY,
        scratch_shapes=[pltpu.VMEM((EARLY * NY * BLOCK, RANK2), BF16)],
        compiler_params=params(),
        cost_estimate=pl.CostEstimate(
            flops=2 * EARLY * 128 * 256 * 256, bytes_accessed=1_500_000, transcendentals=0
        ),
        name="up_early",
    )(place, half, theirs, *received, *chunks)


def up_late_kernel(hot_ref, low_ref, *refs):
    received = refs[:NY]
    chunks = refs[NY : NY + EARLY]
    zero, one = refs[NY + EARLY : NY + EARLY + 2]
    outs = refs[NY + EARLY + 2 :]
    last = jnp.concatenate([zero[0, COLS:], one[0, COLS:]], axis=0)
    hot_up = last.astype(F32)
    for k in range(EARLY):
        hot_up = jnp.where(hot_ref[0] == k, up_rows(chunks[k]).astype(F32), hot_up)
    for at, up in ((0, last), (1, hot_up)):
        local = jnp.concatenate([local_column(r[EARLY + at, :, :128]) for r in received], axis=0)
        delta = jnp.dot(
            spread(low_ref[at].astype(F32), local), up_matrix(up), preferred_element_type=F32
        ).astype(BF16)
        for s in range(NY):
            outs[s][at] = delta[s * BLOCK : (s + 1) * BLOCK]


def up_late(hot, low, received, chunks, last):
    return pl.pallas_call(
        up_late_kernel,
        in_specs=[scalars()] + [whole()] * (1 + NY + EARLY + 2),
        out_specs=[whole()] * NY,
        out_shape=[jax.ShapeDtypeStruct((LATE, BLOCK, 256), BF16)] * NY,
        compiler_params=params(),
        cost_estimate=pl.CostEstimate(
            flops=2 * 2 * 128 * 256 * 256, bytes_accessed=1_000_000, transcendentals=0
        ),
        name="up_late",
    )(hot, low, *received, *chunks, *last)


def collect(dst, first, count, back):
    total = jnp.zeros((TOK, 256), F32)
    for part in range(NY):
        size = count * BLOCK
        at = iota((TOK, size), 1) + (part * SLOTS + first * BLOCK)
        pick = jnp.where(at == dst, 1.0, 0.0).astype(BF16)
        total = total + jnp.dot(
            pick, back[part][...].reshape(size, 256), preferred_element_type=F32
        )
    return total


def finish_early_kernel(base_ref, inv_ref, dst_ref, *refs):
    total = collect(dst_ref[:, :1], 0, EARLY, refs[:NY])
    refs[NY][...] = base_ref[...] + (adapter_scale * inv_ref[:, :1]) * total


def finish_late_kernel(sum_ref, inv_ref, dst_ref, *refs):
    total = collect(dst_ref[:, :1], EARLY, LATE, refs[:NY])
    refs[NY][...] = (sum_ref[...] + (adapter_scale * inv_ref[:, :1]) * total).astype(BF16)


def finish(kernel, start, inv, dst, back, kind):
    return pl.pallas_call(
        kernel,
        in_specs=[whole()] * (3 + NY),
        out_specs=whole(),
        out_shape=jax.ShapeDtypeStruct((TOK, 256), kind),
        compiler_params=params(),
        cost_estimate=pl.CostEstimate(
            flops=2 * TOK * 1024 * 256, bytes_accessed=1_500_000, transcendentals=0
        ),
    )(start, inv, dst, *back)


def shift(x, axis, size, by):
    return lax.ppermute(x, axis, [(i, (i + by) % size) for i in range(size)])


def on_device(hidden, gain, kv_weight, down_weight, up_weight, pair_index, row_index):
    tp = lax.axis_index("x") * 2 + lax.axis_index("core")
    places = [tp, lax.axis_index("y"), lax.axis_index("z"), lax.axis_index("core")]
    place = jnp.stack(places).astype(jnp.int32)

    own = jnp.concatenate([down_weight, up_weight.reshape(2, RANK2, 128)], axis=1)
    chunks = {0: own}
    plus = minus = own
    for k in range(1, 4):
        plus = shift(plus, "z", NZ, 1)
        minus = shift(minus, "z", NZ, -1)
        chunks[NZ - k] = plus
        chunks[k] = minus
    last = [shift(plus[:1], "z", NZ, 1), shift(minus[1:], "z", NZ, -1)]
    early = [chunks[dz] for dz in ORDER[:EARLY]]

    gains = gain.reshape(DIM // 128, 128)
    send, dst, hot = dispatch(
        place, hidden, gains, pair_index.reshape(1, TOK), row_index.reshape(1, -1)
    )
    received = [send[0]] + [shift(send[dy], "y", NY, dy) for dy in range(1, NY)]

    base, inv = base_projection(hidden, gains, kv_weight.transpose(1, 0, 2))

    mine, other, more = down_early(place, hot, received, early)
    got = shift(other, "core", 2, 1)
    chip = (mine.astype(F32) + got.astype(F32)).astype(BF16)
    total = chip.astype(F32)
    for k in range(1, 4):
        total = total + shift(chip, "x", 4, k).astype(F32)
    half = total.astype(BF16)
    theirs = shift(half, "core", 2, 1)
    delta = up_early(place, half, theirs, received, early)
    back = [delta[0]] + [shift(delta[dy], "y", NY, -dy) for dy in range(1, NY)]
    summed = finish(finish_early_kernel, base, inv, dst, back, F32)

    low = down_late(hot, received, last, more)
    chip = (low.astype(F32) + shift(low, "core", 2, 1).astype(F32)).astype(BF16)
    total = chip.astype(F32)
    for k in range(1, 4):
        total = total + shift(chip, "x", 4, k).astype(F32)
    delta = up_late(hot, total.astype(BF16), received, early, last)
    back = [delta[0]] + [shift(delta[dy], "y", NY, -dy) for dy in range(1, NY)]
    out = finish(finish_late_kernel, summed, inv, dst, back, BF16)
    return out.reshape(TOK, 2, 128)


def solution(mesh):
    split = Mesh(mesh.devices.reshape(4, 2, NY, NZ), ("x", "core", "y", "z"))
    tp = ("x", "core")
    ad = ("y", "z")
    return jax.shard_map(
        on_device,
        mesh=split,
        in_specs=(
            P(ad, None),
            P(),
            P(None, None, tp),
            P(ad, tp, None),
            P(ad, None, None, tp),
            P(ad),
            P(),
        ),
        out_specs=P(ad, None, tp),
        check_vma=False,
    )
```

time: 253 us -> 110 us (0.43)
  the two profiles are of different devices: /device:TPU:6 before, /device:TPU:8 now
where the time goes in v1:
time: 110 us; the launch traced here: 109 us
  starting transfers between devices  41.2 us (37%)
  waiting for transfers between devices  37 us (34%)
  Pallas kernels  22.8 us (21%)
  local copies, waits for them, and re-layouts  6.33 us (6%)
  other arithmetic  1.84 us (2%)
    ppermute x26, starting transfers between devices, shift(): return lax.ppermute(x, axis, [(i, (i + by) % size) for i in range(size)])  41.2 us
    ppermute x26, waiting for transfers between devices, shift(): return lax.ppermute(x, axis, [(i, (i + by) % size) for i in range(size)])  37 us
    pallas_call x1, Pallas kernels, base_projection(): pl.pallas_call(base_kernel, grid=(DIM // tile,), in_specs=[pl.BlockSpec((...  9.21 us
    unnamed x15, local copies, waits for them, and re-layouts  5.54 us
    pallas_call x1, Pallas kernels, dispatch(): pl.pallas_call(dispatch_kernel, grid_spec=pltpu.PrefetchScalarGridSpec(nu...  5.12 us
    pallas_call x1, Pallas kernels, down_early(): pl.pallas_call(down_early_kernel, in_specs=[scalars(), scalars()] + [whol...  3.3 us
  transfers between devices with their start and end apart: 26, of which 7 were waited for; matrix products, arithmetic and copies ran while one was open for 3% of the time, Pallas kernels for 17%

profile of v1, /device:TPU:8, one launch (start us, length us, event | category | flops | bytes accessed | tf_op | source)
XLA Modules:
  0.0 109.4 jit_solution(6691372376041493452)
XLA Ops:
  1.1 2.0 %collective-permute-start.3 = (bf16[2,1152,128]{2,1,0:T(8,128)(2,1)S(1)}, bf16[2,1152,128]{2,1,0:T(8,128)(2,1)S(1)}, u32[]{:S(2)}, u32[]{:S(2)}) collective-permute-start(bf16[2,1152,128]{2,1,0:T(8,128)(2,1)S(1)} %pad_maximum_fusion.refs_4_), channel_id=1, source_target_pairs={{0,1},{1,2},{2,3},{3,4},{4,5},{5,6},{6,7},{7,0},{8,9},{9,10},{10,1... | collective-permute-start | bytes 1769480 | tf_op jit(solution)/shard_map/ppermute | solution.py:386
  3.1 4.0 %collective-permute-start.4 = (bf16[2,1152,128]{2,1,0:T(8,128)(2,1)S(1)}, bf16[2,1152,128]{2,1,0:T(8,128)(2,1)S(1)}, u32[]{:S(2)}, u32[]{:S(2)}) collective-permute-start(bf16[2,1152,128]{2,1,0:T(8,128)(2,1)S(1)} %pad_maximum_fusion.refs_4_), channel_id=1, source_target_pairs={{0,7},{1,0},{2,1},{3,2},{4,3},{5,4},{6,5},{7,6},{8,15},{9,8},{10,9... | collective-permute-start | bytes 1769480 | tf_op jit(solution)/shard_map/ppermute | solution.py:386
  7.1 13.2 %collective-permute-done.3.refs_5_ = bf16[2,1152,128]{2,1,0:T(8,128)(2,1)S(1)} collective-permute-done((bf16[2,1152,128]{2,1,0:T(8,128)(2,1)S(1)}, bf16[2,1152,128]{2,1,0:T(8,128)(2,1)S(1)}, u32[]{:S(2)}, u32[]{:S(2)}) %collective-permute-start.3) | collective-permute-done | bytes 589856 | tf_op jit(solution)/shard_map/ppermute | solution.py:386
  20.4 3.2 %collective-permute-start.6 = (bf16[2,1152,128]{2,1,0:T(8,128)(2,1)S(1)}, bf16[2,1152,128]{2,1,0:T(8,128)(2,1)S(1)}, u32[]{:S(2)}, u32[]{:S(2)}) collective-permute-start(bf16[2,1152,128]{2,1,0:T(8,128)(2,1)S(1)} %collective-permute-done.4.refs_6_), channel_id=1, source_target_pairs={{0,7},{1,0},{2,1},{3,2},{4,3},{5,4},{6,5},{7,6},{8,15},{9,8},{10,9... | collective-permute-start | bytes 1769480 | tf_op jit(solution)/shard_map/ppermute | solution.py:386
  24.2 5.1 %dispatch.1 = (bf16[9,32,1024]{2,1,0:T(8,128)(2,1)}, bf16[9,32,1024]{2,1,0:T(8,128)(2,1)}, bf16[9,32,1024]{2,1,0:T(8,128)(2,1)}, bf16[9,32,1024]{2,1,0:T(8,128)(2,1)}, f32[448,128]{1,0:T(8,128)}, /*index=5*/s32[1]{0:T(128)}) custom-call(s32[4]{0:T(128)} %pad_add_fusion.place_ref, bf16[448,8192]{1,0:T(8,128)(2,1)} %hidden_ref.3, bf16[64,128]{1,0:T(8,128)(2,1)} %bitcast.12, ...), custom_call_target="tpu_custom_call" | custom-call | flops 1056964608 | bytes 4000000 | tf_op jit(solution)/shard_map/dispatch/pallas_call | solution.py:98
  29.3 1.7 %collective-permute-start = (bf16[9,32,1024]{2,1,0:T(8,128)(2,1)}, bf16[9,32,1024]{2,1,0:T(8,128)(2,1)S(1)}, u32[]{:S(2)}, u32[]{:S(2)}) collective-permute-start(bf16[9,32,1024]{2,1,0:T(8,128)(2,1)} %get-tuple-element.29), channel_id=1, source_target_pairs={{0,8},{8,16},{16,24},{24,0},{1,9},{9,17},{17,25},{25,1},{2,10},{10... | collective-permute-start | bytes 1769480 | tf_op jit(solution)/shard_map/ppermute | solution.py:386
  31.9 2.4 %collective-permute-start.2 = (bf16[9,32,1024]{2,1,0:T(8,128)(2,1)}, bf16[9,32,1024]{2,1,0:T(8,128)(2,1)S(1)}, u32[]{:S(2)}, u32[]{:S(2)}) collective-permute-start(bf16[9,32,1024]{2,1,0:T(8,128)(2,1)} %get-tuple-element.31), channel_id=1, source_target_pairs={{0,24},{8,0},{16,8},{24,16},{1,25},{9,1},{17,9},{25,17},{2,26},{10... | collective-permute-start | bytes 1769480 | tf_op jit(solution)/shard_map/ppermute | solution.py:386
  34.3 1.8 %collective-permute-done.5.refs_7_ = bf16[2,1152,128]{2,1,0:T(8,128)(2,1)S(1)} collective-permute-done((bf16[2,1152,128]{2,1,0:T(8,128)(2,1)S(1)}, bf16[2,1152,128]{2,1,0:T(8,128)(2,1)S(1)}, u32[]{:S(2)}, u32[]{:S(2)}) %collective-permute-start.5) | collective-permute-done | bytes 589856 | tf_op jit(solution)/shard_map/ppermute | solution.py:386
  36.1 3.2 %collective-permute-start.8 = (bf16[2,1152,128]{2,1,0:T(8,128)(2,1)S(1)}, bf16[2,1152,128]{2,1,0:T(8,128)(2,1)S(1)}, u32[]{:S(2)}, u32[]{:S(2)}) collective-permute-start(bf16[2,1152,128]{2,1,0:T(8,128)(2,1)S(1)} %collective-permute-done.6.refs_8_), channel_id=1, source_target_pairs={{0,7},{1,0},{2,1},{3,2},{4,3},{5,4},{6,5},{7,6},{8,15},{9,8},{10,9... | collective-permute-start | bytes 1769480 | tf_op jit(solution)/shard_map/ppermute | solution.py:386
  39.3 6.5 %collective-permute-done.refs_1_ = bf16[9,32,1024]{2,1,0:T(8,128)(2,1)S(1)} collective-permute-done((bf16[9,32,1024]{2,1,0:T(8,128)(2,1)}, bf16[9,32,1024]{2,1,0:T(8,128)(2,1)S(1)}, u32[]{:S(2)}, u32[]{:S(2)}) %collective-permute-start) | collective-permute-done | bytes 589856 | tf_op jit(solution)/shard_map/ppermute | solution.py:386
  45.8 3.1 %collective-permute-done.1.refs_2_ = bf16[9,32,1024]{2,1,0:T(8,128)(2,1)S(1)} collective-permute-done((bf16[9,32,1024]{2,1,0:T(8,128)(2,1)}, bf16[9,32,1024]{2,1,0:T(8,128)(2,1)S(1)}, u32[]{:S(2)}, u32[]{:S(2)}) %collective-permute-start.1) | collective-permute-done | bytes 589856 | tf_op jit(solution)/shard_map/ppermute | solution.py:386
  48.9 9.4 %collective-permute-done.2.refs_3_ = bf16[9,32,1024]{2,1,0:T(8,128)(2,1)S(1)} collective-permute-done((bf16[9,32,1024]{2,1,0:T(8,128)(2,1)}, bf16[9,32,1024]{2,1,0:T(8,128)(2,1)S(1)}, u32[]{:S(2)}, u32[]{:S(2)}) %collective-permute-start.2) | collective-permute-done | bytes 589856 | tf_op jit(solution)/shard_map/ppermute | solution.py:386
  59.4 3.3 %down_early.1 = (bf16[448,128]{1,0:T(8,128)(2,1)S(1)}, bf16[448,128]{1,0:T(8,128)(2,1)S(1)}, bf16[128,128]{1,0:T(8,128)(2,1)S(1)}) custom-call(s32[4]{0:T(128)S(1)} %copy-done.5, s32[1]{0:T(128)} %get-tuple-element.27.hot_ref, bf16[9,32,1024]{2,1,0:T(8,128)(2,1)S(1)} %copy-done, bf16[9,32,1024]{2,1,0:T(8,128)(2,1)S(1)} %collective-permute-done.refs_1_, ...), custom_call_target="tpu_custom_call" | custom-call | flops 469762048 | bytes 6000000 | tf_op jit(solution)/shard_map/down_early/pallas_call | solution.py:218
  62.9 3.5 %collective-permute-start.18 = (bf16[1,1152,128]{2,1,0:T(8,128)(2,1)S(1)}, bf16[1,1152,128]{2,1,0:T(8,128)(2,1)S(1)}, u32[]{:S(2)}, u32[]{:S(2)}) collective-permute-start(bf16[1,1152,128]{2,1,0:T(8,128)(2,1)S(1)} %slice.9), channel_id=1, source_target_pairs={{0,7},{1,0},{2,1},{3,2},{4,3},{5,4},{6,5},{7,6},{8,15},{9,8},{10,9... | collective-permute-start | bytes 884744 | tf_op jit(solution)/shard_map/ppermute | solution.py:386
  68.0 2.7 %collective-permute-start.11 = (bf16[448,128]{1,0:T(8,128)(2,1)S(1)}, bf16[448,128]{1,0:T(8,128)(2,1)S(1)}, u32[]{:S(2)}, u32[]{:S(2)}) collective-permute-start(bf16[448,128]{1,0:T(8,128)(2,1)S(1)} %add_convert_fusion.1), channel_id=1, source_target_pairs={{0,128},{64,192},{128,0},{192,64},{1,129},{65,193},{129,1},{193,65... | collective-permute-start | bytes 344072 | tf_op jit(solution)/shard_map/ppermute | solution.py:386
  74.6 1.6 %collective-permute-done.11 = bf16[448,128]{1,0:T(8,128)(2,1)S(1)} collective-permute-done((bf16[448,128]{1,0:T(8,128)(2,1)S(1)}, bf16[448,128]{1,0:T(8,128)(2,1)S(1)}, u32[]{:S(2)}, u32[]{:S(2)}) %collective-permute-start.11) | collective-permute-done | bytes 114720 | tf_op jit(solution)/shard_map/ppermute | solution.py:386
  77.8 2.5 %collective-permute-start.21 = (bf16[2,128,128]{2,1,0:T(8,128)(2,1)S(1)}, bf16[2,128,128]{2,1,0:T(8,128)(2,1)S(1)}, u32[]{:S(2)}, u32[]{:S(2)}) collective-permute-start(bf16[2,128,128]{2,1,0:T(8,128)(2,1)S(1)} %add_convert_fusion.3), channel_id=1, source_target_pairs={{0,128},{64,192},{128,0},{192,64},{1,129},{65,193},{129,1},{193,65... | collective-permute-start | bytes 196616 | tf_op jit(solution)/shard_map/ppermute | solution.py:386
  81.7 2.5 %copy.10 = bf16[8192,2,128]{2,0,1:T(8,128)(2,1)} copy(bf16[8192,2,128]{2,1,0:T(2,128)(2,1)S(1)} %copy-done.6) | data formatting | bytes 8388608 | tf_op args[2]
  84.3 1.7 %up_early.1 = (bf16[7,32,256]{2,1,0:T(8,128)(2,1)S(1)}, bf16[7,32,256]{2,1,0:T(8,128)(2,1)S(1)}, bf16[7,32,256]{2,1,0:T(8,128)(2,1)}, bf16[7,32,256]{2,1,0:T(8,128)(2,1)S(1)}) custom-call(s32[4]{0:T(128)S(1)} %copy-done.5, bf16[448,128]{1,0:T(8,128)(2,1)S(1)} %add_convert_fusion.half_ref, bf16[448,128]{1,0:T(8,128)(2,1)S(1)} %collective-permute-done.13.theirs_ref, ...), custom_call_target="tpu_custom_call" | custom-call | flops 117440512 | bytes 1500000 | tf_op jit(solution)/shard_map/up_early/pallas_call | solution.py:304
  86.8 2.0 %collective-permute-start.15 = (bf16[7,32,256]{2,1,0:T(8,128)(2,1)}, bf16[7,32,256]{2,1,0:T(8,128)(2,1)S(1)}, u32[]{:S(2)}, u32[]{:S(2)}) collective-permute-start(bf16[7,32,256]{2,1,0:T(8,128)(2,1)} %get-tuple-element.36), channel_id=1, source_target_pairs={{0,16},{8,24},{16,0},{24,8},{1,17},{9,25},{17,1},{25,9},{2,18},{10... | collective-permute-start | bytes 344072 | tf_op jit(solution)/shard_map/ppermute | solution.py:386
  88.7 1.7 %collective-permute-start.16 = (bf16[7,32,256]{2,1,0:T(8,128)(2,1)S(1)}, bf16[7,32,256]{2,1,0:T(8,128)(2,1)S(1)}, u32[]{:S(2)}, u32[]{:S(2)}) collective-permute-start(bf16[7,32,256]{2,1,0:T(8,128)(2,1)S(1)} %get-tuple-element.37), channel_id=1, source_target_pairs={{0,8},{8,16},{16,24},{24,0},{1,9},{9,17},{17,25},{25,1},{2,10},{10... | collective-permute-start | bytes 344072 | tf_op jit(solution)/shard_map/ppermute | solution.py:386
  90.4 1.6 %up_late.1 = (bf16[2,32,256]{2,1,0:T(8,128)(2,1)S(1)}, bf16[2,32,256]{2,1,0:T(8,128)(2,1)}, bf16[2,32,256]{2,1,0:T(8,128)(2,1)}, bf16[2,32,256]{2,1,0:T(8,128)(2,1)}) custom-call(s32[1]{0:T(128)} %get-tuple-element.27.hot_ref, bf16[2,128,128]{2,1,0:T(8,128)(2,1)S(1)} %add_convert_fusion.2.low_ref, bf16[9,32,1024]{2,1,0:T(8,128)(2,1)S(1)} %copy-done.1, ...), custom_call_target="tpu_custom_call" | custom-call | flops 33554432 | bytes 1000000 | tf_op jit(solution)/shard_map/up_late/pallas_call | solution.py:337
  94.0 2.4 %collective-permute-start.25 = (bf16[2,32,256]{2,1,0:T(8,128)(2,1)}, bf16[2,32,256]{2,1,0:T(8,128)(2,1)S(1)}, u32[]{:S(2)}, u32[]{:S(2)}) collective-permute-start(bf16[2,32,256]{2,1,0:T(8,128)(2,1)} %get-tuple-element.42), channel_id=1, source_target_pairs={{0,8},{8,16},{16,24},{24,0},{1,9},{9,17},{17,25},{25,1},{2,10},{10... | collective-permute-start | bytes 98312 | tf_op jit(solution)/shard_map/ppermute | solution.py:386
  96.5 9.2 %base.1 = (f32[448,256]{1,0:T(8,128)}, f32[448,128]{1,0:T(8,128)}) custom-call(bf16[448,8192]{1,0:T(8,128)(2,1)} %hidden_ref.3, bf16[64,128]{1,0:T(8,128)(2,1)} %bitcast.13, bf16[2,8192,128]{2,1,0:T(8,128)(2,1)} %bitcast.11), custom_call_target="tpu_custom_call" | custom-call | flops 1879048192 | bytes 12000000 | tf_op jit(solution)/shard_map/base/pallas_call | solution.py:152
  (60 shorter events, 18.8 us)
Async XLA Ops:
  1.1 19.3 %collective-permute-start.3 = (bf16[2,1152,128]{2,1,0:T(8,128)(2,1)S(1)}, bf16[2,1152,128]{2,1,0:T(8,128)(2,1)S(1)}, u32[]{:S(2)}, u32[]{:S(2)}) collective-permute-start(bf16[2,1152,128]{2,1,0:T(8,128)(2,1)S(1)} %pad_maximum_fusion.refs_4_), channel_id=1, source_target_pairs={{0,1},{1,2},{2,3},{3,4},{4,5},{5,6},{6,7},{7,0},{8,9},{9,10},{10,1... | collective-permute-start | bytes 1769480 | tf_op jit(solution)/shard_map/ppermute | solution.py:386
  3.1 17.3 %collective-permute-start.4 = (bf16[2,1152,128]{2,1,0:T(8,128)(2,1)S(1)}, bf16[2,1152,128]{2,1,0:T(8,128)(2,1)S(1)}, u32[]{:S(2)}, u32[]{:S(2)}) collective-permute-start(bf16[2,1152,128]{2,1,0:T(8,128)(2,1)S(1)} %pad_maximum_fusion.refs_4_), channel_id=1, source_target_pairs={{0,7},{1,0},{2,1},{3,2},{4,3},{5,4},{6,5},{7,6},{8,15},{9,8},{10,9... | collective-permute-start | bytes 1769480 | tf_op jit(solution)/shard_map/ppermute | solution.py:386
  20.4 15.7 %collective-permute-start.5 = (bf16[2,1152,128]{2,1,0:T(8,128)(2,1)S(1)}, bf16[2,1152,128]{2,1,0:T(8,128)(2,1)S(1)}, u32[]{:S(2)}, u32[]{:S(2)}) collective-permute-start(bf16[2,1152,128]{2,1,0:T(8,128)(2,1)S(1)} %collective-permute-done.3.refs_5_), channel_id=1, source_target_pairs={{0,1},{1,2},{2,3},{3,4},{4,5},{5,6},{6,7},{7,0},{8,9},{9,10},{10,1... | collective-permute-start | bytes 1769480 | tf_op jit(solution)/shard_map/ppermute | solution.py:386
  20.4 15.7 %collective-permute-start.6 = (bf16[2,1152,128]{2,1,0:T(8,128)(2,1)S(1)}, bf16[2,1152,128]{2,1,0:T(8,128)(2,1)S(1)}, u32[]{:S(2)}, u32[]{:S(2)}) collective-permute-start(bf16[2,1152,128]{2,1,0:T(8,128)(2,1)S(1)} %collective-permute-done.4.refs_6_), channel_id=1, source_target_pairs={{0,7},{1,0},{2,1},{3,2},{4,3},{5,4},{6,5},{7,6},{8,15},{9,8},{10,9... | collective-permute-start | bytes 1769480 | tf_op jit(solution)/shard_map/ppermute | solution.py:386
  29.3 16.5 %collective-permute-start = (bf16[9,32,1024]{2,1,0:T(8,128)(2,1)}, bf16[9,32,1024]{2,1,0:T(8,128)(2,1)S(1)}, u32[]{:S(2)}, u32[]{:S(2)}) collective-permute-start(bf16[9,32,1024]{2,1,0:T(8,128)(2,1)} %get-tuple-element.29), channel_id=1, source_target_pairs={{0,8},{8,16},{16,24},{24,0},{1,9},{9,17},{17,25},{25,1},{2,10},{10... | collective-permute-start | bytes 1769480 | tf_op jit(solution)/shard_map/ppermute | solution.py:386
  31.0 17.9 %collective-permute-start.1 = (bf16[9,32,1024]{2,1,0:T(8,128)(2,1)}, bf16[9,32,1024]{2,1,0:T(8,128)(2,1)S(1)}, u32[]{:S(2)}, u32[]{:S(2)}) collective-permute-start(bf16[9,32,1024]{2,1,0:T(8,128)(2,1)} %get-tuple-element.30), channel_id=1, source_target_pairs={{0,16},{8,24},{16,0},{24,8},{1,17},{9,25},{17,1},{25,9},{2,18},{10... | collective-permute-start | bytes 1769480 | tf_op jit(solution)/shard_map/ppermute | solution.py:386
  31.9 26.4 %collective-permute-start.2 = (bf16[9,32,1024]{2,1,0:T(8,128)(2,1)}, bf16[9,32,1024]{2,1,0:T(8,128)(2,1)S(1)}, u32[]{:S(2)}, u32[]{:S(2)}) collective-permute-start(bf16[9,32,1024]{2,1,0:T(8,128)(2,1)} %get-tuple-element.31), channel_id=1, source_target_pairs={{0,24},{8,0},{16,8},{24,16},{1,25},{9,1},{17,9},{25,17},{2,26},{10... | collective-permute-start | bytes 1769480 | tf_op jit(solution)/shard_map/ppermute | solution.py:386
  36.1 22.2 %collective-permute-start.7 = (bf16[2,1152,128]{2,1,0:T(8,128)(2,1)S(1)}, bf16[2,1152,128]{2,1,0:T(8,128)(2,1)S(1)}, u32[]{:S(2)}, u32[]{:S(2)}) collective-permute-start(bf16[2,1152,128]{2,1,0:T(8,128)(2,1)S(1)} %collective-permute-done.5.refs_7_), channel_id=1, source_target_pairs={{0,1},{1,2},{2,3},{3,4},{4,5},{5,6},{6,7},{7,0},{8,9},{9,10},{10,1... | collective-permute-start | bytes 1769480 | tf_op jit(solution)/shard_map/ppermute | solution.py:386
  36.1 22.2 %collective-permute-start.8 = (bf16[2,1152,128]{2,1,0:T(8,128)(2,1)S(1)}, bf16[2,1152,128]{2,1,0:T(8,128)(2,1)S(1)}, u32[]{:S(2)}, u32[]{:S(2)}) collective-permute-start(bf16[2,1152,128]{2,1,0:T(8,128)(2,1)S(1)} %collective-permute-done.6.refs_8_), channel_id=1, source_target_pairs={{0,7},{1,0},{2,1},{3,2},{4,3},{5,4},{6,5},{7,6},{8,15},{9,8},{10,9... | collective-permute-start | bytes 1769480 | tf_op jit(solution)/shard_map/ppermute | solution.py:386
  62.8 10.7 %collective-permute-start.17 = (bf16[1,1152,128]{2,1,0:T(8,128)(2,1)S(1)}, bf16[1,1152,128]{2,1,0:T(8,128)(2,1)S(1)}, u32[]{:S(2)}, u32[]{:S(2)}) collective-permute-start(bf16[1,1152,128]{2,1,0:T(8,128)(2,1)S(1)} %slice.8), channel_id=1, source_target_pairs={{0,1},{1,2},{2,3},{3,4},{4,5},{5,6},{6,7},{7,0},{8,9},{9,10},{10,1... | collective-permute-start | bytes 884744 | tf_op jit(solution)/shard_map/ppermute | solution.py:386
  62.9 10.6 %collective-permute-start.18 = (bf16[1,1152,128]{2,1,0:T(8,128)(2,1)S(1)}, bf16[1,1152,128]{2,1,0:T(8,128)(2,1)S(1)}, u32[]{:S(2)}, u32[]{:S(2)}) collective-permute-start(bf16[1,1152,128]{2,1,0:T(8,128)(2,1)S(1)} %slice.9), channel_id=1, source_target_pairs={{0,7},{1,0},{2,1},{3,2},{4,3},{5,4},{6,5},{7,6},{8,15},{9,8},{10,9... | collective-permute-start | bytes 884744 | tf_op jit(solution)/shard_map/ppermute | solution.py:386
  66.5 8.1 %collective-permute-start.10 = (bf16[448,128]{1,0:T(8,128)(2,1)S(1)}, bf16[448,128]{1,0:T(8,128)(2,1)S(1)}, u32[]{:S(2)}, u32[]{:S(2)}) collective-permute-start(bf16[448,128]{1,0:T(8,128)(2,1)S(1)} %add_convert_fusion.1), channel_id=1, source_target_pairs={{0,64},{64,128},{128,192},{192,0},{1,65},{65,129},{129,193},{193,1... | collective-permute-start | bytes 344072 | tf_op jit(solution)/shard_map/ppermute | solution.py:386
  68.0 8.1 %collective-permute-start.11 = (bf16[448,128]{1,0:T(8,128)(2,1)S(1)}, bf16[448,128]{1,0:T(8,128)(2,1)S(1)}, u32[]{:S(2)}, u32[]{:S(2)}) collective-permute-start(bf16[448,128]{1,0:T(8,128)(2,1)S(1)} %add_convert_fusion.1), channel_id=1, source_target_pairs={{0,128},{64,192},{128,0},{192,64},{1,129},{65,193},{129,1},{193,65... | collective-permute-start | bytes 344072 | tf_op jit(solution)/shard_map/ppermute | solution.py:386
  70.8 5.4 %collective-permute-start.12 = (bf16[448,128]{1,0:T(8,128)(2,1)S(1)}, bf16[448,128]{1,0:T(8,128)(2,1)S(1)}, u32[]{:S(2)}, u32[]{:S(2)}) collective-permute-start(bf16[448,128]{1,0:T(8,128)(2,1)S(1)} %add_convert_fusion.1), channel_id=1, source_target_pairs={{0,192},{64,0},{128,64},{192,128},{1,193},{65,1},{129,65},{193,129... | collective-permute-start | bytes 344072 | tf_op jit(solution)/shard_map/ppermute | solution.py:386
  76.2 8.0 %collective-permute-start.13 = (bf16[448,128]{1,0:T(8,128)(2,1)S(1)}, bf16[448,128]{1,0:T(8,128)(2,1)S(1)}, u32[]{:S(2)}, u32[]{:S(2)}) collective-permute-start(bf16[448,128]{1,0:T(8,128)(2,1)S(1)} %add_convert_fusion.half_ref), channel_id=1, source_target_pairs={{0,32},{32,0},{1,33},{33,1},{2,34},{34,2},{3,35},{35,3},{4,36},{36... | collective-permute-start | bytes 344072 | tf_op jit(solution)/shard_map/ppermute | solution.py:386
  76.4 12.4 %collective-permute-start.20 = (bf16[2,128,128]{2,1,0:T(8,128)(2,1)S(1)}, bf16[2,128,128]{2,1,0:T(8,128)(2,1)S(1)}, u32[]{:S(2)}, u32[]{:S(2)}) collective-permute-start(bf16[2,128,128]{2,1,0:T(8,128)(2,1)S(1)} %add_convert_fusion.3), channel_id=1, source_target_pairs={{0,64},{64,128},{128,192},{192,0},{1,65},{65,129},{129,193},{193,1... | collective-permute-start | bytes 196616 | tf_op jit(solution)/shard_map/ppermute | solution.py:386
  77.8 12.6 %collective-permute-start.21 = (bf16[2,128,128]{2,1,0:T(8,128)(2,1)S(1)}, bf16[2,128,128]{2,1,0:T(8,128)(2,1)S(1)}, u32[]{:S(2)}, u32[]{:S(2)}) collective-permute-start(bf16[2,128,128]{2,1,0:T(8,128)(2,1)S(1)} %add_convert_fusion.3), channel_id=1, source_target_pairs={{0,128},{64,192},{128,0},{192,64},{1,129},{65,193},{129,1},{193,65... | collective-permute-start | bytes 196616 | tf_op jit(solution)/shard_map/ppermute | solution.py:386
  80.3 10.1 %collective-permute-start.22 = (bf16[2,128,128]{2,1,0:T(8,128)(2,1)S(1)}, bf16[2,128,128]{2,1,0:T(8,128)(2,1)S(1)}, u32[]{:S(2)}, u32[]{:S(2)}) collective-permute-start(bf16[2,128,128]{2,1,0:T(8,128)(2,1)S(1)} %add_convert_fusion.3), channel_id=1, source_target_pairs={{0,192},{64,0},{128,64},{192,128},{1,193},{65,1},{129,65},{193,129... | collective-permute-start | bytes 196616 | tf_op jit(solution)/shard_map/ppermute | solution.py:386
  86.0 8.1 %collective-permute-start.14 = (bf16[7,32,256]{2,1,0:T(8,128)(2,1)S(1)}, bf16[7,32,256]{2,1,0:T(8,128)(2,1)S(1)}, u32[]{:S(2)}, u32[]{:S(2)}) collective-permute-start(bf16[7,32,256]{2,1,0:T(8,128)(2,1)S(1)} %get-tuple-element.35), channel_id=1, source_target_pairs={{0,24},{8,0},{16,8},{24,16},{1,25},{9,1},{17,9},{25,17},{2,26},{10... | collective-permute-start | bytes 344072 | tf_op jit(solution)/shard_map/ppermute | solution.py:386
  86.8 18.9 %collective-permute-start.15 = (bf16[7,32,256]{2,1,0:T(8,128)(2,1)}, bf16[7,32,256]{2,1,0:T(8,128)(2,1)S(1)}, u32[]{:S(2)}, u32[]{:S(2)}) collective-permute-start(bf16[7,32,256]{2,1,0:T(8,128)(2,1)} %get-tuple-element.36), channel_id=1, source_target_pairs={{0,16},{8,24},{16,0},{24,8},{1,17},{9,25},{17,1},{25,9},{2,18},{10... | collective-permute-start | bytes 344072 | tf_op jit(solution)/shard_map/ppermute | solution.py:386
  88.7 17.0 %collective-permute-start.16 = (bf16[7,32,256]{2,1,0:T(8,128)(2,1)S(1)}, bf16[7,32,256]{2,1,0:T(8,128)(2,1)S(1)}, u32[]{:S(2)}, u32[]{:S(2)}) collective-permute-start(bf16[7,32,256]{2,1,0:T(8,128)(2,1)S(1)} %get-tuple-element.37), channel_id=1, source_target_pairs={{0,8},{8,16},{16,24},{24,0},{1,9},{9,17},{17,25},{25,1},{2,10},{10... | collective-permute-start | bytes 344072 | tf_op jit(solution)/shard_map/ppermute | solution.py:386
  92.1 16.0 %collective-permute-start.23 = (bf16[2,32,256]{2,1,0:T(8,128)(2,1)}, bf16[2,32,256]{2,1,0:T(8,128)(2,1)S(1)}, u32[]{:S(2)}, u32[]{:S(2)}) collective-permute-start(bf16[2,32,256]{2,1,0:T(8,128)(2,1)} %get-tuple-element.40), channel_id=1, source_target_pairs={{0,24},{8,0},{16,8},{24,16},{1,25},{9,1},{17,9},{25,17},{2,26},{10... | collective-permute-start | bytes 98312 | tf_op jit(solution)/shard_map/ppermute | solution.py:386
  92.5 15.7 %collective-permute-start.24 = (bf16[2,32,256]{2,1,0:T(8,128)(2,1)}, bf16[2,32,256]{2,1,0:T(8,128)(2,1)S(1)}, u32[]{:S(2)}, u32[]{:S(2)}) collective-permute-start(bf16[2,32,256]{2,1,0:T(8,128)(2,1)} %get-tuple-element.41), channel_id=1, source_target_pairs={{0,16},{8,24},{16,0},{24,8},{1,17},{9,25},{17,1},{25,9},{2,18},{10... | collective-permute-start | bytes 98312 | tf_op jit(solution)/shard_map/ppermute | solution.py:386
  94.0 14.1 %collective-permute-start.25 = (bf16[2,32,256]{2,1,0:T(8,128)(2,1)}, bf16[2,32,256]{2,1,0:T(8,128)(2,1)S(1)}, u32[]{:S(2)}, u32[]{:S(2)}) collective-permute-start(bf16[2,32,256]{2,1,0:T(8,128)(2,1)} %get-tuple-element.42), channel_id=1, source_target_pairs={{0,8},{8,16},{16,24},{24,0},{1,9},{9,17},{17,25},{25,1},{2,10},{10... | collective-permute-start | bytes 98312 | tf_op jit(solution)/shard_map/ppermute | solution.py:386
  (9 other events, 85.2 us)

commit v2 on v1

--- a/solution.py
+++ b/solution.py
@@ -20,7 +20,7 @@
 NY = 4
 BUCKETS = NZ + 1
 SLOTS = BUCKETS * BLOCK
-EARLY = 7
+EARLY = 5
 LATE = BUCKETS - EARLY
 ORDER = (0, 7, 1, 6, 2, 5, 3, 4)
 RANK2 = 128
@@ -78,7 +78,7 @@
     bucket = dy * BUCKETS + jnp.where(over, float(NZ), rank)
     place = jnp.where(over, pos - CAP, pos)
     dst = bucket * BLOCK + place
-    dst_ref[...] = jnp.broadcast_to(to_column(dst, TOK), (TOK, 128))
+    dst_ref[...] = dst
     hot_ref[0] = jnp.max(jnp.where(over, rank, -1.0)).astype(jnp.int32)
     spot = jnp.where(iota((TOK, 128), 1) == to_column(place, TOK), 1.0, 0.0).astype(BF16)
     for part in range(NY):
@@ -107,10 +107,10 @@
                 pl.BlockSpec((1, table.shape[1]), lambda i, p: (0, 0)),
             ],
             out_specs=[pl.BlockSpec((BUCKETS, BLOCK, COLS), lambda i, p: (0, 0, 0))] * NY
-            + [pl.BlockSpec((TOK, 128), lambda i, p: (0, 0)), scalars()],
+            + [pl.BlockSpec((1, TOK), lambda i, p: (0, 0)), scalars()],
         ),
         out_shape=[message] * NY
-        + [jax.ShapeDtypeStruct((TOK, 128), F32), jax.ShapeDtypeStruct((1,), jnp.int32)],
+        + [jax.ShapeDtypeStruct((1, TOK), F32), jax.ShapeDtypeStruct((1,), jnp.int32)],
         cost_estimate=pl.CostEstimate(
             flops=2 * NY * SLOTS * TOK * COLS, bytes_accessed=4_000_000, transcendentals=0
         ),
@@ -119,25 +119,63 @@
     return out[:NY], out[NY], out[NY + 1]
 
 
-def base_kernel(hidden_ref, gain_ref, weight_ref, out_ref, inv_ref, square_ref):
+def columns_kernel(row_ref, column_ref):
+    column_ref[...] = jnp.broadcast_to(to_column(row_ref[...], TOK), (TOK, 128))
+
+
+def columns(row):
+    return pl.pallas_call(
+        columns_kernel,
+        in_specs=[whole()],
+        out_specs=whole(),
+        out_shape=jax.ShapeDtypeStruct((TOK, 128), F32),
+        compiler_params=params(),
+        cost_estimate=pl.CostEstimate(flops=1_000_000, bytes_accessed=300_000, transcendentals=0),
+        name="columns",
+    )(row)
+
+
+def base_kernel(
+    hidden_ref, gain_ref, mixed_ref, out_ref, inv_ref, square_ref, scaled_ref, weight_ref
+):
     step = pl.program_id(0)
-    wide = hidden_ref[...].astype(F32)
-    scaled = (wide * gain_row(gain_ref[...])).astype(BF16)
-    weight = jnp.concatenate([weight_ref[0], weight_ref[1]], axis=1)
-    term = jnp.dot(scaled, weight, preferred_element_type=F32)
-    lanes = sum(
-        wide[:, c : c + 128] * wide[:, c : c + 128] for c in range(0, wide.shape[1], 128)
-    )
+    gain = gain_row(gain_ref[...]).astype(BF16)
+    rows = 64
+
+    @pl.when(step == 0)
+    def _():
+        square_ref[...] = jnp.zeros_like(square_ref)
+
+    for r in range(0, TOK, rows):
+        square = square_ref[r : r + rows, :]
+        for c in range(0, hidden_ref.shape[1], 128):
+            part = hidden_ref[r : r + rows, c : c + 128]
+            scaled_ref[r : r + rows, c : c + 128] = part * gain[:, c : c + 128]
+            wide = part.astype(F32)
+            square = square + wide * wide
+        square_ref[r : r + rows, :] = square
+    row = lax.broadcasted_iota(jnp.int32, (256, 256), 0)
+    source = 2 * (row % 128) + row // 128
+    part_rows = jnp.where(
+        lax.broadcasted_iota(jnp.int32, (256, 256), 1) == source, 1.0, 0.0
+    ).astype(BF16)
+    for b in range(0, mixed_ref.shape[0], 512):
+        pair = jnp.concatenate([mixed_ref[b : b + 256], mixed_ref[b + 256 : b + 512]], axis=1)
+        parted = jnp.dot(part_rows, pair, preferred_element_type=F32).astype(BF16)
+        d = b // 2
+        weight_ref[d : d + 128, :128] = parted[:128, :128]
+        weight_ref[d : d + 128, 128:] = parted[128:, :128]
+        weight_ref[d + 128 : d + 256, :128] = parted[:128, 128:]
+        weight_ref[d + 128 : d + 256, 128:] = parted[128:, 128:]
+    term = jnp.dot(scaled_ref[...], weight_ref[...], preferred_element_type=F32)
 
     @pl.when(step == 0)
     def _():
         out_ref[...] = term
-        square_ref[...] = lanes
 
     @pl.when(step > 0)
     def _():
         out_ref[...] += term
-        square_ref[...] += lanes
 
     @pl.when(step == pl.num_programs(0) - 1)
     def _():
@@ -155,7 +193,7 @@
         in_specs=[
             pl.BlockSpec((TOK, tile), lambda k: (0, k)),
             pl.BlockSpec((8, 128), lambda k: (k, 0)),
-            pl.BlockSpec((2, tile, 128), lambda k: (0, k, 0)),
+            pl.BlockSpec((2 * tile, 128), lambda k: (k, 0)),
         ],
         out_specs=[
             pl.BlockSpec((TOK, 256), lambda k: (0, 0)),
@@ -165,7 +203,7 @@
             jax.ShapeDtypeStruct((TOK, 256), F32),
             jax.ShapeDtypeStruct((TOK, 128), F32),
         ],
-        scratch_shapes=[pltpu.VMEM((TOK, 128), F32)],
+        scratch_shapes=[pltpu.VMEM((TOK, 128), F32), pltpu.VMEM((TOK, tile), BF16), pltpu.VMEM((tile, 256), BF16)],
         cost_estimate=pl.CostEstimate(
             flops=2 * TOK * DIM * 256, bytes_accessed=12_000_000, transcendentals=0
         ),
@@ -235,27 +273,33 @@
 
 def down_late_kernel(hot_ref, *refs):
     received = refs[:NY]
-    zero, one, more_ref, low_ref = refs[NY:]
-    weight = jnp.concatenate([zero[0, :COLS], one[0, :COLS]], axis=1)
-    rows, local = bucket_rows(received, EARLY)
-    low_ref[0] = project(rows, local, weight).astype(BF16)
-    low_ref[1] = more_ref[...]
-
-    @pl.when(hot_ref[0] == EARLY)
-    def _():
-        rows, local = bucket_rows(received, NZ)
-        low_ref[1] = project(rows, local, weight).astype(BF16)
+    chunks = refs[NY:-2]
+    more_ref, low_ref = refs[-2:]
+    low_ref[LATE - 1] = more_ref[...]
+    for at in range(LATE - 1):
+        if at < LATE - 2:
+            zero, one = chunks[at][0, :COLS], chunks[at][1, :COLS]
+        else:
+            zero, one = chunks[at][0, :COLS], chunks[at + 1][0, :COLS]
+        weight = jnp.concatenate([zero, one], axis=1)
+        rows, local = bucket_rows(received, EARLY + at)
+        low_ref[at] = project(rows, local, weight).astype(BF16)
+
+        @pl.when(hot_ref[0] == EARLY + at)
+        def _():
+            rows, local = bucket_rows(received, NZ)
+            low_ref[LATE - 1] = project(rows, local, weight).astype(BF16)
 
 
 def down_late(hot, received, chunks, more):
     return pl.pallas_call(
         down_late_kernel,
-        in_specs=[scalars()] + [whole()] * (NY + 3),
+        in_specs=[scalars()] + [whole()] * (NY + len(chunks) + 1),
         out_specs=whole(),
         out_shape=jax.ShapeDtypeStruct((LATE, NY * BLOCK, RANK2), BF16),
         compiler_params=params(),
         cost_estimate=pl.CostEstimate(
-            flops=2 * 256 * 1024 * 256, bytes_accessed=1_000_000, transcendentals=0
+            flops=2 * 512 * 1024 * 256, bytes_accessed=2_000_000, transcendentals=0
         ),
         name="down_late",
     )(hot, *received, *chunks, more)
@@ -317,14 +361,15 @@
 
 def up_late_kernel(hot_ref, low_ref, *refs):
     received = refs[:NY]
-    chunks = refs[NY : NY + EARLY]
-    zero, one = refs[NY + EARLY : NY + EARLY + 2]
-    outs = refs[NY + EARLY + 2 :]
-    last = jnp.concatenate([zero[0, COLS:], one[0, COLS:]], axis=0)
-    hot_up = last.astype(F32)
-    for k in range(EARLY):
-        hot_up = jnp.where(hot_ref[0] == k, up_rows(chunks[k]).astype(F32), hot_up)
-    for at, up in ((0, last), (1, hot_up)):
+    chunks = refs[NY:-NY]
+    outs = refs[-NY:]
+    ups = [up_rows(c) for c in chunks[:-2]]
+    ups.append(jnp.concatenate([chunks[-2][0, COLS:], chunks[-1][0, COLS:]], axis=0))
+    hot_up = ups[0].astype(F32)
+    for k in range(1, NZ):
+        hot_up = jnp.where(hot_ref[0] == k, ups[k].astype(F32), hot_up)
+    for at in range(LATE):
+        up = hot_up if at == LATE - 1 else ups[EARLY + at]
         local = jnp.concatenate([local_column(r[EARLY + at, :, :128]) for r in received], axis=0)
         delta = jnp.dot(
             spread(low_ref[at].astype(F32), local), up_matrix(up), preferred_element_type=F32
@@ -333,18 +378,18 @@
             outs[s][at] = delta[s * BLOCK : (s + 1) * BLOCK]
 
 
-def up_late(hot, low, received, chunks, last):
+def up_late(hot, low, received, chunks):
     return pl.pallas_call(
         up_late_kernel,
-        in_specs=[scalars()] + [whole()] * (1 + NY + EARLY + 2),
+        in_specs=[scalars()] + [whole()] * (1 + NY + len(chunks)),
         out_specs=[whole()] * NY,
         out_shape=[jax.ShapeDtypeStruct((LATE, BLOCK, 256), BF16)] * NY,
         compiler_params=params(),
         cost_estimate=pl.CostEstimate(
-            flops=2 * 2 * 128 * 256 * 256, bytes_accessed=1_000_000, transcendentals=0
+            flops=2 * 512 * 256 * 256, bytes_accessed=1_500_000, transcendentals=0
         ),
         name="up_late",
-    )(hot, low, *received, *chunks, *last)
+    )(hot, low, *received, *chunks)
 
 
 def collect(dst, first, count, back):
@@ -401,14 +446,16 @@
         chunks[k] = minus
     last = [shift(plus[:1], "z", NZ, 1), shift(minus[1:], "z", NZ, -1)]
     early = [chunks[dz] for dz in ORDER[:EARLY]]
+    late = [chunks[dz] for dz in ORDER[EARLY:-1]] + last
 
     gains = gain.reshape(DIM // 128, 128)
     send, dst, hot = dispatch(
         place, hidden, gains, pair_index.reshape(1, TOK), row_index.reshape(1, -1)
     )
+    dst = columns(dst)
     received = [send[0]] + [shift(send[dy], "y", NY, dy) for dy in range(1, NY)]
 
-    base, inv = base_projection(hidden, gains, kv_weight.transpose(1, 0, 2))
+    base, inv = base_projection(hidden, gains, kv_weight.reshape(2 * DIM, 128))
 
     mine, other, more = down_early(place, hot, received, early)
     got = shift(other, "core", 2, 1)
@@ -422,12 +469,12 @@
     back = [delta[0]] + [shift(delta[dy], "y", NY, -dy) for dy in range(1, NY)]
     summed = finish(finish_early_kernel, base, inv, dst, back, F32)
 
-    low = down_late(hot, received, last, more)
+    low = down_late(hot, received, late, more)
     chip = (low.astype(F32) + shift(low, "core", 2, 1).astype(F32)).astype(BF16)
     total = chip.astype(F32)
     for k in range(1, 4):
         total = total + shift(chip, "x", 4, k).astype(F32)
-    delta = up_late(hot, total.astype(BF16), received, early, last)
+    delta = up_late(hot, total.astype(BF16), received, early + late)
     back = [delta[0]] + [shift(delta[dy], "y", NY, -dy) for dy in range(1, NY)]
     out = finish(finish_late_kernel, summed, inv, dst, back, BF16)
     return out.reshape(TOK, 2, 128)

time: 110 us -> 122 us (1.11)
  the two profiles are of different devices: /device:TPU:8 before, /device:TPU:6 now
where the time goes in v2:
time: 122 us; the launch traced here: 120 us
  waiting for transfers between devices  46.5 us (38%)
  starting transfers between devices  38.8 us (32%)
  Pallas kernels  27.2 us (22%)
  local copies, waits for them, and re-layouts  4.98 us (4%)
  other arithmetic  1.97 us (2%)
    ppermute x26, waiting for transfers between devices, shift(): return lax.ppermute(x, axis, [(i, (i + by) % size) for i in range(size)])  46.5 us
    ppermute x26, starting transfers between devices, shift(): return lax.ppermute(x, axis, [(i, (i + by) % size) for i in range(size)])  38.8 us
    pallas_call x1, Pallas kernels, base_projection(): pl.pallas_call(base_kernel, grid=(DIM // tile,), in_specs=[pl.BlockSpec((...  10.7 us
    pallas_call x1, Pallas kernels, dispatch(): pl.pallas_call(dispatch_kernel, grid_spec=pltpu.PrefetchScalarGridSpec(nu...  4.82 us
    unnamed x22, local copies, waits for them, and re-layouts  3.23 us
    pallas_call x1, Pallas kernels, up_late(): pl.pallas_call(up_late_kernel, in_specs=[scalars()] + [whole()] * (1 + NY...  2.77 us
    pallas_call x1, Pallas kernels, down_early(): pl.pallas_call(down_early_kernel, in_specs=[scalars(), scalars()] + [whol...  2.71 us
    pallas_call x1, Pallas kernels, down_late(): pl.pallas_call(down_late_kernel, in_specs=[scalars()] + [whole()] * (NY +...  2.48 us
  transfers between devices with their start and end apart: 26, of which 7 were waited for; matrix products, arithmetic and copies ran while one was open for 2% of the time, Pallas kernels for 22%

profile of v2, /device:TPU:6, one launch (start us, length us, event | category | flops | bytes accessed | tf_op | source)
XLA Modules:
  0.0 119.7 jit_solution(13127995297887796315)
XLA Ops:
  1.1 2.0 %collective-permute-start.3 = (bf16[2,1152,128]{2,1,0:T(8,128)(2,1)S(1)}, bf16[2,1152,128]{2,1,0:T(8,128)(2,1)S(1)}, u32[]{:S(2)}, u32[]{:S(2)}) collective-permute-start(bf16[2,1152,128]{2,1,0:T(8,128)(2,1)S(1)} %pad_maximum_fusion.refs_4_), channel_id=1, source_target_pairs={{0,1},{1,2},{2,3},{3,4},{4,5},{5,6},{6,7},{7,0},{8,9},{9,10},{10,1... | collective-permute-start | bytes 1769480 | tf_op jit(solution)/shard_map/ppermute | solution.py:431
  3.1 4.0 %collective-permute-start.4 = (bf16[2,1152,128]{2,1,0:T(8,128)(2,1)S(1)}, bf16[2,1152,128]{2,1,0:T(8,128)(2,1)S(1)}, u32[]{:S(2)}, u32[]{:S(2)}) collective-permute-start(bf16[2,1152,128]{2,1,0:T(8,128)(2,1)S(1)} %pad_maximum_fusion.refs_4_), channel_id=1, source_target_pairs={{0,7},{1,0},{2,1},{3,2},{4,3},{5,4},{6,5},{7,6},{8,15},{9,8},{10,9... | collective-permute-start | bytes 1769480 | tf_op jit(solution)/shard_map/ppermute | solution.py:431
  7.1 13.2 %collective-permute-done.3.refs_5_ = bf16[2,1152,128]{2,1,0:T(8,128)(2,1)S(1)} collective-permute-done((bf16[2,1152,128]{2,1,0:T(8,128)(2,1)S(1)}, bf16[2,1152,128]{2,1,0:T(8,128)(2,1)S(1)}, u32[]{:S(2)}, u32[]{:S(2)}) %collective-permute-start.3) | collective-permute-done | bytes 589856 | tf_op jit(solution)/shard_map/ppermute | solution.py:431
  20.4 3.2 %collective-permute-start.6 = (bf16[2,1152,128]{2,1,0:T(8,128)(2,1)S(1)}, bf16[2,1152,128]{2,1,0:T(8,128)(2,1)S(1)}, u32[]{:S(2)}, u32[]{:S(2)}) collective-permute-start(bf16[2,1152,128]{2,1,0:T(8,128)(2,1)S(1)} %collective-permute-done.4.refs_6_), channel_id=1, source_target_pairs={{0,7},{1,0},{2,1},{3,2},{4,3},{5,4},{6,5},{7,6},{8,15},{9,8},{10,9... | collective-permute-start | bytes 1769480 | tf_op jit(solution)/shard_map/ppermute | solution.py:431
  23.6 12.5 %collective-permute-done.5.refs_7_ = bf16[2,1152,128]{2,1,0:T(8,128)(2,1)S(1)} collective-permute-done((bf16[2,1152,128]{2,1,0:T(8,128)(2,1)S(1)}, bf16[2,1152,128]{2,1,0:T(8,128)(2,1)S(1)}, u32[]{:S(2)}, u32[]{:S(2)}) %collective-permute-start.5) | collective-permute-done | bytes 589856 | tf_op jit(solution)/shard_map/ppermute | solution.py:431
  36.1 3.2 %collective-permute-start.16 = (bf16[2,1152,128]{2,1,0:T(8,128)(2,1)S(1)}, bf16[2,1152,128]{2,1,0:T(8,128)(2,1)}, u32[]{:S(2)}, u32[]{:S(2)}) collective-permute-start(bf16[2,1152,128]{2,1,0:T(8,128)(2,1)S(1)} %collective-permute-done.6.refs_8_), channel_id=1, source_target_pairs={{0,7},{1,0},{2,1},{3,2},{4,3},{5,4},{6,5},{7,6},{8,15},{9,8},{10,9... | collective-permute-start | bytes 1769480 | tf_op jit(solution)/shard_map/ppermute | solution.py:431
  40.0 4.8 %dispatch.1 = (bf16[9,32,1024]{2,1,0:T(8,128)(2,1)}, bf16[9,32,1024]{2,1,0:T(8,128)(2,1)}, bf16[9,32,1024]{2,1,0:T(8,128)(2,1)}, bf16[9,32,1024]{2,1,0:T(8,128)(2,1)}, f32[1,448]{1,0:T(1,128)}, /*index=5*/s32[1]{0:T(128)}) custom-call(s32[4]{0:T(128)} %pad_add_fusion.place_ref, bf16[448,8192]{1,0:T(8,128)(2,1)} %hidden_ref.3, bf16[64,128]{1,0:T(8,128)(2,1)} %bitcast.10, ...), custom_call_target="tpu_custom_call" | custom-call | flops 1056964608 | bytes 4000000 | tf_op jit(solution)/shard_map/dispatch/pallas_call | solution.py:98
  44.8 1.7 %collective-permute-start = (bf16[9,32,1024]{2,1,0:T(8,128)(2,1)}, bf16[9,32,1024]{2,1,0:T(8,128)(2,1)S(1)}, u32[]{:S(2)}, u32[]{:S(2)}) collective-permute-start(bf16[9,32,1024]{2,1,0:T(8,128)(2,1)} %get-tuple-element.29), channel_id=1, source_target_pairs={{0,8},{8,16},{16,24},{24,0},{1,9},{9,17},{17,25},{25,1},{2,10},{10... | collective-permute-start | bytes 1769480 | tf_op jit(solution)/shard_map/ppermute | solution.py:431
  46.5 2.9 %collective-permute-start.1 = (bf16[9,32,1024]{2,1,0:T(8,128)(2,1)}, bf16[9,32,1024]{2,1,0:T(8,128)(2,1)S(1)}, u32[]{:S(2)}, u32[]{:S(2)}) collective-permute-start(bf16[9,32,1024]{2,1,0:T(8,128)(2,1)} %get-tuple-element.30), channel_id=1, source_target_pairs={{0,16},{8,24},{16,0},{24,8},{1,17},{9,25},{17,1},{25,9},{2,18},{10... | collective-permute-start | bytes 1769480 | tf_op jit(solution)/shard_map/ppermute | solution.py:431
  49.4 1.3 %collective-permute-start.2 = (bf16[9,32,1024]{2,1,0:T(8,128)(2,1)}, bf16[9,32,1024]{2,1,0:T(8,128)(2,1)S(1)}, u32[]{:S(2)}, u32[]{:S(2)}) collective-permute-start(bf16[9,32,1024]{2,1,0:T(8,128)(2,1)} %get-tuple-element.31), channel_id=1, source_target_pairs={{0,24},{8,0},{16,8},{24,16},{1,25},{9,1},{17,9},{25,17},{2,26},{10... | collective-permute-start | bytes 1769480 | tf_op jit(solution)/shard_map/ppermute | solution.py:431
  52.0 3.3 %collective-permute-start.18 = (bf16[1,1152,128]{2,1,0:T(8,128)(2,1)S(1)}, bf16[1,1152,128]{2,1,0:T(8,128)(2,1)S(1)}, u32[]{:S(2)}, u32[]{:S(2)}) collective-permute-start(bf16[1,1152,128]{2,1,0:T(8,128)(2,1)S(1)} %slice.9), channel_id=1, source_target_pairs={{0,7},{1,0},{2,1},{3,2},{4,3},{5,4},{6,5},{7,6},{8,15},{9,8},{10,9... | collective-permute-start | bytes 884744 | tf_op jit(solution)/shard_map/ppermute | solution.py:431
  55.3 6.1 %collective-permute-done.refs_1_ = bf16[9,32,1024]{2,1,0:T(8,128)(2,1)S(1)} collective-permute-done((bf16[9,32,1024]{2,1,0:T(8,128)(2,1)}, bf16[9,32,1024]{2,1,0:T(8,128)(2,1)S(1)}, u32[]{:S(2)}, u32[]{:S(2)}) %collective-permute-start) | collective-permute-done | bytes 589856 | tf_op jit(solution)/shard_map/ppermute | solution.py:431
  61.4 11.9 %collective-permute-done.1.refs_2_ = bf16[9,32,1024]{2,1,0:T(8,128)(2,1)S(1)} collective-permute-done((bf16[9,32,1024]{2,1,0:T(8,128)(2,1)}, bf16[9,32,1024]{2,1,0:T(8,128)(2,1)S(1)}, u32[]{:S(2)}, u32[]{:S(2)}) %collective-permute-start.1) | collective-permute-done | bytes 589856 | tf_op jit(solution)/shard_map/ppermute | solution.py:431
  73.3 2.7 %down_early.1 = (bf16[320,128]{1,0:T(8,128)(2,1)S(1)}, bf16[320,128]{1,0:T(8,128)(2,1)S(1)}, bf16[128,128]{1,0:T(8,128)(2,1)S(1)}) custom-call(s32[4]{0:T(128)S(1)} %copy-done.9, s32[1]{0:T(128)} %get-tuple-element.27.hot_ref, bf16[9,32,1024]{2,1,0:T(8,128)(2,1)S(1)} %copy-done, bf16[9,32,1024]{2,1,0:T(8,128)(2,1)S(1)} %collective-permute-done.refs_1_, ...), custom_call_target="tpu_custom_call" | custom-call | flops 335544320 | bytes 6000000 | tf_op jit(solution)/shard_map/down_early/pallas_call | solution.py:256
  76.3 2.5 %down_late.1 = bf16[4,128,128]{2,1,0:T(8,128)(2,1)S(1)} custom-call(s32[1]{0:T(128)} %get-tuple-element.27.hot_ref, bf16[9,32,1024]{2,1,0:T(8,128)(2,1)S(1)} %copy-done, bf16[9,32,1024]{2,1,0:T(8,128)(2,1)S(1)} %collective-permute-done.refs_1_, bf16[9,32,1024]{2,1,0:T(8,128)(2,1)S(1)} %collective-permute-done.1.refs_2_, ...), custom_call_target="tpu_custom_call" | custom-call | flops 268435456 | bytes 2000000 | tf_op jit(solution)/shard_map/down_late/pallas_call | solution.py:295
  80.3 2.4 %collective-permute-start.8 = (bf16[320,128]{1,0:T(8,128)(2,1)S(1)}, bf16[320,128]{1,0:T(8,128)(2,1)S(1)}, u32[]{:S(2)}, u32[]{:S(2)}) collective-permute-start(bf16[320,128]{1,0:T(8,128)(2,1)S(1)} %add_convert_fusion.3), channel_id=1, source_target_pairs={{0,64},{64,128},{128,192},{192,0},{1,65},{65,129},{129,193},{193,1... | collective-permute-start | bytes 245768 | tf_op jit(solution)/shard_map/ppermute | solution.py:431
  83.0 2.2 %collective-permute-start.20 = (bf16[4,128,128]{2,1,0:T(8,128)(2,1)S(1)}, bf16[4,128,128]{2,1,0:T(8,128)(2,1)S(1)}, u32[]{:S(2)}, u32[]{:S(2)}) collective-permute-start(bf16[4,128,128]{2,1,0:T(8,128)(2,1)S(1)} %add_convert_fusion.1), channel_id=1, source_target_pairs={{0,64},{64,128},{128,192},{192,0},{1,65},{65,129},{129,193},{193,1... | collective-permute-start | bytes 393224 | tf_op jit(solution)/shard_map/ppermute | solution.py:431
  87.8 1.4 %collective-permute-done.9 = bf16[320,128]{1,0:T(8,128)(2,1)S(1)} collective-permute-done((bf16[320,128]{1,0:T(8,128)(2,1)S(1)}, bf16[320,128]{1,0:T(8,128)(2,1)S(1)}, u32[]{:S(2)}, u32[]{:S(2)}) %collective-permute-start.9) | collective-permute-done | bytes 81952 | tf_op jit(solution)/shard_map/ppermute | solution.py:431
  90.6 1.7 %up_early.1 = (bf16[5,32,256]{2,1,0:T(8,128)(2,1)S(1)}, bf16[5,32,256]{2,1,0:T(8,128)(2,1)S(1)}, bf16[5,32,256]{2,1,0:T(8,128)(2,1)}, bf16[5,32,256]{2,1,0:T(8,128)(2,1)}) custom-call(s32[4]{0:T(128)S(1)} %copy-done.9, bf16[320,128]{1,0:T(8,128)(2,1)S(1)} %add_convert_fusion.2.half_ref, bf16[320,128]{1,0:T(8,128)(2,1)S(1)} %collective-permute-done.11.theirs_ref, ...), custom_call_target="tpu_custom_call" | custom-call | flops 83886080 | bytes 1500000 | tf_op jit(solution)/shard_map/up_early/pallas_call | solution.py:348
  92.3 2.2 %collective-permute-start.12 = (bf16[5,32,256]{2,1,0:T(8,128)(2,1)S(1)}, bf16[5,32,256]{2,1,0:T(8,128)(2,1)S(1)}, u32[]{:S(2)}, u32[]{:S(2)}) collective-permute-start(bf16[5,32,256]{2,1,0:T(8,128)(2,1)S(1)} %get-tuple-element.35), channel_id=1, source_target_pairs={{0,24},{8,0},{16,8},{24,16},{1,25},{9,1},{17,9},{25,17},{2,26},{10... | collective-permute-start | bytes 245768 | tf_op jit(solution)/shard_map/ppermute | solution.py:431
  96.4 2.8 %up_late.1 = (bf16[4,32,256]{2,1,0:T(8,128)(2,1)S(1)}, bf16[4,32,256]{2,1,0:T(8,128)(2,1)}, bf16[4,32,256]{2,1,0:T(8,128)(2,1)}, bf16[4,32,256]{2,1,0:T(8,128)(2,1)}) custom-call(s32[1]{0:T(128)} %get-tuple-element.27.hot_ref, bf16[4,128,128]{2,1,0:T(8,128)(2,1)S(1)} %add_convert_fusion.low_ref, bf16[9,32,1024]{2,1,0:T(8,128)(2,1)S(1)} %copy-done, ...), custom_call_target="tpu_custom_call" | custom-call | flops 67108864 | bytes 1500000 | tf_op jit(solution)/shard_map/up_late/pallas_call | solution.py:382
  99.8 2.5 %collective-permute-start.23 = (bf16[4,32,256]{2,1,0:T(8,128)(2,1)}, bf16[4,32,256]{2,1,0:T(8,128)(2,1)S(1)}, u32[]{:S(2)}, u32[]{:S(2)}) collective-permute-start(bf16[4,32,256]{2,1,0:T(8,128)(2,1)} %get-tuple-element.40), channel_id=1, source_target_pairs={{0,24},{8,0},{16,8},{24,16},{1,25},{9,1},{17,9},{25,17},{2,26},{10... | collective-permute-start | bytes 196616 | tf_op jit(solution)/shard_map/ppermute | solution.py:431
  104.2 10.7 %base.1 = (f32[448,256]{1,0:T(8,128)}, f32[448,128]{1,0:T(8,128)}) custom-call(bf16[448,8192]{1,0:T(8,128)(2,1)} %hidden_ref.3, bf16[64,128]{1,0:T(8,128)(2,1)} %bitcast.11, bf16[16384,128]{1,0:T(8,128)(2,1)} %bitcast.9), custom_call_target="tpu_custom_call" | custom-call | flops 1879048192 | bytes 12000000 | tf_op jit(solution)/shard_map/base/pallas_call | solution.py:190
  117.0 1.4 %shard_map.73.sum_ref = f32[448,256]{1,0:T(8,128)S(1)} custom-call(f32[448,256]{1,0:T(8,128)S(1)} %copy-done.2, f32[448,128]{1,0:T(8,128)S(1)} %copy-done.1, f32[448,128]{1,0:T(8,128)S(1)} %columns.1.dst_ref, bf16[5,32,256]{2,1,0:T(8,128)(2,1)S(1)} %copy-done.4, bf16[5,32,256]{2,1,0:T(8,128)(2,1)S(1)} %copy-done.6, ...), custom_call_target="tpu_custom_call" | custom-call | flops 234881024 | bytes 1500000 | tf_op jit(solution)/shard_map/pallas_call | solution.py:418
  (68 shorter events, 16.9 us)
Async XLA Ops:
  1.1 19.3 %collective-permute-start.3 = (bf16[2,1152,128]{2,1,0:T(8,128)(2,1)S(1)}, bf16[2,1152,128]{2,1,0:T(8,128)(2,1)S(1)}, u32[]{:S(2)}, u32[]{:S(2)}) collective-permute-start(bf16[2,1152,128]{2,1,0:T(8,128)(2,1)S(1)} %pad_maximum_fusion.refs_4_), channel_id=1, source_target_pairs={{0,1},{1,2},{2,3},{3,4},{4,5},{5,6},{6,7},{7,0},{8,9},{9,10},{10,1... | collective-permute-start | bytes 1769480 | tf_op jit(solution)/shard_map/ppermute | solution.py:431
  3.1 17.3 %collective-permute-start.4 = (bf16[2,1152,128]{2,1,0:T(8,128)(2,1)S(1)}, bf16[2,1152,128]{2,1,0:T(8,128)(2,1)S(1)}, u32[]{:S(2)}, u32[]{:S(2)}) collective-permute-start(bf16[2,1152,128]{2,1,0:T(8,128)(2,1)S(1)} %pad_maximum_fusion.refs_4_), channel_id=1, source_target_pairs={{0,7},{1,0},{2,1},{3,2},{4,3},{5,4},{6,5},{7,6},{8,15},{9,8},{10,9... | collective-permute-start | bytes 1769480 | tf_op jit(solution)/shard_map/ppermute | solution.py:431
  20.4 15.7 %collective-permute-start.5 = (bf16[2,1152,128]{2,1,0:T(8,128)(2,1)S(1)}, bf16[2,1152,128]{2,1,0:T(8,128)(2,1)S(1)}, u32[]{:S(2)}, u32[]{:S(2)}) collective-permute-start(bf16[2,1152,128]{2,1,0:T(8,128)(2,1)S(1)} %collective-permute-done.3.refs_5_), channel_id=1, source_target_pairs={{0,1},{1,2},{2,3},{3,4},{4,5},{5,6},{6,7},{7,0},{8,9},{9,10},{10,1... | collective-permute-start | bytes 1769480 | tf_op jit(solution)/shard_map/ppermute | solution.py:431
  20.4 15.7 %collective-permute-start.6 = (bf16[2,1152,128]{2,1,0:T(8,128)(2,1)S(1)}, bf16[2,1152,128]{2,1,0:T(8,128)(2,1)S(1)}, u32[]{:S(2)}, u32[]{:S(2)}) collective-permute-start(bf16[2,1152,128]{2,1,0:T(8,128)(2,1)S(1)} %collective-permute-done.4.refs_6_), channel_id=1, source_target_pairs={{0,7},{1,0},{2,1},{3,2},{4,3},{5,4},{6,5},{7,6},{8,15},{9,8},{10,9... | collective-permute-start | bytes 1769480 | tf_op jit(solution)/shard_map/ppermute | solution.py:431
  36.1 14.8 %collective-permute-start.15 = (bf16[2,1152,128]{2,1,0:T(8,128)(2,1)S(1)}, bf16[2,1152,128]{2,1,0:T(8,128)(2,1)S(1)}, u32[]{:S(2)}, u32[]{:S(2)}) collective-permute-start(bf16[2,1152,128]{2,1,0:T(8,128)(2,1)S(1)} %collective-permute-done.5.refs_7_), channel_id=1, source_target_pairs={{0,1},{1,2},{2,3},{3,4},{4,5},{5,6},{6,7},{7,0},{8,9},{9,10},{10,1... | collective-permute-start | bytes 1769480 | tf_op jit(solution)/shard_map/ppermute | solution.py:431
  36.1 15.0 %collective-permute-start.16 = (bf16[2,1152,128]{2,1,0:T(8,128)(2,1)S(1)}, bf16[2,1152,128]{2,1,0:T(8,128)(2,1)}, u32[]{:S(2)}, u32[]{:S(2)}) collective-permute-start(bf16[2,1152,128]{2,1,0:T(8,128)(2,1)S(1)} %collective-permute-done.6.refs_8_), channel_id=1, source_target_pairs={{0,7},{1,0},{2,1},{3,2},{4,3},{5,4},{6,5},{7,6},{8,15},{9,8},{10,9... | collective-permute-start | bytes 1769480 | tf_op jit(solution)/shard_map/ppermute | solution.py:431
  44.8 16.6 %collective-permute-start = (bf16[9,32,1024]{2,1,0:T(8,128)(2,1)}, bf16[9,32,1024]{2,1,0:T(8,128)(2,1)S(1)}, u32[]{:S(2)}, u32[]{:S(2)}) collective-permute-start(bf16[9,32,1024]{2,1,0:T(8,128)(2,1)} %get-tuple-element.29), channel_id=1, source_target_pairs={{0,8},{8,16},{16,24},{24,0},{1,9},{9,17},{17,25},{25,1},{2,10},{10... | collective-permute-start | bytes 1769480 | tf_op jit(solution)/shard_map/ppermute | solution.py:431
  46.5 26.8 %collective-permute-start.1 = (bf16[9,32,1024]{2,1,0:T(8,128)(2,1)}, bf16[9,32,1024]{2,1,0:T(8,128)(2,1)S(1)}, u32[]{:S(2)}, u32[]{:S(2)}) collective-permute-start(bf16[9,32,1024]{2,1,0:T(8,128)(2,1)} %get-tuple-element.30), channel_id=1, source_target_pairs={{0,16},{8,24},{16,0},{24,8},{1,17},{9,25},{17,1},{25,9},{2,18},{10... | collective-permute-start | bytes 1769480 | tf_op jit(solution)/shard_map/ppermute | solution.py:431
  49.4 23.9 %collective-permute-start.2 = (bf16[9,32,1024]{2,1,0:T(8,128)(2,1)}, bf16[9,32,1024]{2,1,0:T(8,128)(2,1)S(1)}, u32[]{:S(2)}, u32[]{:S(2)}) collective-permute-start(bf16[9,32,1024]{2,1,0:T(8,128)(2,1)} %get-tuple-element.31), channel_id=1, source_target_pairs={{0,24},{8,0},{16,8},{24,16},{1,25},{9,1},{17,9},{25,17},{2,26},{10... | collective-permute-start | bytes 1769480 | tf_op jit(solution)/shard_map/ppermute | solution.py:431
  51.0 25.4 %collective-permute-start.17 = (bf16[1,1152,128]{2,1,0:T(8,128)(2,1)S(1)}, bf16[1,1152,128]{2,1,0:T(8,128)(2,1)S(1)}, u32[]{:S(2)}, u32[]{:S(2)}) collective-permute-start(bf16[1,1152,128]{2,1,0:T(8,128)(2,1)S(1)} %slice.8), channel_id=1, source_target_pairs={{0,1},{1,2},{2,3},{3,4},{4,5},{5,6},{6,7},{7,0},{8,9},{9,10},{10,1... | collective-permute-start | bytes 884744 | tf_op jit(solution)/shard_map/ppermute | solution.py:431
  52.0 24.3 %collective-permute-start.18 = (bf16[1,1152,128]{2,1,0:T(8,128)(2,1)S(1)}, bf16[1,1152,128]{2,1,0:T(8,128)(2,1)S(1)}, u32[]{:S(2)}, u32[]{:S(2)}) collective-permute-start(bf16[1,1152,128]{2,1,0:T(8,128)(2,1)S(1)} %slice.9), channel_id=1, source_target_pairs={{0,7},{1,0},{2,1},{3,2},{4,3},{5,4},{6,5},{7,6},{8,15},{9,8},{10,9... | collective-permute-start | bytes 884744 | tf_op jit(solution)/shard_map/ppermute | solution.py:431
  78.8 4.1 %collective-permute-start.19 = (bf16[4,128,128]{2,1,0:T(8,128)(2,1)S(1)}, bf16[4,128,128]{2,1,0:T(8,128)(2,1)S(1)}, u32[]{:S(2)}, u32[]{:S(2)}) collective-permute-start(bf16[4,128,128]{2,1,0:T(8,128)(2,1)S(1)} %down_late.1), channel_id=1, source_target_pairs={{0,32},{32,0},{1,33},{33,1},{2,34},{34,2},{3,35},{35,3},{4,36},{36... | collective-permute-start | bytes 393224 | tf_op jit(solution)/shard_map/ppermute | solution.py:431
  79.4 7.1 %collective-permute-start.10 = (bf16[320,128]{1,0:T(8,128)(2,1)S(1)}, bf16[320,128]{1,0:T(8,128)(2,1)S(1)}, u32[]{:S(2)}, u32[]{:S(2)}) collective-permute-start(bf16[320,128]{1,0:T(8,128)(2,1)S(1)} %add_convert_fusion.3), channel_id=1, source_target_pairs={{0,192},{64,0},{128,64},{192,128},{1,193},{65,1},{129,65},{193,129... | collective-permute-start | bytes 245768 | tf_op jit(solution)/shard_map/ppermute | solution.py:431
  80.3 7.5 %collective-permute-start.8 = (bf16[320,128]{1,0:T(8,128)(2,1)S(1)}, bf16[320,128]{1,0:T(8,128)(2,1)S(1)}, u32[]{:S(2)}, u32[]{:S(2)}) collective-permute-start(bf16[320,128]{1,0:T(8,128)(2,1)S(1)} %add_convert_fusion.3), channel_id=1, source_target_pairs={{0,64},{64,128},{128,192},{192,0},{1,65},{65,129},{129,193},{193,1... | collective-permute-start | bytes 245768 | tf_op jit(solution)/shard_map/ppermute | solution.py:431
  82.7 6.5 %collective-permute-start.9 = (bf16[320,128]{1,0:T(8,128)(2,1)S(1)}, bf16[320,128]{1,0:T(8,128)(2,1)S(1)}, u32[]{:S(2)}, u32[]{:S(2)}) collective-permute-start(bf16[320,128]{1,0:T(8,128)(2,1)S(1)} %add_convert_fusion.3), channel_id=1, source_target_pairs={{0,128},{64,192},{128,0},{192,64},{1,129},{65,193},{129,1},{193,65... | collective-permute-start | bytes 245768 | tf_op jit(solution)/shard_map/ppermute | solution.py:431
  83.0 12.6 %collective-permute-start.20 = (bf16[4,128,128]{2,1,0:T(8,128)(2,1)S(1)}, bf16[4,128,128]{2,1,0:T(8,128)(2,1)S(1)}, u32[]{:S(2)}, u32[]{:S(2)}) collective-permute-start(bf16[4,128,128]{2,1,0:T(8,128)(2,1)S(1)} %add_convert_fusion.1), channel_id=1, source_target_pairs={{0,64},{64,128},{128,192},{192,0},{1,65},{65,129},{129,193},{193,1... | collective-permute-start | bytes 393224 | tf_op jit(solution)/shard_map/ppermute | solution.py:431
  85.2 11.1 %collective-permute-start.21 = (bf16[4,128,128]{2,1,0:T(8,128)(2,1)S(1)}, bf16[4,128,128]{2,1,0:T(8,128)(2,1)S(1)}, u32[]{:S(2)}, u32[]{:S(2)}) collective-permute-start(bf16[4,128,128]{2,1,0:T(8,128)(2,1)S(1)} %add_convert_fusion.1), channel_id=1, source_target_pairs={{0,128},{64,192},{128,0},{192,64},{1,129},{65,193},{129,1},{193,65... | collective-permute-start | bytes 393224 | tf_op jit(solution)/shard_map/ppermute | solution.py:431
  86.5 9.8 %collective-permute-start.22 = (bf16[4,128,128]{2,1,0:T(8,128)(2,1)S(1)}, bf16[4,128,128]{2,1,0:T(8,128)(2,1)S(1)}, u32[]{:S(2)}, u32[]{:S(2)}) collective-permute-start(bf16[4,128,128]{2,1,0:T(8,128)(2,1)S(1)} %add_convert_fusion.1), channel_id=1, source_target_pairs={{0,192},{64,0},{128,64},{192,128},{1,193},{65,1},{129,65},{193,129... | collective-permute-start | bytes 393224 | tf_op jit(solution)/shard_map/ppermute | solution.py:431
  92.3 11.2 %collective-permute-start.12 = (bf16[5,32,256]{2,1,0:T(8,128)(2,1)S(1)}, bf16[5,32,256]{2,1,0:T(8,128)(2,1)S(1)}, u32[]{:S(2)}, u32[]{:S(2)}) collective-permute-start(bf16[5,32,256]{2,1,0:T(8,128)(2,1)S(1)} %get-tuple-element.35), channel_id=1, source_target_pairs={{0,24},{8,0},{16,8},{24,16},{1,25},{9,1},{17,9},{25,17},{2,26},{10... | collective-permute-start | bytes 245768 | tf_op jit(solution)/shard_map/ppermute | solution.py:431
  94.5 20.6 %collective-permute-start.13 = (bf16[5,32,256]{2,1,0:T(8,128)(2,1)}, bf16[5,32,256]{2,1,0:T(8,128)(2,1)}, u32[]{:S(2)}, u32[]{:S(2)}) collective-permute-start(bf16[5,32,256]{2,1,0:T(8,128)(2,1)} %get-tuple-element.36), channel_id=1, source_target_pairs={{0,16},{8,24},{16,0},{24,8},{1,17},{9,25},{17,1},{25,9},{2,18},{10... | collective-permute-start | bytes 245768 | tf_op jit(solution)/shard_map/ppermute | solution.py:431
  95.6 19.5 %collective-permute-start.14 = (bf16[5,32,256]{2,1,0:T(8,128)(2,1)}, bf16[5,32,256]{2,1,0:T(8,128)(2,1)}, u32[]{:S(2)}, u32[]{:S(2)}) collective-permute-start(bf16[5,32,256]{2,1,0:T(8,128)(2,1)} %get-tuple-element.37), channel_id=1, source_target_pairs={{0,8},{8,16},{16,24},{24,0},{1,9},{9,17},{17,25},{25,1},{2,10},{10... | collective-permute-start | bytes 245768 | tf_op jit(solution)/shard_map/ppermute | solution.py:431
  99.8 18.7 %collective-permute-start.23 = (bf16[4,32,256]{2,1,0:T(8,128)(2,1)}, bf16[4,32,256]{2,1,0:T(8,128)(2,1)S(1)}, u32[]{:S(2)}, u32[]{:S(2)}) collective-permute-start(bf16[4,32,256]{2,1,0:T(8,128)(2,1)} %get-tuple-element.40), channel_id=1, source_target_pairs={{0,24},{8,0},{16,8},{24,16},{1,25},{9,1},{17,9},{25,17},{2,26},{10... | collective-permute-start | bytes 196616 | tf_op jit(solution)/shard_map/ppermute | solution.py:431
  102.3 16.1 %collective-permute-start.24 = (bf16[4,32,256]{2,1,0:T(8,128)(2,1)}, bf16[4,32,256]{2,1,0:T(8,128)(2,1)S(1)}, u32[]{:S(2)}, u32[]{:S(2)}) collective-permute-start(bf16[4,32,256]{2,1,0:T(8,128)(2,1)} %get-tuple-element.41), channel_id=1, source_target_pairs={{0,16},{8,24},{16,0},{24,8},{1,17},{9,25},{17,1},{25,9},{2,18},{10... | collective-permute-start | bytes 196616 | tf_op jit(solution)/shard_map/ppermute | solution.py:431
  104.1 14.3 %collective-permute-start.25 = (bf16[4,32,256]{2,1,0:T(8,128)(2,1)}, bf16[4,32,256]{2,1,0:T(8,128)(2,1)S(1)}, u32[]{:S(2)}, u32[]{:S(2)}) collective-permute-start(bf16[4,32,256]{2,1,0:T(8,128)(2,1)} %get-tuple-element.42), channel_id=1, source_target_pairs={{0,8},{8,16},{16,24},{24,0},{1,9},{9,17},{17,25},{25,1},{2,10},{10... | collective-permute-start | bytes 196616 | tf_op jit(solution)/shard_map/ppermute | solution.py:431
  (13 other events, 108.0 us)

commit v3 on v2

--- a/solution.py
+++ b/solution.py
@@ -228,47 +228,38 @@
     return jnp.where(local < 0.5, both[:, :RANK2], both[:, RANK2:])
 
 
-def down_early_kernel(place_ref, hot_ref, *refs):
+def down_early_kernel(hot_ref, *refs):
     received = refs[:NY]
     chunks = refs[NY : NY + EARLY]
-    mine_ref, other_ref, more_ref, low_ref = refs[NY + EARLY :]
+    low_ref, more_ref = refs[NY + EARLY :]
     more_ref[...] = jnp.zeros_like(more_ref)
     for k in range(EARLY):
         c = chunks[k]
         weight = jnp.concatenate([c[0, :COLS], c[1, :COLS]], axis=1)
         rows, local = bucket_rows(received, k)
-        low_ref[k * NY * BLOCK : (k + 1) * NY * BLOCK] = project(rows, local, weight).astype(BF16)
+        low_ref[k] = project(rows, local, weight).astype(BF16)
 
         @pl.when(hot_ref[0] == k)
         def _():
             rows, local = bucket_rows(received, NZ)
             more_ref[...] = project(rows, local, weight).astype(BF16)
 
-    size = EARLY * NY * BLOCK // 2
-    first = pl.multiple_of(place_ref[3] * size, size)
-    second = pl.multiple_of(size - place_ref[3] * size, size)
-    mine_ref[...] = low_ref[pl.ds(first, size), :]
-    other_ref[...] = low_ref[pl.ds(second, size), :]
-
-
-def down_early(place, hot, received, chunks):
-    size = EARLY * NY * BLOCK // 2
+
+def down_early(hot, received, chunks):
     return pl.pallas_call(
         down_early_kernel,
-        in_specs=[scalars(), scalars()] + [whole()] * (NY + EARLY),
-        out_specs=[whole()] * 3,
+        in_specs=[scalars()] + [whole()] * (NY + EARLY),
+        out_specs=[whole()] * 2,
         out_shape=[
-            jax.ShapeDtypeStruct((size, RANK2), BF16),
-            jax.ShapeDtypeStruct((size, RANK2), BF16),
+            jax.ShapeDtypeStruct((EARLY, NY * BLOCK, RANK2), BF16),
             jax.ShapeDtypeStruct((NY * BLOCK, RANK2), BF16),
         ],
-        scratch_shapes=[pltpu.VMEM((2 * size, RANK2), BF16)],
         compiler_params=params(),
         cost_estimate=pl.CostEstimate(
             flops=2 * EARLY * 128 * 1024 * 256, bytes_accessed=6_000_000, transcendentals=0
         ),
         name="down_early",
-    )(place, hot, *received, *chunks)
+    )(hot, *received, *chunks)
 
 
 def down_late_kernel(hot_ref, *refs):
@@ -324,19 +315,13 @@
     return jnp.concatenate([chunk[0, COLS:], chunk[1, COLS:]], axis=0)
 
 
-def up_early_kernel(place_ref, half_ref, theirs_ref, *refs):
+def up_early_kernel(low_ref, *refs):
     received = refs[:NY]
     chunks = refs[NY : NY + EARLY]
-    outs = refs[NY + EARLY : -1]
-    low_ref = refs[-1]
-    size = EARLY * NY * BLOCK // 2
-    first = pl.multiple_of(place_ref[3] * size, size)
-    second = pl.multiple_of(size - place_ref[3] * size, size)
-    low_ref[pl.ds(first, size), :] = half_ref[...]
-    low_ref[pl.ds(second, size), :] = theirs_ref[...]
+    outs = refs[NY + EARLY :]
     for k in range(EARLY):
         local = jnp.concatenate([local_column(r[k, :, :128]) for r in received], axis=0)
-        low = low_ref[k * NY * BLOCK : (k + 1) * NY * BLOCK, :].astype(F32)
+        low = low_ref[k].astype(F32)
         delta = jnp.dot(
             spread(low, local), up_matrix(up_rows(chunks[k])), preferred_element_type=F32
         ).astype(BF16)
@@ -344,52 +329,74 @@
             outs[s][k] = delta[s * BLOCK : (s + 1) * BLOCK]
 
 
-def up_early(place, half, theirs, received, chunks):
+def up_early(low, received, chunks):
     return pl.pallas_call(
         up_early_kernel,
-        in_specs=[scalars()] + [whole()] * (2 + NY + EARLY),
+        in_specs=[whole()] * (1 + NY + EARLY),
         out_specs=[whole()] * NY,
         out_shape=[jax.ShapeDtypeStruct((EARLY, BLOCK, 256), BF16)] * NY,
-        scratch_shapes=[pltpu.VMEM((EARLY * NY * BLOCK, RANK2), BF16)],
         compiler_params=params(),
         cost_estimate=pl.CostEstimate(
             flops=2 * EARLY * 128 * 256 * 256, bytes_accessed=1_500_000, transcendentals=0
         ),
         name="up_early",
-    )(place, half, theirs, *received, *chunks)
-
-
-def up_late_kernel(hot_ref, low_ref, *refs):
+    )(low, *received, *chunks)
+
+
+def up_prepare_kernel(hot_ref, *refs):
     received = refs[:NY]
-    chunks = refs[NY:-NY]
-    outs = refs[-NY:]
+    chunks = refs[NY:-2]
+    matrix_ref, mask_ref = refs[-2:]
     ups = [up_rows(c) for c in chunks[:-2]]
     ups.append(jnp.concatenate([chunks[-2][0, COLS:], chunks[-1][0, COLS:]], axis=0))
     hot_up = ups[0].astype(F32)
     for k in range(1, NZ):
         hot_up = jnp.where(hot_ref[0] == k, ups[k].astype(F32), hot_up)
+    ones = jnp.ones((NY * BLOCK, RANK2), F32)
     for at in range(LATE):
-        up = hot_up if at == LATE - 1 else ups[EARLY + at]
+        matrix_ref[at] = up_matrix(hot_up if at == LATE - 1 else ups[EARLY + at])
         local = jnp.concatenate([local_column(r[EARLY + at, :, :128]) for r in received], axis=0)
-        delta = jnp.dot(
-            spread(low_ref[at].astype(F32), local), up_matrix(up), preferred_element_type=F32
-        ).astype(BF16)
+        mask_ref[at] = spread(ones, local)
+
+
+def up_prepare(hot, received, chunks):
+    return pl.pallas_call(
+        up_prepare_kernel,
+        in_specs=[scalars()] + [whole()] * (NY + len(chunks)),
+        out_specs=[whole()] * 2,
+        out_shape=[
+            jax.ShapeDtypeStruct((LATE, 256, 256), BF16),
+            jax.ShapeDtypeStruct((LATE, NY * BLOCK, 256), BF16),
+        ],
+        compiler_params=params(),
+        cost_estimate=pl.CostEstimate(
+            flops=4_000_000, bytes_accessed=1_500_000, transcendentals=0
+        ),
+        name="up_prepare",
+    )(hot, *received, *chunks)
+
+
+def up_late_kernel(low_ref, matrix_ref, mask_ref, *outs):
+    for at in range(LATE):
+        low = low_ref[at]
+        both = jnp.concatenate([low, low], axis=1) * mask_ref[at]
+        delta = jnp.dot(both, matrix_ref[at], preferred_element_type=F32).astype(BF16)
         for s in range(NY):
             outs[s][at] = delta[s * BLOCK : (s + 1) * BLOCK]
 
 
-def up_late(hot, low, received, chunks):
+def up_late(low, matrix, mask):
     return pl.pallas_call(
         up_late_kernel,
-        in_specs=[scalars()] + [whole()] * (1 + NY + len(chunks)),
+        in_specs=[whole()] * 3,
         out_specs=[whole()] * NY,
         out_shape=[jax.ShapeDtypeStruct((LATE, BLOCK, 256), BF16)] * NY,
         compiler_params=params(),
         cost_estimate=pl.CostEstimate(
-            flops=2 * 512 * 256 * 256, bytes_accessed=1_500_000, transcendentals=0
+            flops=2 * 512 * 256 * 256, bytes_accessed=1_000_000, transcendentals=0
         ),
         name="up_late",
-    )(hot, low, *received, *chunks)
+    )(low, matrix, mask)
 
 
 def collect(dst, first, count, back):
@@ -431,9 +438,20 @@
     return lax.ppermute(x, axis, [(i, (i + by) % size) for i in range(size)])
 
 
+def pair_sum(x, axis, size, flip):
+    other = lax.ppermute(x, axis, [(i, i ^ flip) for i in range(size)])
+    return (x.astype(F32) + other.astype(F32)).astype(BF16)
+
+
+def sum_over_tp(x):
+    x = pair_sum(x, "core", 2, 1)
+    x = pair_sum(x, "x", 4, 1)
+    return pair_sum(x, "x", 4, 3)
+
+
 def on_device(hidden, gain, kv_weight, down_weight, up_weight, pair_index, row_index):
     tp = lax.axis_index("x") * 2 + lax.axis_index("core")
-    places = [tp, lax.axis_index("y"), lax.axis_index("z"), lax.axis_index("core")]
+    places = [tp, lax.axis_index("y"), lax.axis_index("z")]
     place = jnp.stack(places).astype(jnp.int32)
 
     own = jnp.concatenate([down_weight, up_weight.reshape(2, RANK2, 128)], axis=1)
@@ -457,24 +475,16 @@
 
     base, inv = base_projection(hidden, gains, kv_weight.reshape(2 * DIM, 128))
 
-    mine, other, more = down_early(place, hot, received, early)
-    got = shift(other, "core", 2, 1)
-    chip = (mine.astype(F32) + got.astype(F32)).astype(BF16)
-    total = chip.astype(F32)
-    for k in range(1, 4):
-        total = total + shift(chip, "x", 4, k).astype(F32)
-    half = total.astype(BF16)
-    theirs = shift(half, "core", 2, 1)
-    delta = up_early(place, half, theirs, received, early)
+    low, more = down_early(hot, received, early)
+    low = sum_over_tp(low)
+    delta = up_early(low, received, early)
     back = [delta[0]] + [shift(delta[dy], "y", NY, -dy) for dy in range(1, NY)]
     summed = finish(finish_early_kernel, base, inv, dst, back, F32)
 
     low = down_late(hot, received, late, more)
-    chip = (low.astype(F32) + shift(low, "core", 2, 1).astype(F32)).astype(BF16)
-    total = chip.astype(F32)
-    for k in range(1, 4):
-        total = total + shift(chip, "x", 4, k).astype(F32)
-    delta = up_late(hot, total.astype(BF16), received, early + late)
+    matrix, mask = up_prepare(hot, received, early + late)
+    low = sum_over_tp(low)
+    delta = up_late(low, matrix, mask)
     back = [delta[0]] + [shift(delta[dy], "y", NY, -dy) for dy in range(1, NY)]
     out = finish(finish_late_kernel, summed, inv, dst, back, BF16)
     return out.reshape(TOK, 2, 128)

time: 122 us -> 123 us (level)
  waiting for transfers between devices: 46.5 us -> 54.6 us
  starting transfers between devices: 38.8 us -> 34.7 us
  Pallas kernels: 27.2 us -> 25.6 us
    ppermute x0 -> x6, waiting for transfers between devices: none -> 10.8 us  [pair_sum(): other = lax.ppermute(x, axis, [(i, i ^ flip) for i in range(size)])]
    ppermute x26 -> x17, starting transfers between devices: 38.8 us -> 29.6 us  [shift(): return lax.ppermute(x, axis, [(i, (i + by) % size) for i in range(size)])]
    ppermute x0 -> x6, starting transfers between devices: none -> 5.17 us  [pair_sum(): other = lax.ppermute(x, axis, [(i, i ^ flip) for i in range(size)])]
    ppermute x26 -> x17, waiting for transfers between devices: 46.5 us -> 43.9 us  [shift(): return lax.ppermute(x, axis, [(i, (i + by) % size) for i in range(size)])]
    pallas_call x3 -> x4, Pallas kernels: 7.15 us -> 5.59 us  [the longest x1 2.15 us: down_early(): pl.pallas_call(down_early_kernel, in_specs=[scalars()] + [whole()] * (NY...]
    unnamed x22 -> x16, local copies, waits for them, and re-layouts: 3.23 us -> 2.6 us
  transfers between devices with their start and end apart: 26 -> 23, of which waited for: 7 -> 8; matrix products, arithmetic and copies ran while one was open for 2% -> 1% of each run, Pallas kernels for 22% -> 21%
where the time goes in v3:
time: 123 us; the launch traced here: 122 us
  waiting for transfers between devices  54.6 us (44%)
  starting transfers between devices  34.7 us (28%)
  Pallas kernels  25.6 us (21%)
  local copies, waits for them, and re-layouts  4.35 us (4%)
  other arithmetic  1.93 us (2%)
    ppermute x17, waiting for transfers between devices, shift(): return lax.ppermute(x, axis, [(i, (i + by) % size) for i in range(size)])  43.9 us
    ppermute x17, starting transfers between devices, shift(): return lax.ppermute(x, axis, [(i, (i + by) % size) for i in range(size)])  29.6 us
    ppermute x6, waiting for transfers between devices, pair_sum(): other = lax.ppermute(x, axis, [(i, i ^ flip) for i in range(size)])  10.8 us
    pallas_call x1, Pallas kernels, base_projection(): pl.pallas_call(base_kernel, grid=(DIM // tile,), in_specs=[pl.BlockSpec((...  10.7 us
    ppermute x6, starting transfers between devices, pair_sum(): other = lax.ppermute(x, axis, [(i, i ^ flip) for i in range(size)])  5.17 us
    pallas_call x1, Pallas kernels, dispatch(): pl.pallas_call(dispatch_kernel, grid_spec=pltpu.PrefetchScalarGridSpec(nu...  4.82 us
    unnamed x16, local copies, waits for them, and re-layouts  2.6 us
    pallas_call x1, Pallas kernels, down_late(): pl.pallas_call(down_late_kernel, in_specs=[scalars()] + [whole()] * (NY +...  2.48 us
  transfers between devices with their start and end apart: 23, of which 8 were waited for; matrix products, arithmetic and copies ran while one was open for 1% of the time, Pallas kernels for 21%

profile of v3, /device:TPU:6, one launch (start us, length us, event | category | flops | bytes accessed | tf_op | source)
XLA Modules:
  0.0 121.5 jit_solution(2722677119586146372)
XLA Ops:
  1.1 2.0 %collective-permute-start.3 = (bf16[2,1152,128]{2,1,0:T(8,128)(2,1)S(1)}, bf16[2,1152,128]{2,1,0:T(8,128)(2,1)S(1)}, u32[]{:S(2)}, u32[]{:S(2)}) collective-permute-start(bf16[2,1152,128]{2,1,0:T(8,128)(2,1)S(1)} %pad_maximum_fusion.refs_4_), channel_id=1, source_target_pairs={{0,1},{1,2},{2,3},{3,4},{4,5},{5,6},{6,7},{7,0},{8,9},{9,10},{10,1... | collective-permute-start | bytes 1769480 | tf_op jit(solution)/shard_map/ppermute | solution.py:438
  3.1 4.0 %collective-permute-start.4 = (bf16[2,1152,128]{2,1,0:T(8,128)(2,1)S(1)}, bf16[2,1152,128]{2,1,0:T(8,128)(2,1)S(1)}, u32[]{:S(2)}, u32[]{:S(2)}) collective-permute-start(bf16[2,1152,128]{2,1,0:T(8,128)(2,1)S(1)} %pad_maximum_fusion.refs_4_), channel_id=1, source_target_pairs={{0,7},{1,0},{2,1},{3,2},{4,3},{5,4},{6,5},{7,6},{8,15},{9,8},{10,9... | collective-permute-start | bytes 1769480 | tf_op jit(solution)/shard_map/ppermute | solution.py:438
  7.1 13.2 %collective-permute-done.3.refs_5_ = bf16[2,1152,128]{2,1,0:T(8,128)(2,1)S(1)} collective-permute-done((bf16[2,1152,128]{2,1,0:T(8,128)(2,1)S(1)}, bf16[2,1152,128]{2,1,0:T(8,128)(2,1)S(1)}, u32[]{:S(2)}, u32[]{:S(2)}) %collective-permute-start.3) | collective-permute-done | bytes 589856 | tf_op jit(solution)/shard_map/ppermute | solution.py:438
  20.4 3.2 %collective-permute-start.6 = (bf16[2,1152,128]{2,1,0:T(8,128)(2,1)S(1)}, bf16[2,1152,128]{2,1,0:T(8,128)(2,1)S(1)}, u32[]{:S(2)}, u32[]{:S(2)}) collective-permute-start(bf16[2,1152,128]{2,1,0:T(8,128)(2,1)S(1)} %collective-permute-done.4.refs_6_), channel_id=1, source_target_pairs={{0,7},{1,0},{2,1},{3,2},{4,3},{5,4},{6,5},{7,6},{8,15},{9,8},{10,9... | collective-permute-start | bytes 1769480 | tf_op jit(solution)/shard_map/ppermute | solution.py:438
  23.6 12.5 %collective-permute-done.5.refs_7_ = bf16[2,1152,128]{2,1,0:T(8,128)(2,1)S(1)} collective-permute-done((bf16[2,1152,128]{2,1,0:T(8,128)(2,1)S(1)}, bf16[2,1152,128]{2,1,0:T(8,128)(2,1)S(1)}, u32[]{:S(2)}, u32[]{:S(2)}) %collective-permute-start.5) | collective-permute-done | bytes 589856 | tf_op jit(solution)/shard_map/ppermute | solution.py:438
  36.1 3.2 %collective-permute-start.14 = (bf16[2,1152,128]{2,1,0:T(8,128)(2,1)S(1)}, bf16[2,1152,128]{2,1,0:T(8,128)(2,1)}, u32[]{:S(2)}, u32[]{:S(2)}) collective-permute-start(bf16[2,1152,128]{2,1,0:T(8,128)(2,1)S(1)} %collective-permute-done.6.refs_8_), channel_id=1, source_target_pairs={{0,7},{1,0},{2,1},{3,2},{4,3},{5,4},{6,5},{7,6},{8,15},{9,8},{10,9... | collective-permute-start | bytes 1769480 | tf_op jit(solution)/shard_map/ppermute | solution.py:438
  39.9 4.8 %dispatch.1 = (bf16[9,32,1024]{2,1,0:T(8,128)(2,1)}, bf16[9,32,1024]{2,1,0:T(8,128)(2,1)}, bf16[9,32,1024]{2,1,0:T(8,128)(2,1)}, bf16[9,32,1024]{2,1,0:T(8,128)(2,1)}, f32[1,448]{1,0:T(1,128)}, /*index=5*/s32[1]{0:T(128)}) custom-call(s32[3]{0:T(128)} %pad_add_fusion.place_ref, bf16[448,8192]{1,0:T(8,128)(2,1)} %hidden_ref.3, bf16[64,128]{1,0:T(8,128)(2,1)} %bitcast.9, ...), custom_call_target="tpu_custom_call" | custom-call | flops 1056964608 | bytes 4000000 | tf_op jit(solution)/shard_map/dispatch/pallas_call | solution.py:98
  44.7 1.7 %collective-permute-start = (bf16[9,32,1024]{2,1,0:T(8,128)(2,1)}, bf16[9,32,1024]{2,1,0:T(8,128)(2,1)S(1)}, u32[]{:S(2)}, u32[]{:S(2)}) collective-permute-start(bf16[9,32,1024]{2,1,0:T(8,128)(2,1)} %get-tuple-element.30), channel_id=1, source_target_pairs={{0,8},{8,16},{16,24},{24,0},{1,9},{9,17},{17,25},{25,1},{2,10},{10... | collective-permute-start | bytes 1769480 | tf_op jit(solution)/shard_map/ppermute | solution.py:438
  46.4 2.9 %collective-permute-start.1 = (bf16[9,32,1024]{2,1,0:T(8,128)(2,1)}, bf16[9,32,1024]{2,1,0:T(8,128)(2,1)S(1)}, u32[]{:S(2)}, u32[]{:S(2)}) collective-permute-start(bf16[9,32,1024]{2,1,0:T(8,128)(2,1)} %get-tuple-element.31), channel_id=1, source_target_pairs={{0,16},{8,24},{16,0},{24,8},{1,17},{9,25},{17,1},{25,9},{2,18},{10... | collective-permute-start | bytes 1769480 | tf_op jit(solution)/shard_map/ppermute | solution.py:438
  49.3 1.3 %collective-permute-start.2 = (bf16[9,32,1024]{2,1,0:T(8,128)(2,1)}, bf16[9,32,1024]{2,1,0:T(8,128)(2,1)S(1)}, u32[]{:S(2)}, u32[]{:S(2)}) collective-permute-start(bf16[9,32,1024]{2,1,0:T(8,128)(2,1)} %get-tuple-element.32), channel_id=1, source_target_pairs={{0,24},{8,0},{16,8},{24,16},{1,25},{9,1},{17,9},{25,17},{2,26},{10... | collective-permute-start | bytes 1769480 | tf_op jit(solution)/shard_map/ppermute | solution.py:438
  52.0 3.3 %collective-permute-start.16 = (bf16[1,1152,128]{2,1,0:T(8,128)(2,1)S(1)}, bf16[1,1152,128]{2,1,0:T(8,128)(2,1)S(1)}, u32[]{:S(2)}, u32[]{:S(2)}) collective-permute-start(bf16[1,1152,128]{2,1,0:T(8,128)(2,1)S(1)} %slice.9), channel_id=1, source_target_pairs={{0,7},{1,0},{2,1},{3,2},{4,3},{5,4},{6,5},{7,6},{8,15},{9,8},{10,9... | collective-permute-start | bytes 884744 | tf_op jit(solution)/shard_map/ppermute | solution.py:438
  55.3 6.0 %collective-permute-done.refs_1_ = bf16[9,32,1024]{2,1,0:T(8,128)(2,1)S(1)} collective-permute-done((bf16[9,32,1024]{2,1,0:T(8,128)(2,1)}, bf16[9,32,1024]{2,1,0:T(8,128)(2,1)S(1)}, u32[]{:S(2)}, u32[]{:S(2)}) %collective-permute-start) | collective-permute-done | bytes 589856 | tf_op jit(solution)/shard_map/ppermute | solution.py:438
  61.3 11.9 %collective-permute-done.1.refs_2_ = bf16[9,32,1024]{2,1,0:T(8,128)(2,1)S(1)} collective-permute-done((bf16[9,32,1024]{2,1,0:T(8,128)(2,1)}, bf16[9,32,1024]{2,1,0:T(8,128)(2,1)S(1)}, u32[]{:S(2)}, u32[]{:S(2)}) %collective-permute-start.1) | collective-permute-done | bytes 589856 | tf_op jit(solution)/shard_map/ppermute | solution.py:438
  73.2 2.2 %down_early.1 = (bf16[5,128,128]{2,1,0:T(8,128)(2,1)S(1)}, bf16[128,128]{1,0:T(8,128)(2,1)S(1)}) custom-call(s32[1]{0:T(128)} %get-tuple-element.28.hot_ref, bf16[9,32,1024]{2,1,0:T(8,128)(2,1)S(1)} %copy-done, bf16[9,32,1024]{2,1,0:T(8,128)(2,1)S(1)} %collective-permute-done.refs_1_, bf16[9,32,1024]{2,1,0:T(8,128)(2,1)S(1)} %collective-permute-done.1.refs_2_, ...), custom_call_target="tpu_custom_call" | custom-call | flops 335544320 | bytes 6000000 | tf_op jit(solution)/shard_map/down_early/pallas_call | solution.py:249
  75.7 2.5 %down_late.1 = bf16[4,128,128]{2,1,0:T(8,128)(2,1)S(1)} custom-call(s32[1]{0:T(128)} %get-tuple-element.28.hot_ref, bf16[9,32,1024]{2,1,0:T(8,128)(2,1)S(1)} %copy-done, bf16[9,32,1024]{2,1,0:T(8,128)(2,1)S(1)} %collective-permute-done.refs_1_, bf16[9,32,1024]{2,1,0:T(8,128)(2,1)S(1)} %collective-permute-done.1.refs_2_, ...), custom_call_target="tpu_custom_call" | custom-call | flops 268435456 | bytes 2000000 | tf_op jit(solution)/shard_map/down_late/pallas_call | solution.py:286
  79.7 1.3 %collective-permute-start.18 = (bf16[4,128,128]{2,1,0:T(8,128)(2,1)S(1)}, bf16[4,128,128]{2,1,0:T(8,128)(2,1)S(1)}, u32[]{:S(2)}, u32[]{:S(2)}) collective-permute-start(bf16[4,128,128]{2,1,0:T(8,128)(2,1)S(1)} %add_convert_fusion.5), channel_id=1, source_target_pairs={{0,64},{64,0},{128,192},{192,128},{1,65},{65,1},{129,193},{193,129... | collective-permute-start | bytes 393224 | tf_op jit(solution)/shard_map/ppermute | solution.py:442
  81.0 4.9 %collective-permute-done.8 = bf16[5,128,128]{2,1,0:T(8,128)(2,1)S(1)} collective-permute-done((bf16[5,128,128]{2,1,0:T(8,128)(2,1)S(1)}, bf16[5,128,128]{2,1,0:T(8,128)(2,1)S(1)}, u32[]{:S(2)}, u32[]{:S(2)}) %collective-permute-start.8) | collective-permute-done | bytes 163872 | tf_op jit(solution)/shard_map/ppermute | solution.py:442
  87.8 1.6 %collective-permute-start.19 = (bf16[4,128,128]{2,1,0:T(8,128)(2,1)S(1)}, bf16[4,128,128]{2,1,0:T(8,128)(2,1)S(1)}, u32[]{:S(2)}, u32[]{:S(2)}) collective-permute-start(bf16[4,128,128]{2,1,0:T(8,128)(2,1)S(1)} %add_convert_fusion.4), channel_id=1, source_target_pairs={{0,192},{64,128},{128,64},{192,0},{1,193},{65,129},{129,65},{193,1... | collective-permute-start | bytes 393224 | tf_op jit(solution)/shard_map/ppermute | solution.py:442
  89.4 4.6 %collective-permute-done.9 = bf16[5,128,128]{2,1,0:T(8,128)(2,1)S(1)} collective-permute-done((bf16[5,128,128]{2,1,0:T(8,128)(2,1)S(1)}, bf16[5,128,128]{2,1,0:T(8,128)(2,1)S(1)}, u32[]{:S(2)}, u32[]{:S(2)}) %collective-permute-start.9) | collective-permute-done | bytes 163872 | tf_op jit(solution)/shard_map/ppermute | solution.py:442
  95.2 2.2 %collective-permute-start.10 = (bf16[5,32,256]{2,1,0:T(8,128)(2,1)S(1)}, bf16[5,32,256]{2,1,0:T(8,128)(2,1)S(1)}, u32[]{:S(2)}, u32[]{:S(2)}) collective-permute-start(bf16[5,32,256]{2,1,0:T(8,128)(2,1)S(1)} %get-tuple-element.35), channel_id=1, source_target_pairs={{0,24},{8,0},{16,8},{24,16},{1,25},{9,1},{17,9},{25,17},{2,26},{10... | collective-permute-start | bytes 245768 | tf_op jit(solution)/shard_map/ppermute | solution.py:438
  99.2 2.1 %up_prepare.1 = (bf16[4,256,256]{2,1,0:T(8,128)(2,1)S(1)}, bf16[4,128,256]{2,1,0:T(8,128)(2,1)S(1)}) custom-call(s32[1]{0:T(128)} %get-tuple-element.28.hot_ref, bf16[9,32,1024]{2,1,0:T(8,128)(2,1)S(1)} %copy-done, bf16[9,32,1024]{2,1,0:T(8,128)(2,1)S(1)} %collective-permute-done.refs_1_, bf16[9,32,1024]{2,1,0:T(8,128)(2,1)S(1)} %collective-permute-done.1.refs_2_, ...), custom_call_target="tpu_custom_call" | custom-call | flops 4000000 | bytes 1500000 | tf_op jit(solution)/shard_map/up_prepare/pallas_call | solution.py:363
  101.6 2.6 %collective-permute-start.20 = (bf16[4,32,256]{2,1,0:T(8,128)(2,1)S(1)}, bf16[4,32,256]{2,1,0:T(8,128)(2,1)S(1)}, u32[]{:S(2)}, u32[]{:S(2)}) collective-permute-start(bf16[4,32,256]{2,1,0:T(8,128)(2,1)S(1)} %get-tuple-element.42), channel_id=1, source_target_pairs={{0,24},{8,0},{16,8},{24,16},{1,25},{9,1},{17,9},{25,17},{2,26},{10... | collective-permute-start | bytes 196616 | tf_op jit(solution)/shard_map/ppermute | solution.py:438
  106.0 10.7 %base.1 = (f32[448,256]{1,0:T(8,128)}, f32[448,128]{1,0:T(8,128)}) custom-call(bf16[448,8192]{1,0:T(8,128)(2,1)} %hidden_ref.3, bf16[64,128]{1,0:T(8,128)(2,1)} %bitcast.10, bf16[16384,128]{1,0:T(8,128)(2,1)} %bitcast.8), custom_call_target="tpu_custom_call" | custom-call | flops 1879048192 | bytes 12000000 | tf_op jit(solution)/shard_map/base/pallas_call | solution.py:190
  118.9 1.4 %shard_map.73.sum_ref = f32[448,256]{1,0:T(8,128)S(1)} custom-call(f32[448,256]{1,0:T(8,128)S(1)} %copy-done.2, f32[448,128]{1,0:T(8,128)S(1)} %copy-done.1, f32[448,128]{1,0:T(8,128)S(1)} %columns.1.dst_ref, bf16[5,32,256]{2,1,0:T(8,128)(2,1)S(1)} %copy-done.4, bf16[5,32,256]{2,1,0:T(8,128)(2,1)S(1)} %copy-done.6, ...), custom_call_target="tpu_custom_call" | custom-call | flops 234881024 | bytes 1500000 | tf_op jit(solution)/shard_map/pallas_call | solution.py:425
  (59 shorter events, 15.3 us)
Async XLA Ops:
  1.1 19.3 %collective-permute-start.3 = (bf16[2,1152,128]{2,1,0:T(8,128)(2,1)S(1)}, bf16[2,1152,128]{2,1,0:T(8,128)(2,1)S(1)}, u32[]{:S(2)}, u32[]{:S(2)}) collective-permute-start(bf16[2,1152,128]{2,1,0:T(8,128)(2,1)S(1)} %pad_maximum_fusion.refs_4_), channel_id=1, source_target_pairs={{0,1},{1,2},{2,3},{3,4},{4,5},{5,6},{6,7},{7,0},{8,9},{9,10},{10,1... | collective-permute-start | bytes 1769480 | tf_op jit(solution)/shard_map/ppermute | solution.py:438
  3.1 17.3 %collective-permute-start.4 = (bf16[2,1152,128]{2,1,0:T(8,128)(2,1)S(1)}, bf16[2,1152,128]{2,1,0:T(8,128)(2,1)S(1)}, u32[]{:S(2)}, u32[]{:S(2)}) collective-permute-start(bf16[2,1152,128]{2,1,0:T(8,128)(2,1)S(1)} %pad_maximum_fusion.refs_4_), channel_id=1, source_target_pairs={{0,7},{1,0},{2,1},{3,2},{4,3},{5,4},{6,5},{7,6},{8,15},{9,8},{10,9... | collective-permute-start | bytes 1769480 | tf_op jit(solution)/shard_map/ppermute | solution.py:438
  20.4 15.7 %collective-permute-start.5 = (bf16[2,1152,128]{2,1,0:T(8,128)(2,1)S(1)}, bf16[2,1152,128]{2,1,0:T(8,128)(2,1)S(1)}, u32[]{:S(2)}, u32[]{:S(2)}) collective-permute-start(bf16[2,1152,128]{2,1,0:T(8,128)(2,1)S(1)} %collective-permute-done.3.refs_5_), channel_id=1, source_target_pairs={{0,1},{1,2},{2,3},{3,4},{4,5},{5,6},{6,7},{7,0},{8,9},{9,10},{10,1... | collective-permute-start | bytes 1769480 | tf_op jit(solution)/shard_map/ppermute | solution.py:438
  20.4 15.7 %collective-permute-start.6 = (bf16[2,1152,128]{2,1,0:T(8,128)(2,1)S(1)}, bf16[2,1152,128]{2,1,0:T(8,128)(2,1)S(1)}, u32[]{:S(2)}, u32[]{:S(2)}) collective-permute-start(bf16[2,1152,128]{2,1,0:T(8,128)(2,1)S(1)} %collective-permute-done.4.refs_6_), channel_id=1, source_target_pairs={{0,7},{1,0},{2,1},{3,2},{4,3},{5,4},{6,5},{7,6},{8,15},{9,8},{10,9... | collective-permute-start | bytes 1769480 | tf_op jit(solution)/shard_map/ppermute | solution.py:438
  36.1 14.8 %collective-permute-start.13 = (bf16[2,1152,128]{2,1,0:T(8,128)(2,1)S(1)}, bf16[2,1152,128]{2,1,0:T(8,128)(2,1)S(1)}, u32[]{:S(2)}, u32[]{:S(2)}) collective-permute-start(bf16[2,1152,128]{2,1,0:T(8,128)(2,1)S(1)} %collective-permute-done.5.refs_7_), channel_id=1, source_target_pairs={{0,1},{1,2},{2,3},{3,4},{4,5},{5,6},{6,7},{7,0},{8,9},{9,10},{10,1... | collective-permute-start | bytes 1769480 | tf_op jit(solution)/shard_map/ppermute | solution.py:438
  36.1 15.0 %collective-permute-start.14 = (bf16[2,1152,128]{2,1,0:T(8,128)(2,1)S(1)}, bf16[2,1152,128]{2,1,0:T(8,128)(2,1)}, u32[]{:S(2)}, u32[]{:S(2)}) collective-permute-start(bf16[2,1152,128]{2,1,0:T(8,128)(2,1)S(1)} %collective-permute-done.6.refs_8_), channel_id=1, source_target_pairs={{0,7},{1,0},{2,1},{3,2},{4,3},{5,4},{6,5},{7,6},{8,15},{9,8},{10,9... | collective-permute-start | bytes 1769480 | tf_op jit(solution)/shard_map/ppermute | solution.py:438
  44.7 28.5 %copy-start = (bf16[9,32,1024]{2,1,0:T(8,128)(2,1)S(1)}, bf16[9,32,1024]{2,1,0:T(8,128)(2,1)}, u32[]{:S(2)}) copy-start(bf16[9,32,1024]{2,1,0:T(8,128)(2,1)} %get-tuple-element.29.refs_0_) | copy-start | bytes 1769476
  44.7 16.6 %collective-permute-start = (bf16[9,32,1024]{2,1,0:T(8,128)(2,1)}, bf16[9,32,1024]{2,1,0:T(8,128)(2,1)S(1)}, u32[]{:S(2)}, u32[]{:S(2)}) collective-permute-start(bf16[9,32,1024]{2,1,0:T(8,128)(2,1)} %get-tuple-element.30), channel_id=1, source_target_pairs={{0,8},{8,16},{16,24},{24,0},{1,9},{9,17},{17,25},{25,1},{2,10},{10... | collective-permute-start | bytes 1769480 | tf_op jit(solution)/shard_map/ppermute | solution.py:438
  46.4 26.8 %collective-permute-start.1 = (bf16[9,32,1024]{2,1,0:T(8,128)(2,1)}, bf16[9,32,1024]{2,1,0:T(8,128)(2,1)S(1)}, u32[]{:S(2)}, u32[]{:S(2)}) collective-permute-start(bf16[9,32,1024]{2,1,0:T(8,128)(2,1)} %get-tuple-element.31), channel_id=1, source_target_pairs={{0,16},{8,24},{16,0},{24,8},{1,17},{9,25},{17,1},{25,9},{2,18},{10... | collective-permute-start | bytes 1769480 | tf_op jit(solution)/shard_map/ppermute | solution.py:438
  49.3 23.9 %collective-permute-start.2 = (bf16[9,32,1024]{2,1,0:T(8,128)(2,1)}, bf16[9,32,1024]{2,1,0:T(8,128)(2,1)S(1)}, u32[]{:S(2)}, u32[]{:S(2)}) collective-permute-start(bf16[9,32,1024]{2,1,0:T(8,128)(2,1)} %get-tuple-element.32), channel_id=1, source_target_pairs={{0,24},{8,0},{16,8},{24,16},{1,25},{9,1},{17,9},{25,17},{2,26},{10... | collective-permute-start | bytes 1769480 | tf_op jit(solution)/shard_map/ppermute | solution.py:438
  51.0 24.7 %collective-permute-start.15 = (bf16[1,1152,128]{2,1,0:T(8,128)(2,1)S(1)}, bf16[1,1152,128]{2,1,0:T(8,128)(2,1)S(1)}, u32[]{:S(2)}, u32[]{:S(2)}) collective-permute-start(bf16[1,1152,128]{2,1,0:T(8,128)(2,1)S(1)} %slice.8), channel_id=1, source_target_pairs={{0,1},{1,2},{2,3},{3,4},{4,5},{5,6},{6,7},{7,0},{8,9},{9,10},{10,1... | collective-permute-start | bytes 884744 | tf_op jit(solution)/shard_map/ppermute | solution.py:438
  52.0 23.6 %collective-permute-start.16 = (bf16[1,1152,128]{2,1,0:T(8,128)(2,1)S(1)}, bf16[1,1152,128]{2,1,0:T(8,128)(2,1)S(1)}, u32[]{:S(2)}, u32[]{:S(2)}) collective-permute-start(bf16[1,1152,128]{2,1,0:T(8,128)(2,1)S(1)} %slice.9), channel_id=1, source_target_pairs={{0,7},{1,0},{2,1},{3,2},{4,3},{5,4},{6,5},{7,6},{8,15},{9,8},{10,9... | collective-permute-start | bytes 884744 | tf_op jit(solution)/shard_map/ppermute | solution.py:438
  75.3 3.4 %collective-permute-start.7 = (bf16[5,128,128]{2,1,0:T(8,128)(2,1)S(1)}, bf16[5,128,128]{2,1,0:T(8,128)(2,1)S(1)}, u32[]{:S(2)}, u32[]{:S(2)}) collective-permute-start(bf16[5,128,128]{2,1,0:T(8,128)(2,1)S(1)} %get-tuple-element.33), channel_id=1, source_target_pairs={{0,32},{32,0},{1,33},{33,1},{2,34},{34,2},{3,35},{35,3},{4,36},{36... | collective-permute-start | bytes 491528 | tf_op jit(solution)/shard_map/ppermute | solution.py:442
  78.1 1.5 %collective-permute-start.17 = (bf16[4,128,128]{2,1,0:T(8,128)(2,1)S(1)}, bf16[4,128,128]{2,1,0:T(8,128)(2,1)S(1)}, u32[]{:S(2)}, u32[]{:S(2)}) collective-permute-start(bf16[4,128,128]{2,1,0:T(8,128)(2,1)S(1)} %down_late.1), channel_id=1, source_target_pairs={{0,32},{32,0},{1,33},{33,1},{2,34},{34,2},{3,35},{35,3},{4,36},{36... | collective-permute-start | bytes 393224 | tf_op jit(solution)/shard_map/ppermute | solution.py:442
  78.8 7.2 %collective-permute-start.8 = (bf16[5,128,128]{2,1,0:T(8,128)(2,1)S(1)}, bf16[5,128,128]{2,1,0:T(8,128)(2,1)S(1)}, u32[]{:S(2)}, u32[]{:S(2)}) collective-permute-start(bf16[5,128,128]{2,1,0:T(8,128)(2,1)S(1)} %add_convert_fusion.2), channel_id=1, source_target_pairs={{0,64},{64,0},{128,192},{192,128},{1,65},{65,1},{129,193},{193,129... | collective-permute-start | bytes 491528 | tf_op jit(solution)/shard_map/ppermute | solution.py:442
  79.7 8.1 %collective-permute-start.18 = (bf16[4,128,128]{2,1,0:T(8,128)(2,1)S(1)}, bf16[4,128,128]{2,1,0:T(8,128)(2,1)S(1)}, u32[]{:S(2)}, u32[]{:S(2)}) collective-permute-start(bf16[4,128,128]{2,1,0:T(8,128)(2,1)S(1)} %add_convert_fusion.5), channel_id=1, source_target_pairs={{0,64},{64,0},{128,192},{192,128},{1,65},{65,1},{129,193},{193,129... | collective-permute-start | bytes 393224 | tf_op jit(solution)/shard_map/ppermute | solution.py:442
  86.0 8.0 %collective-permute-start.9 = (bf16[5,128,128]{2,1,0:T(8,128)(2,1)S(1)}, bf16[5,128,128]{2,1,0:T(8,128)(2,1)S(1)}, u32[]{:S(2)}, u32[]{:S(2)}) collective-permute-start(bf16[5,128,128]{2,1,0:T(8,128)(2,1)S(1)} %add_convert_fusion.1), channel_id=1, source_target_pairs={{0,192},{64,128},{128,64},{192,0},{1,193},{65,129},{129,65},{193,1... | collective-permute-start | bytes 491528 | tf_op jit(solution)/shard_map/ppermute | solution.py:442
  87.8 13.4 %collective-permute-start.19 = (bf16[4,128,128]{2,1,0:T(8,128)(2,1)S(1)}, bf16[4,128,128]{2,1,0:T(8,128)(2,1)S(1)}, u32[]{:S(2)}, u32[]{:S(2)}) collective-permute-start(bf16[4,128,128]{2,1,0:T(8,128)(2,1)S(1)} %add_convert_fusion.4), channel_id=1, source_target_pairs={{0,192},{64,128},{128,64},{192,0},{1,193},{65,129},{129,65},{193,1... | collective-permute-start | bytes 393224 | tf_op jit(solution)/shard_map/ppermute | solution.py:442
  95.2 10.2 %collective-permute-start.10 = (bf16[5,32,256]{2,1,0:T(8,128)(2,1)S(1)}, bf16[5,32,256]{2,1,0:T(8,128)(2,1)S(1)}, u32[]{:S(2)}, u32[]{:S(2)}) collective-permute-start(bf16[5,32,256]{2,1,0:T(8,128)(2,1)S(1)} %get-tuple-element.35), channel_id=1, source_target_pairs={{0,24},{8,0},{16,8},{24,16},{1,25},{9,1},{17,9},{25,17},{2,26},{10... | collective-permute-start | bytes 245768 | tf_op jit(solution)/shard_map/ppermute | solution.py:438
  97.4 19.5 %collective-permute-start.11 = (bf16[5,32,256]{2,1,0:T(8,128)(2,1)}, bf16[5,32,256]{2,1,0:T(8,128)(2,1)}, u32[]{:S(2)}, u32[]{:S(2)}) collective-permute-start(bf16[5,32,256]{2,1,0:T(8,128)(2,1)} %get-tuple-element.36), channel_id=1, source_target_pairs={{0,16},{8,24},{16,0},{24,8},{1,17},{9,25},{17,1},{25,9},{2,18},{10... | collective-permute-start | bytes 245768 | tf_op jit(solution)/shard_map/ppermute | solution.py:438
  98.5 18.4 %collective-permute-start.12 = (bf16[5,32,256]{2,1,0:T(8,128)(2,1)}, bf16[5,32,256]{2,1,0:T(8,128)(2,1)}, u32[]{:S(2)}, u32[]{:S(2)}) collective-permute-start(bf16[5,32,256]{2,1,0:T(8,128)(2,1)} %get-tuple-element.37), channel_id=1, source_target_pairs={{0,8},{8,16},{16,24},{24,0},{1,9},{9,17},{17,25},{25,1},{2,10},{10... | collective-permute-start | bytes 245768 | tf_op jit(solution)/shard_map/ppermute | solution.py:438
  101.6 18.7 %collective-permute-start.20 = (bf16[4,32,256]{2,1,0:T(8,128)(2,1)S(1)}, bf16[4,32,256]{2,1,0:T(8,128)(2,1)S(1)}, u32[]{:S(2)}, u32[]{:S(2)}) collective-permute-start(bf16[4,32,256]{2,1,0:T(8,128)(2,1)S(1)} %get-tuple-element.42), channel_id=1, source_target_pairs={{0,24},{8,0},{16,8},{24,16},{1,25},{9,1},{17,9},{25,17},{2,26},{10... | collective-permute-start | bytes 196616 | tf_op jit(solution)/shard_map/ppermute | solution.py:438
  104.2 16.1 %collective-permute-start.21 = (bf16[4,32,256]{2,1,0:T(8,128)(2,1)S(1)}, bf16[4,32,256]{2,1,0:T(8,128)(2,1)S(1)}, u32[]{:S(2)}, u32[]{:S(2)}) collective-permute-start(bf16[4,32,256]{2,1,0:T(8,128)(2,1)S(1)} %get-tuple-element.43), channel_id=1, source_target_pairs={{0,16},{8,24},{16,0},{24,8},{1,17},{9,25},{17,1},{25,9},{2,18},{10... | collective-permute-start | bytes 196616 | tf_op jit(solution)/shard_map/ppermute | solution.py:438
  106.0 14.3 %collective-permute-start.22 = (bf16[4,32,256]{2,1,0:T(8,128)(2,1)S(1)}, bf16[4,32,256]{2,1,0:T(8,128)(2,1)S(1)}, u32[]{:S(2)}, u32[]{:S(2)}) collective-permute-start(bf16[4,32,256]{2,1,0:T(8,128)(2,1)S(1)} %get-tuple-element.44), channel_id=1, source_target_pairs={{0,8},{8,16},{16,24},{24,0},{1,9},{9,17},{17,25},{25,1},{2,10},{10... | collective-permute-start | bytes 196616 | tf_op jit(solution)/shard_map/ppermute | solution.py:438
  (7 other events, 41.2 us)

commit v4 on v3

--- a/solution.py
+++ b/solution.py
@@ -1,3 +1,5 @@
+import functools
+
 import jax
 import jax.numpy as jnp
 from jax import lax
@@ -24,6 +26,7 @@
 LATE = BUCKETS - EARLY
 ORDER = (0, 7, 1, 6, 2, 5, 3, 4)
 RANK2 = 128
+CHUNK = COLS + RANK2
 VMEM_LIMIT = 24 * 1024 * 1024
 
 
@@ -46,6 +49,28 @@
 
 def scalars():
     return pl.BlockSpec(memory_space=pltpu.SMEM)
+
+
+def pack_kernel(down_ref, up_ref, zero_ref, one_ref):
+    for a, out_ref in enumerate((zero_ref, one_ref)):
+        out_ref[:COLS] = down_ref[a]
+        out_ref[COLS:] = up_ref[a]
+
+
+def pack(down_weight, up_planes):
+    return pl.pallas_call(
+        pack_kernel,
+        grid=(1,),
+        in_specs=[
+            pl.BlockSpec((2, COLS, 128), lambda i: (0, 0, 0)),
+            pl.BlockSpec((2, RANK2, 128), lambda i: (0, 0, 0)),
+        ],
+        out_specs=[pl.BlockSpec((CHUNK, 128), lambda i: (0, 0))] * 2,
+        out_shape=[jax.ShapeDtypeStruct((CHUNK, 128), BF16)] * 2,
+        compiler_params=params(),
+        cost_estimate=pl.CostEstimate(flops=0, bytes_accessed=1_200_000, transcendentals=0),
+        name="pack",
+    )(down_weight, up_planes)
 
 
 def gain_row(gain):
@@ -135,16 +160,16 @@
     )(row)
 
 
-def base_kernel(
-    hidden_ref, gain_ref, mixed_ref, out_ref, inv_ref, square_ref, scaled_ref, weight_ref
-):
+def base_kernel(last, hidden_ref, gain_ref, mixed_ref, *refs):
+    out_ref, square_ref, scaled_ref, weight_ref = refs[-4:]
     step = pl.program_id(0)
     gain = gain_row(gain_ref[...]).astype(BF16)
     rows = 64
 
     @pl.when(step == 0)
     def _():
-        square_ref[...] = jnp.zeros_like(square_ref)
+        out_ref[...] = refs[0][...] if last else jnp.zeros_like(out_ref)
+        square_ref[...] = refs[1][...] if last else jnp.zeros_like(square_ref)
 
     for r in range(0, TOK, rows):
         square = square_ref[r : r + rows, :]
@@ -167,34 +192,34 @@
         weight_ref[d : d + 128, 128:] = parted[128:, :128]
         weight_ref[d + 128 : d + 256, :128] = parted[:128, 128:]
         weight_ref[d + 128 : d + 256, 128:] = parted[128:, 128:]
-    term = jnp.dot(scaled_ref[...], weight_ref[...], preferred_element_type=F32)
-
-    @pl.when(step == 0)
-    def _():
-        out_ref[...] = term
-
-    @pl.when(step > 0)
-    def _():
-        out_ref[...] += term
-
-    @pl.when(step == pl.num_programs(0) - 1)
-    def _():
-        mean = jnp.sum(square_ref[...], axis=1, keepdims=True) * (1.0 / DIM)
-        inv = lax.rsqrt(mean + epsilon)
-        out_ref[...] = out_ref[...] * inv
-        inv_ref[...] = jnp.broadcast_to(inv, (TOK, 128))
-
-
-def base_projection(hidden, gain, weight):
+    out_ref[...] += jnp.dot(scaled_ref[...], weight_ref[...], preferred_element_type=F32)
+
+    if last:
+
+        @pl.when(step == pl.num_programs(0) - 1)
+        def _():
+            mean = jnp.sum(square_ref[...], axis=1, keepdims=True) * (1.0 / DIM)
+            inv = lax.rsqrt(mean + epsilon)
+            out_ref[...] = out_ref[...] * inv
+            square_ref[...] = jnp.broadcast_to(inv, (TOK, 128))
+
+
+def base_projection(part, hidden, gain, weight, *begun):
     tile = 1024
-    return pl.pallas_call(
-        base_kernel,
-        grid=(DIM // tile,),
+    steps = DIM // tile // 2
+    first = part * steps
+    return pl.pallas_call(
+        functools.partial(base_kernel, part == 1),
+        grid=(steps,),
         in_specs=[
-            pl.BlockSpec((TOK, tile), lambda k: (0, k)),
-            pl.BlockSpec((8, 128), lambda k: (k, 0)),
-            pl.BlockSpec((2 * tile, 128), lambda k: (k, 0)),
-        ],
+            pl.BlockSpec((TOK, tile), lambda k: (0, first + k)),
+            pl.BlockSpec((8, 128), lambda k: (first + k, 0)),
+            pl.BlockSpec((2 * tile, 128), lambda k: (first + k, 0)),
+        ]
+        + [
+            pl.BlockSpec((TOK, 256), lambda k: (0, 0)),
+            pl.BlockSpec((TOK, 128), lambda k: (0, 0)),
+        ][: len(begun)],
         out_specs=[
             pl.BlockSpec((TOK, 256), lambda k: (0, 0)),
             pl.BlockSpec((TOK, 128), lambda k: (0, 0)),
@@ -203,12 +228,12 @@
             jax.ShapeDtypeStruct((TOK, 256), F32),
             jax.ShapeDtypeStruct((TOK, 128), F32),
         ],
-        scratch_shapes=[pltpu.VMEM((TOK, 128), F32), pltpu.VMEM((TOK, tile), BF16), pltpu.VMEM((tile, 256), BF16)],
-        cost_estimate=pl.CostEstimate(
-            flops=2 * TOK * DIM * 256, bytes_accessed=12_000_000, transcendentals=0
+        scratch_shapes=[pltpu.VMEM((TOK, tile), BF16), pltpu.VMEM((tile, 256), BF16)],
+        cost_estimate=pl.CostEstimate(
+            flops=TOK * DIM * 256, bytes_accessed=6_000_000, transcendentals=0
         ),
         name="base",
-    )(hidden, gain, weight)
+    )(hidden, gain, weight, *begun)
 
 
 def local_column(head):
@@ -230,12 +255,11 @@
 
 def down_early_kernel(hot_ref, *refs):
     received = refs[:NY]
-    chunks = refs[NY : NY + EARLY]
-    low_ref, more_ref = refs[NY + EARLY :]
+    chunks = refs[NY:-2]
+    low_ref, more_ref = refs[-2:]
     more_ref[...] = jnp.zeros_like(more_ref)
     for k in range(EARLY):
-        c = chunks[k]
-        weight = jnp.concatenate([c[0, :COLS], c[1, :COLS]], axis=1)
+        weight = jnp.concatenate([chunks[2 * k][:COLS], chunks[2 * k + 1][:COLS]], axis=1)
         rows, local = bucket_rows(received, k)
         low_ref[k] = project(rows, local, weight).astype(BF16)
 
@@ -248,7 +272,7 @@
 def down_early(hot, received, chunks):
     return pl.pallas_call(
         down_early_kernel,
-        in_specs=[scalars()] + [whole()] * (NY + EARLY),
+        in_specs=[scalars()] + [whole()] * (NY + len(chunks)),
         out_specs=[whole()] * 2,
         out_shape=[
             jax.ShapeDtypeStruct((EARLY, NY * BLOCK, RANK2), BF16),
@@ -268,11 +292,7 @@
     more_ref, low_ref = refs[-2:]
     low_ref[LATE - 1] = more_ref[...]
     for at in range(LATE - 1):
-        if at < LATE - 2:
-            zero, one = chunks[at][0, :COLS], chunks[at][1, :COLS]
-        else:
-            zero, one = chunks[at][0, :COLS], chunks[at + 1][0, :COLS]
-        weight = jnp.concatenate([zero, one], axis=1)
+        weight = jnp.concatenate([chunks[2 * at][:COLS], chunks[2 * at + 1][:COLS]], axis=1)
         rows, local = bucket_rows(received, EARLY + at)
         low_ref[at] = project(rows, local, weight).astype(BF16)
 
@@ -311,19 +331,19 @@
     ).astype(BF16)
 
 
-def up_rows(chunk):
-    return jnp.concatenate([chunk[0, COLS:], chunk[1, COLS:]], axis=0)
+def up_rows(zero, one):
+    return jnp.concatenate([zero[COLS:], one[COLS:]], axis=0)
 
 
 def up_early_kernel(low_ref, *refs):
     received = refs[:NY]
-    chunks = refs[NY : NY + EARLY]
-    outs = refs[NY + EARLY :]
+    chunks = refs[NY:-NY]
+    outs = refs[-NY:]
     for k in range(EARLY):
         local = jnp.concatenate([local_column(r[k, :, :128]) for r in received], axis=0)
         low = low_ref[k].astype(F32)
         delta = jnp.dot(
-            spread(low, local), up_matrix(up_rows(chunks[k])), preferred_element_type=F32
+            spread(low, local), up_matrix(up_rows(chunks[2 * k], chunks[2 * k + 1])), preferred_element_type=F32
         ).astype(BF16)
         for s in range(NY):
             outs[s][k] = delta[s * BLOCK : (s + 1) * BLOCK]
@@ -332,7 +352,7 @@
 def up_early(low, received, chunks):
     return pl.pallas_call(
         up_early_kernel,
-        in_specs=[whole()] * (1 + NY + EARLY),
+        in_specs=[whole()] * (1 + NY + len(chunks)),
         out_specs=[whole()] * NY,
         out_shape=[jax.ShapeDtypeStruct((EARLY, BLOCK, 256), BF16)] * NY,
         compiler_params=params(),
@@ -347,14 +367,15 @@
     received = refs[:NY]
     chunks = refs[NY:-2]
     matrix_ref, mask_ref = refs[-2:]
-    ups = [up_rows(c) for c in chunks[:-2]]
-    ups.append(jnp.concatenate([chunks[-2][0, COLS:], chunks[-1][0, COLS:]], axis=0))
+    ups = [up_rows(chunks[2 * k], chunks[2 * k + 1]) for k in range(NZ - 1)]
     hot_up = ups[0].astype(F32)
-    for k in range(1, NZ):
+    for k in range(1, NZ - 1):
         hot_up = jnp.where(hot_ref[0] == k, ups[k].astype(F32), hot_up)
     ones = jnp.ones((NY * BLOCK, RANK2), F32)
+    for at in range(LATE - 2):
+        matrix_ref[at] = up_matrix(ups[EARLY + at])
+    matrix_ref[LATE - 2] = up_matrix(hot_up)
     for at in range(LATE):
-        matrix_ref[at] = up_matrix(hot_up if at == LATE - 1 else ups[EARLY + at])
         local = jnp.concatenate([local_column(r[EARLY + at, :, :128]) for r in received], axis=0)
         mask_ref[at] = spread(ones, local)
 
@@ -365,7 +386,7 @@
         in_specs=[scalars()] + [whole()] * (NY + len(chunks)),
         out_specs=[whole()] * 2,
         out_shape=[
-            jax.ShapeDtypeStruct((LATE, 256, 256), BF16),
+            jax.ShapeDtypeStruct((LATE - 1, 256, 256), BF16),
             jax.ShapeDtypeStruct((LATE, NY * BLOCK, 256), BF16),
         ],
         compiler_params=params(),
@@ -376,19 +397,24 @@
     )(hot, *received, *chunks)
 
 
-def up_late_kernel(low_ref, matrix_ref, mask_ref, *outs):
+def up_late_kernel(hot_ref, low_ref, matrix_ref, mask_ref, zero_ref, one_ref, *outs):
+    last = up_matrix(up_rows(zero_ref, one_ref))
+    hot = jnp.where(
+        hot_ref[0] == NZ - 1, last.astype(F32), matrix_ref[LATE - 2].astype(F32)
+    ).astype(BF16)
     for at in range(LATE):
         low = low_ref[at]
         both = jnp.concatenate([low, low], axis=1) * mask_ref[at]
-        delta = jnp.dot(both, matrix_ref[at], preferred_element_type=F32).astype(BF16)
+        matrix = matrix_ref[at] if at < LATE - 2 else (last if at == LATE - 2 else hot)
+        delta = jnp.dot(both, matrix, preferred_element_type=F32).astype(BF16)
         for s in range(NY):
             outs[s][at] = delta[s * BLOCK : (s + 1) * BLOCK]
 
 
-def up_late(low, matrix, mask):
+def up_late(hot, low, matrix, mask, last):
     return pl.pallas_call(
         up_late_kernel,
-        in_specs=[whole()] * 3,
+        in_specs=[scalars()] + [whole()] * 5,
         out_specs=[whole()] * NY,
         out_shape=[jax.ShapeDtypeStruct((LATE, BLOCK, 256), BF16)] * NY,
         compiler_params=params(),
@@ -396,7 +422,7 @@
             flops=2 * 512 * 256 * 256, bytes_accessed=1_000_000, transcendentals=0
         ),
         name="up_late",
-    )(low, matrix, mask)
+    )(hot, low, matrix, mask, *last)
 
 
 def collect(dst, first, count, back):
@@ -454,17 +480,17 @@
     places = [tp, lax.axis_index("y"), lax.axis_index("z")]
     place = jnp.stack(places).astype(jnp.int32)
 
-    own = jnp.concatenate([down_weight, up_weight.reshape(2, RANK2, 128)], axis=1)
+    own = pack(down_weight, up_weight.reshape(2, RANK2, 128))
     chunks = {0: own}
     plus = minus = own
     for k in range(1, 4):
-        plus = shift(plus, "z", NZ, 1)
-        minus = shift(minus, "z", NZ, -1)
+        plus = [shift(plus[a], "z", NZ, 1) for a in range(2)]
+        minus = [shift(minus[a], "z", NZ, -1) for a in range(2)]
         chunks[NZ - k] = plus
         chunks[k] = minus
-    last = [shift(plus[:1], "z", NZ, 1), shift(minus[1:], "z", NZ, -1)]
-    early = [chunks[dz] for dz in ORDER[:EARLY]]
-    late = [chunks[dz] for dz in ORDER[EARLY:-1]] + last
+    last = [shift(plus[0], "z", NZ, 1), shift(minus[1], "z", NZ, -1)]
+    early = [a for dz in ORDER[:EARLY] for a in chunks[dz]]
+    late = [a for dz in ORDER[EARLY:-1] for a in chunks[dz]] + last
 
     gains = gain.reshape(DIM // 128, 128)
     send, dst, hot = dispatch(
@@ -473,7 +499,9 @@
     dst = columns(dst)
     received = [send[0]] + [shift(send[dy], "y", NY, dy) for dy in range(1, NY)]
 
-    base, inv = base_projection(hidden, gains, kv_weight.reshape(2 * DIM, 128))
+    mixed = kv_weight.reshape(2 * DIM, 128)
+    base, inv = base_projection(0, hidden, gains, mixed)
+    base, inv = base_projection(1, hidden, gains, mixed, base, inv)
 
     low, more = down_early(hot, received, early)
     low = sum_over_tp(low)
@@ -482,9 +510,9 @@
     summed = finish(finish_early_kernel, base, inv, dst, back, F32)
 
     low = down_late(hot, received, late, more)
-    matrix, mask = up_prepare(hot, received, early + late)
+    matrix, mask = up_prepare(hot, received, early + late[:-2])
     low = sum_over_tp(low)
-    delta = up_late(low, matrix, mask)
+    delta = up_late(hot, low, matrix, mask, last)
     back = [delta[0]] + [shift(delta[dy], "y", NY, -dy) for dy in range(1, NY)]
     out = finish(finish_late_kernel, summed, inv, dst, back, BF16)
     return out.reshape(TOK, 2, 128)

time: 123 us -> 117 us (0.951)
  waiting for transfers between devices: 54.6 us -> 26.7 us
  starting transfers between devices: 34.7 us -> 44.8 us
  local copies, waits for them, and re-layouts: 4.35 us -> 11 us
  Pallas kernels: 25.6 us -> 31.3 us
    ppermute x17 -> x23, waiting for transfers between devices: 43.9 us -> 21.6 us  [shift(): return lax.ppermute(x, axis, [(i, (i + by) % size) for i in range(size)])]
    ppermute x17 -> x23, starting transfers between devices: 29.6 us -> 40.2 us  [shift(): return lax.ppermute(x, axis, [(i, (i + by) % size) for i in range(size)])]
    unnamed x16 -> x44, local copies, waits for them, and re-layouts: 2.6 us -> 10.2 us
    ppermute x6, waiting for transfers between devices: 10.8 us -> 5.16 us  [pair_sum(): other = lax.ppermute(x, axis, [(i, i ^ flip) for i in range(size)])]
    pallas_call x3 -> x5, Pallas kernels: 12.1 us -> 16.3 us  [the longest x2 12.2 us: base_projection(): pl.pallas_call(functools.partial(base_kernel, part == 1), grid=(steps,),...]
    pallas_call x1, Pallas kernels: 2.15 us -> 3.89 us  [down_early(): pl.pallas_call(down_early_kernel, in_specs=[scalars()] + [whole()] * (NY...]
  transfers between devices with their start and end apart: 23 -> 29, of which waited for: 8 -> 8; matrix products, arithmetic and copies ran while one was open for 1% -> 2% of each run, Pallas kernels for 21% -> 27%
where the time goes in v4:
time: 117 us; the launch traced here: 116 us
  starting transfers between devices  44.8 us (38%)
  Pallas kernels  31.3 us (27%)
  waiting for transfers between devices  26.7 us (23%)
  local copies, waits for them, and re-layouts  11 us (9%)
  other arithmetic  1.83 us (2%)
    ppermute x23, starting transfers between devices, shift(): return lax.ppermute(x, axis, [(i, (i + by) % size) for i in range(size)])  40.2 us
    ppermute x23, waiting for transfers between devices, shift(): return lax.ppermute(x, axis, [(i, (i + by) % size) for i in range(size)])  21.6 us
    pallas_call x2, Pallas kernels, base_projection(): pl.pallas_call(functools.partial(base_kernel, part == 1), grid=(steps,),...  12.2 us
    unnamed x44, local copies, waits for them, and re-layouts  10.2 us
    ppermute x6, waiting for transfers between devices, pair_sum(): other = lax.ppermute(x, axis, [(i, i ^ flip) for i in range(size)])  5.16 us
    pallas_call x1, Pallas kernels, dispatch(): pl.pallas_call(dispatch_kernel, grid_spec=pltpu.PrefetchScalarGridSpec(nu...  4.82 us
    ppermute x6, starting transfers between devices, pair_sum(): other = lax.ppermute(x, axis, [(i, i ^ flip) for i in range(size)])  4.59 us
    pallas_call x1, Pallas kernels, down_early(): pl.pallas_call(down_early_kernel, in_specs=[scalars()] + [whole()] * (NY...  3.89 us
  transfers between devices with their start and end apart: 29, of which 8 were waited for; matrix products, arithmetic and copies ran while one was open for 2% of the time, Pallas kernels for 27%

profile of v4, /device:TPU:6, one launch (start us, length us, event | category | flops | bytes accessed | tf_op | source)
XLA Modules:
  0.0 115.9 jit_solution(4128173511386305263)
XLA Ops:
  1.9 2.0 %collective-permute-start.3 = (bf16[1152,128]{1,0:T(8,128)(2,1)S(1)}, bf16[1152,128]{1,0:T(8,128)(2,1)S(1)}, u32[]{:S(2)}, u32[]{:S(2)}) collective-permute-start(bf16[1152,128]{1,0:T(8,128)(2,1)S(1)} %get-tuple-element.39.refs_4_), channel_id=1, source_target_pairs={{0,1},{1,2},{2,3},{3,4},{4,5},{5,6},{6,7},{7,0},{8,9},{9,10},{10,1... | collective-permute-start | bytes 884744 | tf_op jit(solution)/shard_map/ppermute | solution.py:464
  4.5 4.8 %dispatch.1 = (bf16[9,32,1024]{2,1,0:T(8,128)(2,1)}, bf16[9,32,1024]{2,1,0:T(8,128)(2,1)}, bf16[9,32,1024]{2,1,0:T(8,128)(2,1)}, bf16[9,32,1024]{2,1,0:T(8,128)(2,1)}, f32[1,448]{1,0:T(1,128)}, /*index=5*/s32[1]{0:T(128)}) custom-call(s32[3]{0:T(128)} %pad_add_fusion.place_ref, bf16[448,8192]{1,0:T(8,128)(2,1)} %hidden_ref.5, bf16[64,128]{1,0:T(8,128)(2,1)} %bitcast.11, ...), custom_call_target="tpu_custom_call" | custom-call | flops 1056964608 | bytes 4000000 | tf_op jit(solution)/shard_map/dispatch/pallas_call | solution.py:123
  11.0 2.9 %collective-permute-start.1 = (bf16[9,32,1024]{2,1,0:T(8,128)(2,1)}, bf16[9,32,1024]{2,1,0:T(8,128)(2,1)S(1)}, u32[]{:S(2)}, u32[]{:S(2)}) collective-permute-start(bf16[9,32,1024]{2,1,0:T(8,128)(2,1)} %get-tuple-element.37), channel_id=1, source_target_pairs={{0,16},{8,24},{16,0},{24,8},{1,17},{9,25},{17,1},{25,9},{2,18},{10... | collective-permute-start | bytes 1769480 | tf_op jit(solution)/shard_map/ppermute | solution.py:464
  13.9 4.0 %collective-permute-start.6 = (bf16[1152,128]{1,0:T(8,128)(2,1)S(1)}, bf16[1152,128]{1,0:T(8,128)(2,1)S(1)}, u32[]{:S(2)}, u32[]{:S(2)}) collective-permute-start(bf16[1152,128]{1,0:T(8,128)(2,1)S(1)} %get-tuple-element.40.refs_5_), channel_id=1, source_target_pairs={{0,7},{1,0},{2,1},{3,2},{4,3},{5,4},{6,5},{7,6},{8,15},{9,8},{10,9... | collective-permute-start | bytes 884744 | tf_op jit(solution)/shard_map/ppermute | solution.py:464
  17.9 3.2 %collective-permute-start.5 = (bf16[1152,128]{1,0:T(8,128)(2,1)S(1)}, bf16[1152,128]{1,0:T(8,128)(2,1)S(1)}, u32[]{:S(2)}, u32[]{:S(2)}) collective-permute-start(bf16[1152,128]{1,0:T(8,128)(2,1)S(1)} %get-tuple-element.39.refs_4_), channel_id=1, source_target_pairs={{0,7},{1,0},{2,1},{3,2},{4,3},{5,4},{6,5},{7,6},{8,15},{9,8},{10,9... | collective-permute-start | bytes 884744 | tf_op jit(solution)/shard_map/ppermute | solution.py:464
  21.1 4.2 %collective-permute-done.6.refs_9_ = bf16[1152,128]{1,0:T(8,128)(2,1)S(1)} collective-permute-done((bf16[1152,128]{1,0:T(8,128)(2,1)S(1)}, bf16[1152,128]{1,0:T(8,128)(2,1)S(1)}, u32[]{:S(2)}, u32[]{:S(2)}) %collective-permute-start.6) | collective-permute-done | bytes 294944 | tf_op jit(solution)/shard_map/ppermute | solution.py:464
  29.0 2.5 %collective-permute-done.5.refs_8_ = bf16[1152,128]{1,0:T(8,128)(2,1)S(1)} collective-permute-done((bf16[1152,128]{1,0:T(8,128)(2,1)S(1)}, bf16[1152,128]{1,0:T(8,128)(2,1)S(1)}, u32[]{:S(2)}, u32[]{:S(2)}) %collective-permute-start.5) | collective-permute-done | bytes 294944 | tf_op jit(solution)/shard_map/ppermute | solution.py:464
  33.1 6.4 %collective-permute-done.1.refs_2_ = bf16[9,32,1024]{2,1,0:T(8,128)(2,1)S(1)} collective-permute-done((bf16[9,32,1024]{2,1,0:T(8,128)(2,1)}, bf16[9,32,1024]{2,1,0:T(8,128)(2,1)S(1)}, u32[]{:S(2)}, u32[]{:S(2)}) %collective-permute-start.1) | collective-permute-done | bytes 589856 | tf_op jit(solution)/shard_map/ppermute | solution.py:464
  39.5 4.2 %collective-permute-start.9 = (bf16[1152,128]{1,0:T(8,128)(2,1)S(1)}, bf16[1152,128]{1,0:T(8,128)(2,1)}, u32[]{:S(2)}, u32[]{:S(2)}) collective-permute-start(bf16[1152,128]{1,0:T(8,128)(2,1)S(1)} %collective-permute-done.5.refs_8_), channel_id=1, source_target_pairs={{0,7},{1,0},{2,1},{3,2},{4,3},{5,4},{6,5},{7,6},{8,15},{9,8},{10,9... | collective-permute-start | bytes 884744 | tf_op jit(solution)/shard_map/ppermute | solution.py:464
  43.8 3.2 %collective-permute-start.20 = (bf16[1152,128]{1,0:T(8,128)(2,1)S(1)}, bf16[1152,128]{1,0:T(8,128)(2,1)}, u32[]{:S(2)}, u32[]{:S(2)}) collective-permute-start(bf16[1152,128]{1,0:T(8,128)(2,1)S(1)} %collective-permute-done.10.refs_13_), channel_id=1, source_target_pairs={{0,7},{1,0},{2,1},{3,2},{4,3},{5,4},{6,5},{7,6},{8,15},{9,8},{10,9... | collective-permute-start | bytes 884744 | tf_op jit(solution)/shard_map/ppermute | solution.py:464
  47.0 4.1 %collective-permute-done.9.refs_12_ = bf16[1152,128]{1,0:T(8,128)(2,1)} collective-permute-done((bf16[1152,128]{1,0:T(8,128)(2,1)S(1)}, bf16[1152,128]{1,0:T(8,128)(2,1)}, u32[]{:S(2)}, u32[]{:S(2)}) %collective-permute-start.9) | collective-permute-done | bytes 294944 | tf_op jit(solution)/shard_map/ppermute | solution.py:464
  51.1 3.8 %collective-permute-start.19 = (bf16[1152,128]{1,0:T(8,128)(2,1)}, bf16[1152,128]{1,0:T(8,128)(2,1)}, u32[]{:S(2)}, u32[]{:S(2)}) collective-permute-start(bf16[1152,128]{1,0:T(8,128)(2,1)} %collective-permute-done.9.refs_12_), channel_id=1, source_target_pairs={{0,7},{1,0},{2,1},{3,2},{4,3},{5,4},{6,5},{7,6},{8,15},{9,8},{10,9... | collective-permute-start | bytes 884744 | tf_op jit(solution)/shard_map/ppermute | solution.py:464
  54.9 2.5 %collective-permute-done.20.refs_7_.refs_17_ = bf16[1152,128]{1,0:T(8,128)(2,1)} collective-permute-done((bf16[1152,128]{1,0:T(8,128)(2,1)S(1)}, bf16[1152,128]{1,0:T(8,128)(2,1)}, u32[]{:S(2)}, u32[]{:S(2)}) %collective-permute-start.20) | collective-permute-done | bytes 294944 | tf_op jit(solution)/shard_map/ppermute | solution.py:464
  57.5 3.8 %collective-permute-start.22 = (bf16[1152,128]{1,0:T(8,128)(2,1)}, bf16[1152,128]{1,0:T(8,128)(2,1)}, u32[]{:S(2)}, u32[]{:S(2)}) collective-permute-start(bf16[1152,128]{1,0:T(8,128)(2,1)} %collective-permute-done.20.refs_7_.refs_17_), channel_id=1, source_target_pairs={{0,7},{1,0},{2,1},{3,2},{4,3},{5,4},{6,5},{7,6},{8,15},{9,8},{10,9... | collective-permute-start | bytes 884744 | tf_op jit(solution)/shard_map/ppermute | solution.py:464
  62.3 3.9 %down_early.1 = (bf16[5,128,128]{2,1,0:T(8,128)(2,1)}, bf16[128,128]{1,0:T(8,128)(2,1)S(1)}) custom-call(s32[1]{0:T(128)} %get-tuple-element.34.hot_ref, bf16[9,32,1024]{2,1,0:T(8,128)(2,1)S(1)} %copy-done, bf16[9,32,1024]{2,1,0:T(8,128)(2,1)S(1)} %collective-permute-done.refs_1_, bf16[9,32,1024]{2,1,0:T(8,128)(2,1)S(1)} %collective-permute-done.1.refs_2_, ...), custom_call_target="tpu_custom_call" | custom-call | flops 335544320 | bytes 6000000 | tf_op jit(solution)/shard_map/down_early/pallas_call | solution.py:273
  66.9 5.9 %base.2 = (f32[448,256]{1,0:T(8,128)}, f32[448,128]{1,0:T(8,128)}) custom-call(bf16[448,8192]{1,0:T(8,128)(2,1)} %hidden_ref.5, bf16[64,128]{1,0:T(8,128)(2,1)} %bitcast.12, bf16[16384,128]{1,0:T(8,128)(2,1)} %bitcast.9), custom_call_target="tpu_custom_call" | custom-call | flops 939524096 | bytes 6000000 | tf_op jit(solution)/shard_map/base/pallas_call | solution.py:211
  73.6 2.8 %down_late.1 = bf16[4,128,128]{2,1,0:T(8,128)(2,1)S(1)} custom-call(s32[1]{0:T(128)} %get-tuple-element.34.hot_ref, bf16[9,32,1024]{2,1,0:T(8,128)(2,1)S(1)} %copy-done.1, bf16[9,32,1024]{2,1,0:T(8,128)(2,1)S(1)} %collective-permute-done.refs_1_, bf16[9,32,1024]{2,1,0:T(8,128)(2,1)S(1)} %collective-permute-done.1.refs_2_, ...), custom_call_target="tpu_custom_call" | custom-call | flops 268435456 | bytes 2000000 | tf_op jit(solution)/shard_map/down_late/pallas_call | solution.py:306
  82.8 2.4 %up_prepare.1 = (bf16[3,256,256]{2,1,0:T(8,128)(2,1)S(1)}, bf16[4,128,256]{2,1,0:T(8,128)(2,1)S(1)}) custom-call(s32[1]{0:T(128)} %get-tuple-element.34.hot_ref, bf16[9,32,1024]{2,1,0:T(8,128)(2,1)S(1)} %copy-done.1, bf16[9,32,1024]{2,1,0:T(8,128)(2,1)S(1)} %collective-permute-done.refs_1_, bf16[9,32,1024]{2,1,0:T(8,128)(2,1)S(1)} %collective-permute-done.1.refs_2_, ...), custom_call_target="tpu_custom_call" | custom-call | flops 4000000 | bytes 1500000 | tf_op jit(solution)/shard_map/up_prepare/pallas_call | solution.py:384
  87.2 3.3 %collective-permute-done.24 = bf16[4,128,128]{2,1,0:T(8,128)(2,1)S(1)} collective-permute-done((bf16[4,128,128]{2,1,0:T(8,128)(2,1)S(1)}, bf16[4,128,128]{2,1,0:T(8,128)(2,1)S(1)}, u32[]{:S(2)}, u32[]{:S(2)}) %collective-permute-start.24) | collective-permute-done | bytes 131104 | tf_op jit(solution)/shard_map/ppermute | solution.py:468
  91.8 1.8 %collective-permute-done.13 = bf16[5,128,128]{2,1,0:T(8,128)(2,1)S(1)} collective-permute-done((bf16[5,128,128]{2,1,0:T(8,128)(2,1)S(1)}, bf16[5,128,128]{2,1,0:T(8,128)(2,1)S(1)}, u32[]{:S(2)}, u32[]{:S(2)}) %collective-permute-start.13) | collective-permute-done | bytes 163872 | tf_op jit(solution)/shard_map/ppermute | solution.py:468
  93.7 2.2 %up_early.1 = (bf16[5,32,256]{2,1,0:T(8,128)(2,1)S(1)}, bf16[5,32,256]{2,1,0:T(8,128)(2,1)S(1)}, bf16[5,32,256]{2,1,0:T(8,128)(2,1)}, bf16[5,32,256]{2,1,0:T(8,128)(2,1)}) custom-call(bf16[5,128,128]{2,1,0:T(8,128)(2,1)S(1)} %add_convert_fusion.low_ref, bf16[9,32,1024]{2,1,0:T(8,128)(2,1)S(1)} %copy-done.1, ...), custom_call_target="tpu_custom_call" | custom-call | flops 83886080 | bytes 1500000 | tf_op jit(solution)/shard_map/up_early/pallas_call | solution.py:353
  98.1 1.9 %up_late.1 = (bf16[4,32,256]{2,1,0:T(8,128)(2,1)S(1)}, bf16[4,32,256]{2,1,0:T(8,128)(2,1)S(1)}, bf16[4,32,256]{2,1,0:T(8,128)(2,1)S(1)}, bf16[4,32,256]{2,1,0:T(8,128)(2,1)S(1)}) custom-call(s32[1]{0:T(128)} %get-tuple-element.34.hot_ref, bf16[4,128,128]{2,1,0:T(8,128)(2,1)S(1)} %add_convert_fusion.3.low_ref, ...), custom_call_target="tpu_custom_call" | custom-call | flops 67108864 | bytes 1000000 | tf_op jit(solution)/shard_map/up_late/pallas_call | solution.py:415
  100.0 2.8 %collective-permute-start.26 = (bf16[4,32,256]{2,1,0:T(8,128)(2,1)S(1)}, bf16[4,32,256]{2,1,0:T(8,128)(2,1)S(1)}, u32[]{:S(2)}, u32[]{:S(2)}) collective-permute-start(bf16[4,32,256]{2,1,0:T(8,128)(2,1)S(1)} %get-tuple-element.50), channel_id=1, source_target_pairs={{0,24},{8,0},{16,8},{24,16},{1,25},{9,1},{17,9},{25,17},{2,26},{10... | collective-permute-start | bytes 196616 | tf_op jit(solution)/shard_map/ppermute | solution.py:464
  105.7 6.3 %base.3 = (f32[448,256]{1,0:T(8,128)}, f32[448,128]{1,0:T(8,128)}) custom-call(bf16[448,8192]{1,0:T(8,128)(2,1)} %hidden_ref.5, bf16[64,128]{1,0:T(8,128)(2,1)} %bitcast.13, bf16[16384,128]{1,0:T(8,128)(2,1)} %bitcast.10, f32[448,256]{1,0:T(8,128)} %get-tuple-element.29.refs_0_, f32[448,128]{1,0:T(8,128)} %get-tuple-element.30.refs_1_), custom_call_target="tpu_custom_call" | custom-call | flops 939524096 | bytes 6000000 | tf_op jit(solution)/shard_map/base/pallas_call | solution.py:211
  (98 shorter events, 30.6 us)
Async XLA Ops:
  1.9 15.9 %collective-permute-start.3 = (bf16[1152,128]{1,0:T(8,128)(2,1)S(1)}, bf16[1152,128]{1,0:T(8,128)(2,1)S(1)}, u32[]{:S(2)}, u32[]{:S(2)}) collective-permute-start(bf16[1152,128]{1,0:T(8,128)(2,1)S(1)} %get-tuple-element.39.refs_4_), channel_id=1, source_target_pairs={{0,1},{1,2},{2,3},{3,4},{4,5},{5,6},{6,7},{7,0},{8,9},{9,10},{10,1... | collective-permute-start | bytes 884744 | tf_op jit(solution)/shard_map/ppermute | solution.py:464
  9.3 23.6 %collective-permute-start = (bf16[9,32,1024]{2,1,0:T(8,128)(2,1)}, bf16[9,32,1024]{2,1,0:T(8,128)(2,1)S(1)}, u32[]{:S(2)}, u32[]{:S(2)}) collective-permute-start(bf16[9,32,1024]{2,1,0:T(8,128)(2,1)} %get-tuple-element.36), channel_id=1, source_target_pairs={{0,8},{8,16},{16,24},{24,0},{1,9},{9,17},{17,25},{25,1},{2,10},{10... | collective-permute-start | bytes 1769480 | tf_op jit(solution)/shard_map/ppermute | solution.py:464
  11.0 28.5 %collective-permute-start.1 = (bf16[9,32,1024]{2,1,0:T(8,128)(2,1)}, bf16[9,32,1024]{2,1,0:T(8,128)(2,1)S(1)}, u32[]{:S(2)}, u32[]{:S(2)}) collective-permute-start(bf16[9,32,1024]{2,1,0:T(8,128)(2,1)} %get-tuple-element.37), channel_id=1, source_target_pairs={{0,16},{8,24},{16,0},{24,8},{1,17},{9,25},{17,1},{25,9},{2,18},{10... | collective-permute-start | bytes 1769480 | tf_op jit(solution)/shard_map/ppermute | solution.py:464
  13.9 11.4 %collective-permute-start.6 = (bf16[1152,128]{1,0:T(8,128)(2,1)S(1)}, bf16[1152,128]{1,0:T(8,128)(2,1)S(1)}, u32[]{:S(2)}, u32[]{:S(2)}) collective-permute-start(bf16[1152,128]{1,0:T(8,128)(2,1)S(1)} %get-tuple-element.40.refs_5_), channel_id=1, source_target_pairs={{0,7},{1,0},{2,1},{3,2},{4,3},{5,4},{6,5},{7,6},{8,15},{9,8},{10,9... | collective-permute-start | bytes 884744 | tf_op jit(solution)/shard_map/ppermute | solution.py:464
  17.8 9.6 %collective-permute-start.4 = (bf16[1152,128]{1,0:T(8,128)(2,1)S(1)}, bf16[1152,128]{1,0:T(8,128)(2,1)S(1)}, u32[]{:S(2)}, u32[]{:S(2)}) collective-permute-start(bf16[1152,128]{1,0:T(8,128)(2,1)S(1)} %get-tuple-element.40.refs_5_), channel_id=1, source_target_pairs={{0,1},{1,2},{2,3},{3,4},{4,5},{5,6},{6,7},{7,0},{8,9},{9,10},{10,1... | collective-permute-start | bytes 884744 | tf_op jit(solution)/shard_map/ppermute | solution.py:464
  17.9 13.7 %collective-permute-start.5 = (bf16[1152,128]{1,0:T(8,128)(2,1)S(1)}, bf16[1152,128]{1,0:T(8,128)(2,1)S(1)}, u32[]{:S(2)}, u32[]{:S(2)}) collective-permute-start(bf16[1152,128]{1,0:T(8,128)(2,1)S(1)} %get-tuple-element.39.refs_4_), channel_id=1, source_target_pairs={{0,7},{1,0},{2,1},{3,2},{4,3},{5,4},{6,5},{7,6},{8,15},{9,8},{10,9... | collective-permute-start | bytes 884744 | tf_op jit(solution)/shard_map/ppermute | solution.py:464
  25.2 18.5 %collective-permute-start.7 = (bf16[1152,128]{1,0:T(8,128)(2,1)S(1)}, bf16[1152,128]{1,0:T(8,128)(2,1)S(1)}, u32[]{:S(2)}, u32[]{:S(2)}) collective-permute-start(bf16[1152,128]{1,0:T(8,128)(2,1)S(1)} %collective-permute-done.3.refs_6_), channel_id=1, source_target_pairs={{0,1},{1,2},{2,3},{3,4},{4,5},{5,6},{6,7},{7,0},{8,9},{9,10},{10,1... | collective-permute-start | bytes 884744 | tf_op jit(solution)/shard_map/ppermute | solution.py:464
  27.4 16.3 %collective-permute-start.10 = (bf16[1152,128]{1,0:T(8,128)(2,1)S(1)}, bf16[1152,128]{1,0:T(8,128)(2,1)S(1)}, u32[]{:S(2)}, u32[]{:S(2)}) collective-permute-start(bf16[1152,128]{1,0:T(8,128)(2,1)S(1)} %collective-permute-done.6.refs_9_), channel_id=1, source_target_pairs={{0,7},{1,0},{2,1},{3,2},{4,3},{5,4},{6,5},{7,6},{8,15},{9,8},{10,9... | collective-permute-start | bytes 884744 | tf_op jit(solution)/shard_map/ppermute | solution.py:464
  31.6 29.7 %collective-permute-start.2 = (bf16[9,32,1024]{2,1,0:T(8,128)(2,1)}, bf16[9,32,1024]{2,1,0:T(8,128)(2,1)S(1)}, u32[]{:S(2)}, u32[]{:S(2)}) collective-permute-start(bf16[9,32,1024]{2,1,0:T(8,128)(2,1)} %get-tuple-element.38), channel_id=1, source_target_pairs={{0,24},{8,0},{16,8},{24,16},{1,25},{9,1},{17,9},{25,17},{2,26},{10... | collective-permute-start | bytes 1769480 | tf_op jit(solution)/shard_map/ppermute | solution.py:464
  32.9 14.1 %collective-permute-start.8 = (bf16[1152,128]{1,0:T(8,128)(2,1)S(1)}, bf16[1152,128]{1,0:T(8,128)(2,1)}, u32[]{:S(2)}, u32[]{:S(2)}) collective-permute-start(bf16[1152,128]{1,0:T(8,128)(2,1)S(1)} %collective-permute-done.4.refs_7_), channel_id=1, source_target_pairs={{0,1},{1,2},{2,3},{3,4},{4,5},{5,6},{6,7},{7,0},{8,9},{9,10},{10,1... | collective-permute-start | bytes 884744 | tf_op jit(solution)/shard_map/ppermute | solution.py:464
  39.5 11.6 %collective-permute-start.9 = (bf16[1152,128]{1,0:T(8,128)(2,1)S(1)}, bf16[1152,128]{1,0:T(8,128)(2,1)}, u32[]{:S(2)}, u32[]{:S(2)}) collective-permute-start(bf16[1152,128]{1,0:T(8,128)(2,1)S(1)} %collective-permute-done.5.refs_8_), channel_id=1, source_target_pairs={{0,7},{1,0},{2,1},{3,2},{4,3},{5,4},{6,5},{7,6},{8,15},{9,8},{10,9... | collective-permute-start | bytes 884744 | tf_op jit(solution)/shard_map/ppermute | solution.py:464
  43.7 11.2 %collective-permute-start.17 = (bf16[1152,128]{1,0:T(8,128)(2,1)S(1)}, bf16[1152,128]{1,0:T(8,128)(2,1)}, u32[]{:S(2)}, u32[]{:S(2)}) collective-permute-start(bf16[1152,128]{1,0:T(8,128)(2,1)S(1)} %collective-permute-done.7.refs_10_), channel_id=1, source_target_pairs={{0,1},{1,2},{2,3},{3,4},{4,5},{5,6},{6,7},{7,0},{8,9},{9,10},{10,1... | collective-permute-start | bytes 884744 | tf_op jit(solution)/shard_map/ppermute | solution.py:464
  43.8 13.7 %collective-permute-start.20 = (bf16[1152,128]{1,0:T(8,128)(2,1)S(1)}, bf16[1152,128]{1,0:T(8,128)(2,1)}, u32[]{:S(2)}, u32[]{:S(2)}) collective-permute-start(bf16[1152,128]{1,0:T(8,128)(2,1)S(1)} %collective-permute-done.10.refs_13_), channel_id=1, source_target_pairs={{0,7},{1,0},{2,1},{3,2},{4,3},{5,4},{6,5},{7,6},{8,15},{9,8},{10,9... | collective-permute-start | bytes 884744 | tf_op jit(solution)/shard_map/ppermute | solution.py:464
  47.0 25.8 %collective-permute-start.18 = (bf16[1152,128]{1,0:T(8,128)(2,1)}, bf16[1152,128]{1,0:T(8,128)(2,1)}, u32[]{:S(2)}, u32[]{:S(2)}) collective-permute-start(bf16[1152,128]{1,0:T(8,128)(2,1)} %collective-permute-done.8.refs_11_), channel_id=1, source_target_pairs={{0,1},{1,2},{2,3},{3,4},{4,5},{5,6},{6,7},{7,0},{8,9},{9,10},{10,1... | collective-permute-start | bytes 884744 | tf_op jit(solution)/shard_map/ppermute | solution.py:464
  51.1 21.6 %collective-permute-start.19 = (bf16[1152,128]{1,0:T(8,128)(2,1)}, bf16[1152,128]{1,0:T(8,128)(2,1)}, u32[]{:S(2)}, u32[]{:S(2)}) collective-permute-start(bf16[1152,128]{1,0:T(8,128)(2,1)} %collective-permute-done.9.refs_12_), channel_id=1, source_target_pairs={{0,7},{1,0},{2,1},{3,2},{4,3},{5,4},{6,5},{7,6},{8,15},{9,8},{10,9... | collective-permute-start | bytes 884744 | tf_op jit(solution)/shard_map/ppermute | solution.py:464
  54.9 17.8 %collective-permute-start.21 = (bf16[1152,128]{1,0:T(8,128)(2,1)}, bf16[1152,128]{1,0:T(8,128)(2,1)}, u32[]{:S(2)}, u32[]{:S(2)}) collective-permute-start(bf16[1152,128]{1,0:T(8,128)(2,1)} %collective-permute-done.17.refs_4_.refs_14_), channel_id=1, source_target_pairs={{0,1},{1,2},{2,3},{3,4},{4,5},{5,6},{6,7},{7,0},{8,9},{9,10},{10,1... | collective-permute-start | bytes 884744 | tf_op jit(solution)/shard_map/ppermute | solution.py:464
  57.5 15.3 %collective-permute-start.22 = (bf16[1152,128]{1,0:T(8,128)(2,1)}, bf16[1152,128]{1,0:T(8,128)(2,1)}, u32[]{:S(2)}, u32[]{:S(2)}) collective-permute-start(bf16[1152,128]{1,0:T(8,128)(2,1)} %collective-permute-done.20.refs_7_.refs_17_), channel_id=1, source_target_pairs={{0,7},{1,0},{2,1},{3,2},{4,3},{5,4},{6,5},{7,6},{8,15},{9,8},{10,9... | collective-permute-start | bytes 884744 | tf_op jit(solution)/shard_map/ppermute | solution.py:464
  66.8 10.2 %collective-permute-start.11 = (bf16[5,128,128]{2,1,0:T(8,128)(2,1)}, bf16[5,128,128]{2,1,0:T(8,128)(2,1)}, u32[]{:S(2)}, u32[]{:S(2)}) collective-permute-start(bf16[5,128,128]{2,1,0:T(8,128)(2,1)} %get-tuple-element.41), channel_id=1, source_target_pairs={{0,32},{32,0},{1,33},{33,1},{2,34},{34,2},{3,35},{35,3},{4,36},{36... | collective-permute-start | bytes 491528 | tf_op jit(solution)/shard_map/ppermute | solution.py:468
  76.4 8.8 %collective-permute-start.23 = (bf16[4,128,128]{2,1,0:T(8,128)(2,1)S(1)}, bf16[4,128,128]{2,1,0:T(8,128)(2,1)S(1)}, u32[]{:S(2)}, u32[]{:S(2)}) collective-permute-start(bf16[4,128,128]{2,1,0:T(8,128)(2,1)S(1)} %down_late.1), channel_id=1, source_target_pairs={{0,32},{32,0},{1,33},{33,1},{2,34},{34,2},{3,35},{35,3},{4,36},{36... | collective-permute-start | bytes 393224 | tf_op jit(solution)/shard_map/ppermute | solution.py:468
  95.9 16.3 %collective-permute-start.15 = (bf16[5,32,256]{2,1,0:T(8,128)(2,1)}, bf16[5,32,256]{2,1,0:T(8,128)(2,1)S(1)}, u32[]{:S(2)}, u32[]{:S(2)}) collective-permute-start(bf16[5,32,256]{2,1,0:T(8,128)(2,1)} %get-tuple-element.44), channel_id=1, source_target_pairs={{0,16},{8,24},{16,0},{24,8},{1,17},{9,25},{17,1},{25,9},{2,18},{10... | collective-permute-start | bytes 245768 | tf_op jit(solution)/shard_map/ppermute | solution.py:464
  96.7 15.5 %collective-permute-start.16 = (bf16[5,32,256]{2,1,0:T(8,128)(2,1)}, bf16[5,32,256]{2,1,0:T(8,128)(2,1)S(1)}, u32[]{:S(2)}, u32[]{:S(2)}) collective-permute-start(bf16[5,32,256]{2,1,0:T(8,128)(2,1)} %get-tuple-element.45), channel_id=1, source_target_pairs={{0,8},{8,16},{16,24},{24,0},{1,9},{9,17},{17,25},{25,1},{2,10},{10... | collective-permute-start | bytes 245768 | tf_op jit(solution)/shard_map/ppermute | solution.py:464
  100.0 14.6 %collective-permute-start.26 = (bf16[4,32,256]{2,1,0:T(8,128)(2,1)S(1)}, bf16[4,32,256]{2,1,0:T(8,128)(2,1)S(1)}, u32[]{:S(2)}, u32[]{:S(2)}) collective-permute-start(bf16[4,32,256]{2,1,0:T(8,128)(2,1)S(1)} %get-tuple-element.50), channel_id=1, source_target_pairs={{0,24},{8,0},{16,8},{24,16},{1,25},{9,1},{17,9},{25,17},{2,26},{10... | collective-permute-start | bytes 196616 | tf_op jit(solution)/shard_map/ppermute | solution.py:464
  102.8 11.8 %collective-permute-start.27 = (bf16[4,32,256]{2,1,0:T(8,128)(2,1)S(1)}, bf16[4,32,256]{2,1,0:T(8,128)(2,1)S(1)}, u32[]{:S(2)}, u32[]{:S(2)}) collective-permute-start(bf16[4,32,256]{2,1,0:T(8,128)(2,1)S(1)} %get-tuple-element.51), channel_id=1, source_target_pairs={{0,16},{8,24},{16,0},{24,8},{1,17},{9,25},{17,1},{25,9},{2,18},{10... | collective-permute-start | bytes 196616 | tf_op jit(solution)/shard_map/ppermute | solution.py:464
  104.4 10.3 %collective-permute-start.28 = (bf16[4,32,256]{2,1,0:T(8,128)(2,1)S(1)}, bf16[4,32,256]{2,1,0:T(8,128)(2,1)S(1)}, u32[]{:S(2)}, u32[]{:S(2)}) collective-permute-start(bf16[4,32,256]{2,1,0:T(8,128)(2,1)S(1)} %get-tuple-element.52), channel_id=1, source_target_pairs={{0,8},{8,16},{16,24},{24,0},{1,9},{9,17},{17,25},{25,1},{2,10},{10... | collective-permute-start | bytes 196616 | tf_op jit(solution)/shard_map/ppermute | solution.py:464
  (27 other events, 273.0 us)

commit v5 on v4

--- a/solution.py
+++ b/solution.py
@@ -27,7 +27,9 @@
 ORDER = (0, 7, 1, 6, 2, 5, 3, 4)
 RANK2 = 128
 CHUNK = COLS + RANK2
-VMEM_LIMIT = 24 * 1024 * 1024
+VMEM_LIMIT = 20 * 1024 * 1024
+WIDE_LIMIT = 58 * 1024 * 1024
+PACK_LIMIT = 66_200_000
 
 
 def iota(shape, axis):
@@ -51,25 +53,33 @@
     return pl.BlockSpec(memory_space=pltpu.SMEM)
 
 
-def pack_kernel(down_ref, up_ref, zero_ref, one_ref):
+def in_hbm():
+    return pl.BlockSpec(memory_space=pltpu.HBM)
+
+
+def pack_kernel(down_ref, up_ref, zero_ref, one_ref, sems):
+    copies = []
     for a, out_ref in enumerate((zero_ref, one_ref)):
-        out_ref[:COLS] = down_ref[a]
-        out_ref[COLS:] = up_ref[a]
+        for src, dst in (
+            (down_ref.at[a], out_ref.at[pl.ds(0, COLS)]),
+            (up_ref.at[a], out_ref.at[pl.ds(COLS, RANK2)]),
+        ):
+            copies.append(pltpu.make_async_copy(src, dst, sems.at[len(copies)]))
+    for copy in copies:
+        copy.start()
+    for copy in copies:
+        copy.wait()
 
 
 def pack(down_weight, up_planes):
     return pl.pallas_call(
         pack_kernel,
-        grid=(1,),
-        in_specs=[
-            pl.BlockSpec((2, COLS, 128), lambda i: (0, 0, 0)),
-            pl.BlockSpec((2, RANK2, 128), lambda i: (0, 0, 0)),
-        ],
-        out_specs=[pl.BlockSpec((CHUNK, 128), lambda i: (0, 0))] * 2,
+        in_specs=[in_hbm()] * 2,
+        out_specs=[whole()] * 2,
         out_shape=[jax.ShapeDtypeStruct((CHUNK, 128), BF16)] * 2,
-        compiler_params=params(),
+        scratch_shapes=[pltpu.SemaphoreType.DMA((4,))],
+        compiler_params=pltpu.CompilerParams(vmem_limit_bytes=PACK_LIMIT),
         cost_estimate=pl.CostEstimate(flops=0, bytes_accessed=1_200_000, transcendentals=0),
-        name="pack",
     )(down_weight, up_planes)
 
 
@@ -136,10 +146,10 @@
         ),
         out_shape=[message] * NY
         + [jax.ShapeDtypeStruct((1, TOK), F32), jax.ShapeDtypeStruct((1,), jnp.int32)],
+        compiler_params=pltpu.CompilerParams(vmem_limit_bytes=WIDE_LIMIT),
         cost_estimate=pl.CostEstimate(
             flops=2 * NY * SLOTS * TOK * COLS, bytes_accessed=4_000_000, transcendentals=0
         ),
-        name="dispatch",
     )(place, hidden, gain, pair, table)
     return out[:NY], out[NY], out[NY + 1]
 
@@ -156,27 +166,26 @@
         out_shape=jax.ShapeDtypeStruct((TOK, 128), F32),
         compiler_params=params(),
         cost_estimate=pl.CostEstimate(flops=1_000_000, bytes_accessed=300_000, transcendentals=0),
-        name="columns",
     )(row)
 
 
-def base_kernel(last, hidden_ref, gain_ref, mixed_ref, *refs):
+def base_kernel(part, hidden_ref, gain_ref, mixed_ref, *refs):
     out_ref, square_ref, scaled_ref, weight_ref = refs[-4:]
+    rows, tile = 64, hidden_ref.shape[1]
     step = pl.program_id(0)
-    gain = gain_row(gain_ref[...]).astype(BF16)
-    rows = 64
 
     @pl.when(step == 0)
     def _():
-        out_ref[...] = refs[0][...] if last else jnp.zeros_like(out_ref)
-        square_ref[...] = refs[1][...] if last else jnp.zeros_like(square_ref)
-
+        out_ref[...] = refs[0][...] if part else jnp.zeros_like(out_ref)
+        square_ref[...] = refs[1][...] if part else jnp.zeros_like(square_ref)
+
+    gain = gain_row(gain_ref[...]).astype(BF16)
     for r in range(0, TOK, rows):
         square = square_ref[r : r + rows, :]
-        for c in range(0, hidden_ref.shape[1], 128):
-            part = hidden_ref[r : r + rows, c : c + 128]
-            scaled_ref[r : r + rows, c : c + 128] = part * gain[:, c : c + 128]
-            wide = part.astype(F32)
+        for c in range(0, tile, 128):
+            block = hidden_ref[r : r + rows, c : c + 128]
+            scaled_ref[r : r + rows, c : c + 128] = block * gain[:, c : c + 128]
+            wide = block.astype(F32)
             square = square + wide * wide
         square_ref[r : r + rows, :] = square
     row = lax.broadcasted_iota(jnp.int32, (256, 256), 0)
@@ -184,8 +193,12 @@
     part_rows = jnp.where(
         lax.broadcasted_iota(jnp.int32, (256, 256), 1) == source, 1.0, 0.0
     ).astype(BF16)
-    for b in range(0, mixed_ref.shape[0], 512):
-        pair = jnp.concatenate([mixed_ref[b : b + 256], mixed_ref[b + 256 : b + 512]], axis=1)
+    first = (part * pl.num_programs(0) + step) * (2 * tile)
+    for b in range(0, 2 * tile, 512):
+        at = pl.multiple_of(first + b, 512)
+        pair = jnp.concatenate(
+            [mixed_ref[pl.ds(at, 256), :], mixed_ref[pl.ds(at + 256, 256), :]], axis=1
+        )
         parted = jnp.dot(part_rows, pair, preferred_element_type=F32).astype(BF16)
         d = b // 2
         weight_ref[d : d + 128, :128] = parted[:128, :128]
@@ -194,7 +207,7 @@
         weight_ref[d + 128 : d + 256, 128:] = parted[128:, 128:]
     out_ref[...] += jnp.dot(scaled_ref[...], weight_ref[...], preferred_element_type=F32)
 
-    if last:
+    if part:
 
         @pl.when(step == pl.num_programs(0) - 1)
         def _():
@@ -209,30 +222,24 @@
     steps = DIM // tile // 2
     first = part * steps
     return pl.pallas_call(
-        functools.partial(base_kernel, part == 1),
+        functools.partial(base_kernel, part),
         grid=(steps,),
         in_specs=[
             pl.BlockSpec((TOK, tile), lambda k: (0, first + k)),
             pl.BlockSpec((8, 128), lambda k: (first + k, 0)),
-            pl.BlockSpec((2 * tile, 128), lambda k: (first + k, 0)),
+            whole(),
         ]
-        + [
-            pl.BlockSpec((TOK, 256), lambda k: (0, 0)),
-            pl.BlockSpec((TOK, 128), lambda k: (0, 0)),
-        ][: len(begun)],
-        out_specs=[
-            pl.BlockSpec((TOK, 256), lambda k: (0, 0)),
-            pl.BlockSpec((TOK, 128), lambda k: (0, 0)),
-        ],
+        + [whole()] * len(begun),
+        out_specs=[whole()] * 2,
         out_shape=[
             jax.ShapeDtypeStruct((TOK, 256), F32),
             jax.ShapeDtypeStruct((TOK, 128), F32),
         ],
         scratch_shapes=[pltpu.VMEM((TOK, tile), BF16), pltpu.VMEM((tile, 256), BF16)],
+        compiler_params=pltpu.CompilerParams(vmem_limit_bytes=WIDE_LIMIT),
         cost_estimate=pl.CostEstimate(
             flops=TOK * DIM * 256, bytes_accessed=6_000_000, transcendentals=0
         ),
-        name="base",
     )(hidden, gain, weight, *begun)
 
 
@@ -282,7 +289,6 @@
         cost_estimate=pl.CostEstimate(
             flops=2 * EARLY * 128 * 1024 * 256, bytes_accessed=6_000_000, transcendentals=0
         ),
-        name="down_early",
     )(hot, *received, *chunks)
 
 
@@ -312,7 +318,6 @@
         cost_estimate=pl.CostEstimate(
             flops=2 * 512 * 1024 * 256, bytes_accessed=2_000_000, transcendentals=0
         ),
-        name="down_late",
     )(hot, *received, *chunks, more)
 
 
@@ -359,7 +364,6 @@
         cost_estimate=pl.CostEstimate(
             flops=2 * EARLY * 128 * 256 * 256, bytes_accessed=1_500_000, transcendentals=0
         ),
-        name="up_early",
     )(low, *received, *chunks)
 
 
@@ -393,7 +397,6 @@
         cost_estimate=pl.CostEstimate(
             flops=4_000_000, bytes_accessed=1_500_000, transcendentals=0
         ),
-        name="up_prepare",
     )(hot, *received, *chunks)
 
 
@@ -421,7 +424,6 @@
         cost_estimate=pl.CostEstimate(
             flops=2 * 512 * 256 * 256, bytes_accessed=1_000_000, transcendentals=0
         ),
-        name="up_late",
     )(hot, low, matrix, mask, *last)
 
 

time: 117 us -> 115 us (0.983)
  local copies, waits for them, and re-layouts: 11 us -> 5.13 us
  waiting for transfers between devices: 26.7 us -> 31 us
    unnamed x44 -> x18, local copies, waits for them, and re-layouts: 10.2 us -> 4.38 us
    ppermute x6, waiting for transfers between devices: 5.16 us -> 9.26 us  [pair_sum(): other = lax.ppermute(x, axis, [(i, i ^ flip) for i in range(size)])]
    pallas_call x3, Pallas kernels: 12.2 us -> 16 us  [the longest x2 14.1 us: base_projection(): pl.pallas_call(functools.partial(base_kernel, part), grid=(steps,), in_sp...]
    pallas_call x1, Pallas kernels: 2.18 us -> 0.46 us  [up_early(): pl.pallas_call(up_early_kernel, in_specs=[whole()] * (1 + NY + len(chunks...]
  transfers between devices with their start and end apart: 29 -> 29, of which waited for: 8 -> 9; matrix products, arithmetic and copies ran while one was open for 2% -> 2% of each run, Pallas kernels for 27% -> 26%
where the time goes in v5:
time: 115 us; the launch traced here: 114 us
  starting transfers between devices  44.5 us (39%)
  Pallas kernels  31.6 us (27%)
  waiting for transfers between devices  31 us (27%)
  local copies, waits for them, and re-layouts  5.13 us (4%)
  other arithmetic  1.9 us (2%)
    ppermute x23, starting transfers between devices, shift(): return lax.ppermute(x, axis, [(i, (i + by) % size) for i in range(size)])  40 us
    ppermute x23, waiting for transfers between devices, shift(): return lax.ppermute(x, axis, [(i, (i + by) % size) for i in range(size)])  21.7 us
    pallas_call x2, Pallas kernels, base_projection(): pl.pallas_call(functools.partial(base_kernel, part), grid=(steps,), in_sp...  14.1 us
    ppermute x6, waiting for transfers between devices, pair_sum(): other = lax.ppermute(x, axis, [(i, i ^ flip) for i in range(size)])  9.26 us
    pallas_call x1, Pallas kernels, dispatch(): pl.pallas_call(dispatch_kernel, grid_spec=pltpu.PrefetchScalarGridSpec(nu...  4.84 us
    ppermute x6, starting transfers between devices, pair_sum(): other = lax.ppermute(x, axis, [(i, i ^ flip) for i in range(size)])  4.46 us
    unnamed x18, local copies, waits for them, and re-layouts  4.38 us
    pallas_call x1, Pallas kernels, down_early(): pl.pallas_call(down_early_kernel, in_specs=[scalars()] + [whole()] * (NY...  2.88 us
  transfers between devices with their start and end apart: 29, of which 9 were waited for; matrix products, arithmetic and copies ran while one was open for 2% of the time, Pallas kernels for 26%

profile of v5, /device:TPU:6, one launch (start us, length us, event | category | flops | bytes accessed | tf_op | source)
XLA Modules:
  0.0 114.3 jit_solution(3063000619368790574)
XLA Ops:
  0.0 1.9 %shard_map.77 = (bf16[1152,128]{1,0:T(8,128)(2,1)}, bf16[1152,128]{1,0:T(8,128)(2,1)}) custom-call(bf16[2,1024,128]{2,1,0:T(8,128)(2,1)} %down_ref.1, bf16[2,128,128]{2,1,0:T(8,128)(2,1)} %bitcast.13), custom_call_target="tpu_custom_call" | custom-call | bytes 1200000 | tf_op jit(solution)/shard_map/pallas_call | solution.py:75
  1.9 2.0 %collective-permute-start.3 = (bf16[1152,128]{1,0:T(8,128)(2,1)}, bf16[1152,128]{1,0:T(8,128)(2,1)S(1)}, u32[]{:S(2)}, u32[]{:S(2)}) collective-permute-start(bf16[1152,128]{1,0:T(8,128)(2,1)} %get-tuple-element.39.refs_4_), channel_id=1, source_target_pairs={{0,1},{1,2},{2,3},{3,4},{4,5},{5,6},{6,7},{7,0},{8,9},{9,10},{10,1... | collective-permute-start | bytes 884744 | tf_op jit(solution)/shard_map/ppermute | solution.py:466
  4.6 4.8 %shard_map.75 = (bf16[9,32,1024]{2,1,0:T(8,128)(2,1)}, bf16[9,32,1024]{2,1,0:T(8,128)(2,1)}, bf16[9,32,1024]{2,1,0:T(8,128)(2,1)}, bf16[9,32,1024]{2,1,0:T(8,128)(2,1)}, f32[1,448]{1,0:T(1,128)}, /*index=5*/s32[1]{0:T(128)}) custom-call(s32[3]{0:T(128)} %pad_add_fusion.place_ref, bf16[448,8192]{1,0:T(8,128)(2,1)} %hidden_ref.5, bf16[64,128]{1,0:T(8,128)(2,1)} %bitcast.10, ...), custom_call_target="tpu_custom_call" | custom-call | flops 1056964608 | bytes 4000000 | tf_op jit(solution)/shard_map/pallas_call | solution.py:133
  11.1 2.9 %collective-permute-start.1 = (bf16[9,32,1024]{2,1,0:T(8,128)(2,1)}, bf16[9,32,1024]{2,1,0:T(8,128)(2,1)S(1)}, u32[]{:S(2)}, u32[]{:S(2)}) collective-permute-start(bf16[9,32,1024]{2,1,0:T(8,128)(2,1)} %get-tuple-element.37), channel_id=1, source_target_pairs={{0,16},{8,24},{16,0},{24,8},{1,17},{9,25},{17,1},{25,9},{2,18},{10... | collective-permute-start | bytes 1769480 | tf_op jit(solution)/shard_map/ppermute | solution.py:466
  14.0 4.0 %collective-permute-start.6 = (bf16[1152,128]{1,0:T(8,128)(2,1)S(1)}, bf16[1152,128]{1,0:T(8,128)(2,1)S(1)}, u32[]{:S(2)}, u32[]{:S(2)}) collective-permute-start(bf16[1152,128]{1,0:T(8,128)(2,1)S(1)} %copy-done.3), channel_id=1, source_target_pairs={{0,7},{1,0},{2,1},{3,2},{4,3},{5,4},{6,5},{7,6},{8,15},{9,8},{10,9... | collective-permute-start | bytes 884744 | tf_op jit(solution)/shard_map/ppermute | solution.py:466
  17.9 3.2 %collective-permute-start.5 = (bf16[1152,128]{1,0:T(8,128)(2,1)S(1)}, bf16[1152,128]{1,0:T(8,128)(2,1)S(1)}, u32[]{:S(2)}, u32[]{:S(2)}) collective-permute-start(bf16[1152,128]{1,0:T(8,128)(2,1)S(1)} %copy-done.2), channel_id=1, source_target_pairs={{0,7},{1,0},{2,1},{3,2},{4,3},{5,4},{6,5},{7,6},{8,15},{9,8},{10,9... | collective-permute-start | bytes 884744 | tf_op jit(solution)/shard_map/ppermute | solution.py:466
  21.2 4.2 %collective-permute-done.6.refs_9_ = bf16[1152,128]{1,0:T(8,128)(2,1)S(1)} collective-permute-done((bf16[1152,128]{1,0:T(8,128)(2,1)S(1)}, bf16[1152,128]{1,0:T(8,128)(2,1)S(1)}, u32[]{:S(2)}, u32[]{:S(2)}) %collective-permute-start.6) | collective-permute-done | bytes 294944 | tf_op jit(solution)/shard_map/ppermute | solution.py:466
  29.0 2.6 %collective-permute-done.5.refs_8_ = bf16[1152,128]{1,0:T(8,128)(2,1)S(1)} collective-permute-done((bf16[1152,128]{1,0:T(8,128)(2,1)S(1)}, bf16[1152,128]{1,0:T(8,128)(2,1)S(1)}, u32[]{:S(2)}, u32[]{:S(2)}) %collective-permute-start.5) | collective-permute-done | bytes 294944 | tf_op jit(solution)/shard_map/ppermute | solution.py:466
  33.2 6.4 %collective-permute-done.1.refs_2_ = bf16[9,32,1024]{2,1,0:T(8,128)(2,1)S(1)} collective-permute-done((bf16[9,32,1024]{2,1,0:T(8,128)(2,1)}, bf16[9,32,1024]{2,1,0:T(8,128)(2,1)S(1)}, u32[]{:S(2)}, u32[]{:S(2)}) %collective-permute-start.1) | collective-permute-done | bytes 589856 | tf_op jit(solution)/shard_map/ppermute | solution.py:466
  39.6 4.2 %collective-permute-start.9 = (bf16[1152,128]{1,0:T(8,128)(2,1)S(1)}, bf16[1152,128]{1,0:T(8,128)(2,1)S(1)}, u32[]{:S(2)}, u32[]{:S(2)}) collective-permute-start(bf16[1152,128]{1,0:T(8,128)(2,1)S(1)} %collective-permute-done.5.refs_8_), channel_id=1, source_target_pairs={{0,7},{1,0},{2,1},{3,2},{4,3},{5,4},{6,5},{7,6},{8,15},{9,8},{10,9... | collective-permute-start | bytes 884744 | tf_op jit(solution)/shard_map/ppermute | solution.py:466
  43.8 3.2 %collective-permute-start.20 = (bf16[1152,128]{1,0:T(8,128)(2,1)S(1)}, bf16[1152,128]{1,0:T(8,128)(2,1)S(1)}, u32[]{:S(2)}, u32[]{:S(2)}) collective-permute-start(bf16[1152,128]{1,0:T(8,128)(2,1)S(1)} %collective-permute-done.10.refs_13_), channel_id=1, source_target_pairs={{0,7},{1,0},{2,1},{3,2},{4,3},{5,4},{6,5},{7,6},{8,15},{9,8},{10,9... | collective-permute-start | bytes 884744 | tf_op jit(solution)/shard_map/ppermute | solution.py:466
  47.1 4.1 %collective-permute-done.9.refs_12_ = bf16[1152,128]{1,0:T(8,128)(2,1)S(1)} collective-permute-done((bf16[1152,128]{1,0:T(8,128)(2,1)S(1)}, bf16[1152,128]{1,0:T(8,128)(2,1)S(1)}, u32[]{:S(2)}, u32[]{:S(2)}) %collective-permute-start.9) | collective-permute-done | bytes 294944 | tf_op jit(solution)/shard_map/ppermute | solution.py:466
  51.2 3.7 %collective-permute-start.19 = (bf16[1152,128]{1,0:T(8,128)(2,1)S(1)}, bf16[1152,128]{1,0:T(8,128)(2,1)}, u32[]{:S(2)}, u32[]{:S(2)}) collective-permute-start(bf16[1152,128]{1,0:T(8,128)(2,1)S(1)} %collective-permute-done.9.refs_12_), channel_id=1, source_target_pairs={{0,7},{1,0},{2,1},{3,2},{4,3},{5,4},{6,5},{7,6},{8,15},{9,8},{10,9... | collective-permute-start | bytes 884744 | tf_op jit(solution)/shard_map/ppermute | solution.py:466
  54.9 2.6 %collective-permute-done.20.refs_7_.refs_17_ = bf16[1152,128]{1,0:T(8,128)(2,1)S(1)} collective-permute-done((bf16[1152,128]{1,0:T(8,128)(2,1)S(1)}, bf16[1152,128]{1,0:T(8,128)(2,1)S(1)}, u32[]{:S(2)}, u32[]{:S(2)}) %collective-permute-start.20) | collective-permute-done | bytes 294944 | tf_op jit(solution)/shard_map/ppermute | solution.py:466
  57.5 3.7 %collective-permute-start.22 = (bf16[1152,128]{1,0:T(8,128)(2,1)S(1)}, bf16[1152,128]{1,0:T(8,128)(2,1)}, u32[]{:S(2)}, u32[]{:S(2)}) collective-permute-start(bf16[1152,128]{1,0:T(8,128)(2,1)S(1)} %collective-permute-done.20.refs_7_.refs_17_), channel_id=1, source_target_pairs={{0,7},{1,0},{2,1},{3,2},{4,3},{5,4},{6,5},{7,6},{8,15},{9,8},{10,9... | collective-permute-start | bytes 884744 | tf_op jit(solution)/shard_map/ppermute | solution.py:466
  62.3 2.9 %shard_map.78 = (bf16[5,128,128]{2,1,0:T(8,128)(2,1)}, bf16[128,128]{1,0:T(8,128)(2,1)S(1)}) custom-call(s32[1]{0:T(128)} %get-tuple-element.34.hot_ref, bf16[9,32,1024]{2,1,0:T(8,128)(2,1)S(1)} %copy-done, bf16[9,32,1024]{2,1,0:T(8,128)(2,1)S(1)} %collective-permute-done.refs_1_, bf16[9,32,1024]{2,1,0:T(8,128)(2,1)S(1)} %collective-permute-done.1.refs_2_, ...), custom_call_target="tpu_custom_call" | custom-call | flops 335544320 | bytes 6000000 | tf_op jit(solution)/shard_map/pallas_call | solution.py:280
  65.8 6.8 %shard_map.73 = (f32[448,256]{1,0:T(8,128)}, f32[448,128]{1,0:T(8,128)}) custom-call(bf16[448,8192]{1,0:T(8,128)(2,1)} %hidden_ref.5, bf16[64,128]{1,0:T(8,128)(2,1)} %bitcast.11, bf16[16384,128]{1,0:T(8,128)(2,1)} %bitcast.8), custom_call_target="tpu_custom_call" | custom-call | flops 939524096 | bytes 6000000 | tf_op jit(solution)/shard_map/pallas_call | solution.py:224
  73.4 2.5 %shard_map.81 = bf16[4,128,128]{2,1,0:T(8,128)(2,1)S(1)} custom-call(s32[1]{0:T(128)} %get-tuple-element.34.hot_ref, bf16[9,32,1024]{2,1,0:T(8,128)(2,1)S(1)} %copy-done.1, bf16[9,32,1024]{2,1,0:T(8,128)(2,1)S(1)} %collective-permute-done.refs_1_, bf16[9,32,1024]{2,1,0:T(8,128)(2,1)S(1)} %collective-permute-done.1.refs_2_, ...), custom_call_target="tpu_custom_call" | custom-call | flops 268435456 | bytes 2000000 | tf_op jit(solution)/shard_map/pallas_call | solution.py:312
  78.5 1.9 %shard_map.82 = (bf16[3,256,256]{2,1,0:T(8,128)(2,1)S(1)}, bf16[4,128,256]{2,1,0:T(8,128)(2,1)S(1)}) custom-call(s32[1]{0:T(128)} %get-tuple-element.34.hot_ref, bf16[9,32,1024]{2,1,0:T(8,128)(2,1)S(1)} %copy-done.1, bf16[9,32,1024]{2,1,0:T(8,128)(2,1)S(1)} %collective-permute-done.refs_1_, bf16[9,32,1024]{2,1,0:T(8,128)(2,1)S(1)} %collective-permute-done.1.refs_2_, ...), custom_call_target="tpu_custom_call" | custom-call | flops 4000000 | bytes 1500000 | tf_op jit(solution)/shard_map/pallas_call | solution.py:388
  81.8 2.9 %collective-permute-done.12 = bf16[5,128,128]{2,1,0:T(8,128)(2,1)S(1)} collective-permute-done((bf16[5,128,128]{2,1,0:T(8,128)(2,1)S(1)}, bf16[5,128,128]{2,1,0:T(8,128)(2,1)S(1)}, u32[]{:S(2)}, u32[]{:S(2)}) %collective-permute-start.12) | collective-permute-done | bytes 163872 | tf_op jit(solution)/shard_map/ppermute | solution.py:470
  88.2 4.6 %collective-permute-done.13 = bf16[5,128,128]{2,1,0:T(8,128)(2,1)S(1)} collective-permute-done((bf16[5,128,128]{2,1,0:T(8,128)(2,1)S(1)}, bf16[5,128,128]{2,1,0:T(8,128)(2,1)S(1)}, u32[]{:S(2)}, u32[]{:S(2)}) %collective-permute-start.13) | collective-permute-done | bytes 163872 | tf_op jit(solution)/shard_map/ppermute | solution.py:470
  95.6 1.9 %shard_map.83 = (bf16[4,32,256]{2,1,0:T(8,128)(2,1)S(1)}, bf16[4,32,256]{2,1,0:T(8,128)(2,1)S(1)}, bf16[4,32,256]{2,1,0:T(8,128)(2,1)S(1)}, bf16[4,32,256]{2,1,0:T(8,128)(2,1)S(1)}) custom-call(s32[1]{0:T(128)} %get-tuple-element.34.hot_ref, bf16[4,128,128]{2,1,0:T(8,128)(2,1)S(1)} %add_convert_fusion.3.low_ref, ...), custom_call_target="tpu_custom_call" | custom-call | flops 67108864 | bytes 1000000 | tf_op jit(solution)/shard_map/pallas_call | solution.py:418
  97.5 2.8 %collective-permute-start.26 = (bf16[4,32,256]{2,1,0:T(8,128)(2,1)S(1)}, bf16[4,32,256]{2,1,0:T(8,128)(2,1)S(1)}, u32[]{:S(2)}, u32[]{:S(2)}) collective-permute-start(bf16[4,32,256]{2,1,0:T(8,128)(2,1)S(1)} %get-tuple-element.50), channel_id=1, source_target_pairs={{0,24},{8,0},{16,8},{24,16},{1,25},{9,1},{17,9},{25,17},{2,26},{10... | collective-permute-start | bytes 196616 | tf_op jit(solution)/shard_map/ppermute | solution.py:466
  103.2 7.2 %shard_map.74 = (f32[448,256]{1,0:T(8,128)}, f32[448,128]{1,0:T(8,128)}) custom-call(bf16[448,8192]{1,0:T(8,128)(2,1)} %hidden_ref.5, bf16[64,128]{1,0:T(8,128)(2,1)} %bitcast.12, bf16[16384,128]{1,0:T(8,128)(2,1)} %bitcast.9, f32[448,256]{1,0:T(8,128)} %get-tuple-element.29.refs_0_, f32[448,128]{1,0:T(8,128)} %get-tuple-element.30.refs_1_), custom_call_target="tpu_custom_call" | custom-call | flops 939524096 | bytes 6000000 | tf_op jit(solution)/shard_map/pallas_call | solution.py:224
  (72 shorter events, 26.8 us)
Async XLA Ops:
  1.9 16.0 %collective-permute-start.3 = (bf16[1152,128]{1,0:T(8,128)(2,1)}, bf16[1152,128]{1,0:T(8,128)(2,1)S(1)}, u32[]{:S(2)}, u32[]{:S(2)}) collective-permute-start(bf16[1152,128]{1,0:T(8,128)(2,1)} %get-tuple-element.39.refs_4_), channel_id=1, source_target_pairs={{0,1},{1,2},{2,3},{3,4},{4,5},{5,6},{6,7},{7,0},{8,9},{9,10},{10,1... | collective-permute-start | bytes 884744 | tf_op jit(solution)/shard_map/ppermute | solution.py:466
  9.4 23.6 %collective-permute-start = (bf16[9,32,1024]{2,1,0:T(8,128)(2,1)}, bf16[9,32,1024]{2,1,0:T(8,128)(2,1)S(1)}, u32[]{:S(2)}, u32[]{:S(2)}) collective-permute-start(bf16[9,32,1024]{2,1,0:T(8,128)(2,1)} %get-tuple-element.36), channel_id=1, source_target_pairs={{0,8},{8,16},{16,24},{24,0},{1,9},{9,17},{17,25},{25,1},{2,10},{10... | collective-permute-start | bytes 1769480 | tf_op jit(solution)/shard_map/ppermute | solution.py:466
  11.1 28.5 %collective-permute-start.1 = (bf16[9,32,1024]{2,1,0:T(8,128)(2,1)}, bf16[9,32,1024]{2,1,0:T(8,128)(2,1)S(1)}, u32[]{:S(2)}, u32[]{:S(2)}) collective-permute-start(bf16[9,32,1024]{2,1,0:T(8,128)(2,1)} %get-tuple-element.37), channel_id=1, source_target_pairs={{0,16},{8,24},{16,0},{24,8},{1,17},{9,25},{17,1},{25,9},{2,18},{10... | collective-permute-start | bytes 1769480 | tf_op jit(solution)/shard_map/ppermute | solution.py:466
  14.0 11.4 %collective-permute-start.6 = (bf16[1152,128]{1,0:T(8,128)(2,1)S(1)}, bf16[1152,128]{1,0:T(8,128)(2,1)S(1)}, u32[]{:S(2)}, u32[]{:S(2)}) collective-permute-start(bf16[1152,128]{1,0:T(8,128)(2,1)S(1)} %copy-done.3), channel_id=1, source_target_pairs={{0,7},{1,0},{2,1},{3,2},{4,3},{5,4},{6,5},{7,6},{8,15},{9,8},{10,9... | collective-permute-start | bytes 884744 | tf_op jit(solution)/shard_map/ppermute | solution.py:466
  17.9 9.6 %collective-permute-start.4 = (bf16[1152,128]{1,0:T(8,128)(2,1)S(1)}, bf16[1152,128]{1,0:T(8,128)(2,1)S(1)}, u32[]{:S(2)}, u32[]{:S(2)}) collective-permute-start(bf16[1152,128]{1,0:T(8,128)(2,1)S(1)} %copy-done.3), channel_id=1, source_target_pairs={{0,1},{1,2},{2,3},{3,4},{4,5},{5,6},{6,7},{7,0},{8,9},{9,10},{10,1... | collective-permute-start | bytes 884744 | tf_op jit(solution)/shard_map/ppermute | solution.py:466
  17.9 13.7 %collective-permute-start.5 = (bf16[1152,128]{1,0:T(8,128)(2,1)S(1)}, bf16[1152,128]{1,0:T(8,128)(2,1)S(1)}, u32[]{:S(2)}, u32[]{:S(2)}) collective-permute-start(bf16[1152,128]{1,0:T(8,128)(2,1)S(1)} %copy-done.2), channel_id=1, source_target_pairs={{0,7},{1,0},{2,1},{3,2},{4,3},{5,4},{6,5},{7,6},{8,15},{9,8},{10,9... | collective-permute-start | bytes 884744 | tf_op jit(solution)/shard_map/ppermute | solution.py:466
  25.3 18.5 %collective-permute-start.7 = (bf16[1152,128]{1,0:T(8,128)(2,1)S(1)}, bf16[1152,128]{1,0:T(8,128)(2,1)S(1)}, u32[]{:S(2)}, u32[]{:S(2)}) collective-permute-start(bf16[1152,128]{1,0:T(8,128)(2,1)S(1)} %collective-permute-done.3.refs_6_), channel_id=1, source_target_pairs={{0,1},{1,2},{2,3},{3,4},{4,5},{5,6},{6,7},{7,0},{8,9},{9,10},{10,1... | collective-permute-start | bytes 884744 | tf_op jit(solution)/shard_map/ppermute | solution.py:466
  27.5 16.3 %collective-permute-start.10 = (bf16[1152,128]{1,0:T(8,128)(2,1)S(1)}, bf16[1152,128]{1,0:T(8,128)(2,1)S(1)}, u32[]{:S(2)}, u32[]{:S(2)}) collective-permute-start(bf16[1152,128]{1,0:T(8,128)(2,1)S(1)} %collective-permute-done.6.refs_9_), channel_id=1, source_target_pairs={{0,7},{1,0},{2,1},{3,2},{4,3},{5,4},{6,5},{7,6},{8,15},{9,8},{10,9... | collective-permute-start | bytes 884744 | tf_op jit(solution)/shard_map/ppermute | solution.py:466
  31.7 29.6 %collective-permute-start.2 = (bf16[9,32,1024]{2,1,0:T(8,128)(2,1)}, bf16[9,32,1024]{2,1,0:T(8,128)(2,1)S(1)}, u32[]{:S(2)}, u32[]{:S(2)}) collective-permute-start(bf16[9,32,1024]{2,1,0:T(8,128)(2,1)} %get-tuple-element.38), channel_id=1, source_target_pairs={{0,24},{8,0},{16,8},{24,16},{1,25},{9,1},{17,9},{25,17},{2,26},{10... | collective-permute-start | bytes 1769480 | tf_op jit(solution)/shard_map/ppermute | solution.py:466
  33.0 14.1 %collective-permute-start.8 = (bf16[1152,128]{1,0:T(8,128)(2,1)S(1)}, bf16[1152,128]{1,0:T(8,128)(2,1)S(1)}, u32[]{:S(2)}, u32[]{:S(2)}) collective-permute-start(bf16[1152,128]{1,0:T(8,128)(2,1)S(1)} %collective-permute-done.4.refs_7_), channel_id=1, source_target_pairs={{0,1},{1,2},{2,3},{3,4},{4,5},{5,6},{6,7},{7,0},{8,9},{9,10},{10,1... | collective-permute-start | bytes 884744 | tf_op jit(solution)/shard_map/ppermute | solution.py:466
  39.6 11.6 %collective-permute-start.9 = (bf16[1152,128]{1,0:T(8,128)(2,1)S(1)}, bf16[1152,128]{1,0:T(8,128)(2,1)S(1)}, u32[]{:S(2)}, u32[]{:S(2)}) collective-permute-start(bf16[1152,128]{1,0:T(8,128)(2,1)S(1)} %collective-permute-done.5.refs_8_), channel_id=1, source_target_pairs={{0,7},{1,0},{2,1},{3,2},{4,3},{5,4},{6,5},{7,6},{8,15},{9,8},{10,9... | collective-permute-start | bytes 884744 | tf_op jit(solution)/shard_map/ppermute | solution.py:466
  43.8 11.1 %collective-permute-start.17 = (bf16[1152,128]{1,0:T(8,128)(2,1)S(1)}, bf16[1152,128]{1,0:T(8,128)(2,1)S(1)}, u32[]{:S(2)}, u32[]{:S(2)}) collective-permute-start(bf16[1152,128]{1,0:T(8,128)(2,1)S(1)} %collective-permute-done.7.refs_10_), channel_id=1, source_target_pairs={{0,1},{1,2},{2,3},{3,4},{4,5},{5,6},{6,7},{7,0},{8,9},{9,10},{10,1... | collective-permute-start | bytes 884744 | tf_op jit(solution)/shard_map/ppermute | solution.py:466
  43.8 13.7 %collective-permute-start.20 = (bf16[1152,128]{1,0:T(8,128)(2,1)S(1)}, bf16[1152,128]{1,0:T(8,128)(2,1)S(1)}, u32[]{:S(2)}, u32[]{:S(2)}) collective-permute-start(bf16[1152,128]{1,0:T(8,128)(2,1)S(1)} %collective-permute-done.10.refs_13_), channel_id=1, source_target_pairs={{0,7},{1,0},{2,1},{3,2},{4,3},{5,4},{6,5},{7,6},{8,15},{9,8},{10,9... | collective-permute-start | bytes 884744 | tf_op jit(solution)/shard_map/ppermute | solution.py:466
  47.1 25.6 %collective-permute-start.18 = (bf16[1152,128]{1,0:T(8,128)(2,1)S(1)}, bf16[1152,128]{1,0:T(8,128)(2,1)S(1)}, u32[]{:S(2)}, u32[]{:S(2)}) collective-permute-start(bf16[1152,128]{1,0:T(8,128)(2,1)S(1)} %collective-permute-done.8.refs_11_), channel_id=1, source_target_pairs={{0,1},{1,2},{2,3},{3,4},{4,5},{5,6},{6,7},{7,0},{8,9},{9,10},{10,1... | collective-permute-start | bytes 884744 | tf_op jit(solution)/shard_map/ppermute | solution.py:466
  51.2 21.4 %collective-permute-start.19 = (bf16[1152,128]{1,0:T(8,128)(2,1)S(1)}, bf16[1152,128]{1,0:T(8,128)(2,1)}, u32[]{:S(2)}, u32[]{:S(2)}) collective-permute-start(bf16[1152,128]{1,0:T(8,128)(2,1)S(1)} %collective-permute-done.9.refs_12_), channel_id=1, source_target_pairs={{0,7},{1,0},{2,1},{3,2},{4,3},{5,4},{6,5},{7,6},{8,15},{9,8},{10,9... | collective-permute-start | bytes 884744 | tf_op jit(solution)/shard_map/ppermute | solution.py:466
  54.9 17.7 %collective-permute-start.21 = (bf16[1152,128]{1,0:T(8,128)(2,1)S(1)}, bf16[1152,128]{1,0:T(8,128)(2,1)}, u32[]{:S(2)}, u32[]{:S(2)}) collective-permute-start(bf16[1152,128]{1,0:T(8,128)(2,1)S(1)} %collective-permute-done.17.refs_4_.refs_14_), channel_id=1, source_target_pairs={{0,1},{1,2},{2,3},{3,4},{4,5},{5,6},{6,7},{7,0},{8,9},{9,10},{10,1... | collective-permute-start | bytes 884744 | tf_op jit(solution)/shard_map/ppermute | solution.py:466
  57.5 15.1 %collective-permute-start.22 = (bf16[1152,128]{1,0:T(8,128)(2,1)S(1)}, bf16[1152,128]{1,0:T(8,128)(2,1)}, u32[]{:S(2)}, u32[]{:S(2)}) collective-permute-start(bf16[1152,128]{1,0:T(8,128)(2,1)S(1)} %collective-permute-done.20.refs_7_.refs_17_), channel_id=1, source_target_pairs={{0,7},{1,0},{2,1},{3,2},{4,3},{5,4},{6,5},{7,6},{8,15},{9,8},{10,9... | collective-permute-start | bytes 884744 | tf_op jit(solution)/shard_map/ppermute | solution.py:466
  65.8 10.8 %collective-permute-start.11 = (bf16[5,128,128]{2,1,0:T(8,128)(2,1)}, bf16[5,128,128]{2,1,0:T(8,128)(2,1)}, u32[]{:S(2)}, u32[]{:S(2)}) collective-permute-start(bf16[5,128,128]{2,1,0:T(8,128)(2,1)} %get-tuple-element.41), channel_id=1, source_target_pairs={{0,32},{32,0},{1,33},{33,1},{2,34},{34,2},{3,35},{35,3},{4,36},{36... | collective-permute-start | bytes 491528 | tf_op jit(solution)/shard_map/ppermute | solution.py:470
  86.7 8.9 %collective-permute-start.25 = (bf16[4,128,128]{2,1,0:T(8,128)(2,1)S(1)}, bf16[4,128,128]{2,1,0:T(8,128)(2,1)S(1)}, u32[]{:S(2)}, u32[]{:S(2)}) collective-permute-start(bf16[4,128,128]{2,1,0:T(8,128)(2,1)S(1)} %add_convert_fusion.4), channel_id=1, source_target_pairs={{0,192},{64,128},{128,64},{192,0},{1,193},{65,129},{129,65},{193,1... | collective-permute-start | bytes 393224 | tf_op jit(solution)/shard_map/ppermute | solution.py:470
  93.4 17.3 %collective-permute-start.15 = (bf16[5,32,256]{2,1,0:T(8,128)(2,1)S(1)}, bf16[5,32,256]{2,1,0:T(8,128)(2,1)S(1)}, u32[]{:S(2)}, u32[]{:S(2)}) collective-permute-start(bf16[5,32,256]{2,1,0:T(8,128)(2,1)S(1)} %get-tuple-element.44), channel_id=1, source_target_pairs={{0,16},{8,24},{16,0},{24,8},{1,17},{9,25},{17,1},{25,9},{2,18},{10... | collective-permute-start | bytes 245768 | tf_op jit(solution)/shard_map/ppermute | solution.py:466
  94.2 16.5 %collective-permute-start.16 = (bf16[5,32,256]{2,1,0:T(8,128)(2,1)S(1)}, bf16[5,32,256]{2,1,0:T(8,128)(2,1)S(1)}, u32[]{:S(2)}, u32[]{:S(2)}) collective-permute-start(bf16[5,32,256]{2,1,0:T(8,128)(2,1)S(1)} %get-tuple-element.45), channel_id=1, source_target_pairs={{0,8},{8,16},{16,24},{24,0},{1,9},{9,17},{17,25},{25,1},{2,10},{10... | collective-permute-start | bytes 245768 | tf_op jit(solution)/shard_map/ppermute | solution.py:466
  97.5 15.6 %collective-permute-start.26 = (bf16[4,32,256]{2,1,0:T(8,128)(2,1)S(1)}, bf16[4,32,256]{2,1,0:T(8,128)(2,1)S(1)}, u32[]{:S(2)}, u32[]{:S(2)}) collective-permute-start(bf16[4,32,256]{2,1,0:T(8,128)(2,1)S(1)} %get-tuple-element.50), channel_id=1, source_target_pairs={{0,24},{8,0},{16,8},{24,16},{1,25},{9,1},{17,9},{25,17},{2,26},{10... | collective-permute-start | bytes 196616 | tf_op jit(solution)/shard_map/ppermute | solution.py:466
  100.4 12.8 %collective-permute-start.27 = (bf16[4,32,256]{2,1,0:T(8,128)(2,1)S(1)}, bf16[4,32,256]{2,1,0:T(8,128)(2,1)S(1)}, u32[]{:S(2)}, u32[]{:S(2)}) collective-permute-start(bf16[4,32,256]{2,1,0:T(8,128)(2,1)S(1)} %get-tuple-element.51), channel_id=1, source_target_pairs={{0,16},{8,24},{16,0},{24,8},{1,17},{9,25},{17,1},{25,9},{2,18},{10... | collective-permute-start | bytes 196616 | tf_op jit(solution)/shard_map/ppermute | solution.py:466
  101.9 11.2 %collective-permute-start.28 = (bf16[4,32,256]{2,1,0:T(8,128)(2,1)S(1)}, bf16[4,32,256]{2,1,0:T(8,128)(2,1)S(1)}, u32[]{:S(2)}, u32[]{:S(2)}) collective-permute-start(bf16[4,32,256]{2,1,0:T(8,128)(2,1)S(1)} %get-tuple-element.52), channel_id=1, source_target_pairs={{0,8},{8,16},{16,24},{24,0},{1,9},{9,17},{17,25},{25,1},{2,10},{10... | collective-permute-start | bytes 196616 | tf_op jit(solution)/shard_map/ppermute | solution.py:466
  (14 other events, 94.4 us)

commit v6 on v5

--- a/solution.py
+++ b/solution.py
@@ -28,7 +28,6 @@
 RANK2 = 128
 CHUNK = COLS + RANK2
 VMEM_LIMIT = 20 * 1024 * 1024
-WIDE_LIMIT = 58 * 1024 * 1024
 PACK_LIMIT = 66_200_000
 
 
@@ -85,12 +84,12 @@
 
 def gain_row(gain):
     wide = gain.astype(F32)
-    return jnp.concatenate([wide[i : i + 1] for i in range(8)], axis=1)
+    return jnp.concatenate([wide[i : i + 1] for i in range(gain.shape[0])], axis=1)
 
 
 def dispatch_kernel(place_ref, hidden_ref, gain_ref, pair_ref, table_ref, *outs):
     sends = outs[:NY]
-    dst_ref, hot_ref = outs[NY:]
+    dst_ref, hot_ref, stage_ref, sems = outs[NY:]
     own = (hidden_ref[...].astype(F32) * gain_row(gain_ref[...])).astype(BF16)
     y_me = place_ref[1].astype(F32)
     z_me = place_ref[2].astype(F32)
@@ -116,16 +115,22 @@
     dst_ref[...] = dst
     hot_ref[0] = jnp.max(jnp.where(over, rank, -1.0)).astype(jnp.int32)
     spot = jnp.where(iota((TOK, 128), 1) == to_column(place, TOK), 1.0, 0.0).astype(BF16)
-    for part in range(NY):
+    copies = []
+    for part in (2, 1, 3, 0):
         pick = jnp.where(iota((SLOTS, TOK), 0) + part * SLOTS == dst, 1.0, 0.0).astype(BF16)
         rows = jnp.dot(pick, own, preferred_element_type=F32).astype(BF16)
-        sends[part][...] = rows.reshape(BUCKETS, BLOCK, COLS)
+        stage_ref[part] = rows.reshape(BUCKETS, BLOCK, COLS)
         marks = jnp.where(iota((16, TOK), 0) + part * BUCKETS == bucket, local, 0.0).astype(BF16)
         ids = jnp.dot(marks, spot, preferred_element_type=F32)
         for b in range(BUCKETS):
             head = rows[b * BLOCK : (b + 1) * BLOCK, :128].astype(F32)
             head = jnp.where(iota((BLOCK, 128), 0) == CAP, ids[b : b + 1], head)
-            sends[part][b, :, pl.ds(0, 128)] = head.astype(BF16)
+            stage_ref[part, b, :, pl.ds(0, 128)] = head.astype(BF16)
+        copy = pltpu.make_async_copy(stage_ref.at[part], sends[part], sems.at[part])
+        copy.start()
+        copies.append(copy)
+    for copy in copies:
+        copy.wait()
 
 
 def dispatch(place, hidden, gain, pair, table):
@@ -141,12 +146,15 @@
                 pl.BlockSpec((1, TOK), lambda i, p: (0, 0)),
                 pl.BlockSpec((1, table.shape[1]), lambda i, p: (0, 0)),
             ],
-            out_specs=[pl.BlockSpec((BUCKETS, BLOCK, COLS), lambda i, p: (0, 0, 0))] * NY
+            out_specs=[pl.BlockSpec(memory_space=pl.ANY)] * NY
             + [pl.BlockSpec((1, TOK), lambda i, p: (0, 0)), scalars()],
+            scratch_shapes=[
+                pltpu.VMEM((NY, BUCKETS, BLOCK, COLS), BF16),
+                pltpu.SemaphoreType.DMA((NY,)),
+            ],
         ),
         out_shape=[message] * NY
         + [jax.ShapeDtypeStruct((1, TOK), F32), jax.ShapeDtypeStruct((1,), jnp.int32)],
-        compiler_params=pltpu.CompilerParams(vmem_limit_bytes=WIDE_LIMIT),
         cost_estimate=pl.CostEstimate(
             flops=2 * NY * SLOTS * TOK * COLS, bytes_accessed=4_000_000, transcendentals=0
         ),
@@ -193,11 +201,9 @@
     part_rows = jnp.where(
         lax.broadcasted_iota(jnp.int32, (256, 256), 1) == source, 1.0, 0.0
     ).astype(BF16)
-    first = (part * pl.num_programs(0) + step) * (2 * tile)
     for b in range(0, 2 * tile, 512):
-        at = pl.multiple_of(first + b, 512)
         pair = jnp.concatenate(
-            [mixed_ref[pl.ds(at, 256), :], mixed_ref[pl.ds(at + 256, 256), :]], axis=1
+            [mixed_ref[b : b + 256], mixed_ref[b + 256 : b + 512]], axis=1
         )
         parted = jnp.dot(part_rows, pair, preferred_element_type=F32).astype(BF16)
         d = b // 2
@@ -218,25 +224,25 @@
 
 
 def base_projection(part, hidden, gain, weight, *begun):
-    tile = 1024
+    tile = 2048
     steps = DIM // tile // 2
     first = part * steps
+    sums = [pl.BlockSpec((TOK, 256), lambda k: (0, 0)), pl.BlockSpec((TOK, 128), lambda k: (0, 0))]
     return pl.pallas_call(
         functools.partial(base_kernel, part),
         grid=(steps,),
         in_specs=[
             pl.BlockSpec((TOK, tile), lambda k: (0, first + k)),
-            pl.BlockSpec((8, 128), lambda k: (first + k, 0)),
-            whole(),
+            pl.BlockSpec((tile // 128, 128), lambda k: (first + k, 0)),
+            pl.BlockSpec((2 * tile, 128), lambda k: (first + k, 0)),
         ]
-        + [whole()] * len(begun),
-        out_specs=[whole()] * 2,
+        + sums[: len(begun)],
+        out_specs=sums,
         out_shape=[
             jax.ShapeDtypeStruct((TOK, 256), F32),
             jax.ShapeDtypeStruct((TOK, 128), F32),
         ],
         scratch_shapes=[pltpu.VMEM((TOK, tile), BF16), pltpu.VMEM((tile, 256), BF16)],
-        compiler_params=pltpu.CompilerParams(vmem_limit_bytes=WIDE_LIMIT),
         cost_estimate=pl.CostEstimate(
             flops=TOK * DIM * 256, bytes_accessed=6_000_000, transcendentals=0
         ),

time: 115 us -> 116 us (level)
  waiting for transfers between devices: 31 us -> 26.7 us
  local copies, waits for them, and re-layouts: 5.13 us -> 9.09 us
    ppermute x6, waiting for transfers between devices: 9.26 us -> 5.19 us  [pair_sum(): other = lax.ppermute(x, axis, [(i, i ^ flip) for i in range(size)])]
    unnamed x18 -> x44, local copies, waits for them, and re-layouts: 4.38 us -> 8.34 us
    pallas_call x2, Pallas kernels: 14.1 us -> 10.8 us  [base_projection(): pl.pallas_call(functools.partial(base_kernel, part), grid=(steps,), in_sp...]
    pallas_call x1, Pallas kernels: 0.46 us -> 2.18 us  [up_early(): pl.pallas_call(up_early_kernel, in_specs=[whole()] * (1 + NY + len(chunks...]
  transfers between devices with their start and end apart: 29 -> 29, of which waited for: 9 -> 8; matrix products, arithmetic and copies ran while one was open for 2% -> 2% of each run, Pallas kernels for 26% -> 26%
where the time goes in v6:
time: 116 us; the launch traced here: 115 us
  starting transfers between devices  44.6 us (38%)
  Pallas kernels  32.4 us (28%)
  waiting for transfers between devices  26.7 us (23%)
  local copies, waits for them, and re-layouts  9.09 us (8%)
  other arithmetic  1.91 us (2%)
    ppermute x23, starting transfers between devices, shift(): return lax.ppermute(x, axis, [(i, (i + by) % size) for i in range(size)])  40 us
    ppermute x23, waiting for transfers between devices, shift(): return lax.ppermute(x, axis, [(i, (i + by) % size) for i in range(size)])  21.5 us
    pallas_call x2, Pallas kernels, base_projection(): pl.pallas_call(functools.partial(base_kernel, part), grid=(steps,), in_sp...  10.8 us
    unnamed x44, local copies, waits for them, and re-layouts  8.34 us
    pallas_call x1, Pallas kernels, dispatch(): pl.pallas_call(dispatch_kernel, grid_spec=pltpu.PrefetchScalarGridSpec(nu...  5.48 us
    ppermute x6, waiting for transfers between devices, pair_sum(): other = lax.ppermute(x, axis, [(i, i ^ flip) for i in range(size)])  5.19 us
    ppermute x6, starting transfers between devices, pair_sum(): other = lax.ppermute(x, axis, [(i, i ^ flip) for i in range(size)])  4.57 us
    pallas_call x1, Pallas kernels, down_early(): pl.pallas_call(down_early_kernel, in_specs=[scalars()] + [whole()] * (NY...  3.9 us
  transfers between devices with their start and end apart: 29, of which 8 were waited for; matrix products, arithmetic and copies ran while one was open for 2% of the time, Pallas kernels for 26%

profile of v6, /device:TPU:6, one launch (start us, length us, event | category | flops | bytes accessed | tf_op | source)
XLA Modules:
  0.0 115.0 jit_solution(8528429470588453526)
XLA Ops:
  0.0 1.9 %shard_map.77 = (bf16[1152,128]{1,0:T(8,128)(2,1)}, bf16[1152,128]{1,0:T(8,128)(2,1)}) custom-call(bf16[2,1024,128]{2,1,0:T(8,128)(2,1)} %down_ref.1, bf16[2,128,128]{2,1,0:T(8,128)(2,1)} %bitcast.13), custom_call_target="tpu_custom_call" | custom-call | bytes 1200000 | tf_op jit(solution)/shard_map/pallas_call | solution.py:74
  1.9 2.0 %collective-permute-start.3 = (bf16[1152,128]{1,0:T(8,128)(2,1)}, bf16[1152,128]{1,0:T(8,128)(2,1)S(1)}, u32[]{:S(2)}, u32[]{:S(2)}) collective-permute-start(bf16[1152,128]{1,0:T(8,128)(2,1)} %get-tuple-element.39.refs_4_), channel_id=1, source_target_pairs={{0,1},{1,2},{2,3},{3,4},{4,5},{5,6},{6,7},{7,0},{8,9},{9,10},{10,1... | collective-permute-start | bytes 884744 | tf_op jit(solution)/shard_map/ppermute | solution.py:472
  4.6 5.5 %shard_map.75 = (bf16[9,32,1024]{2,1,0:T(8,128)(2,1)}, bf16[9,32,1024]{2,1,0:T(8,128)(2,1)}, bf16[9,32,1024]{2,1,0:T(8,128)(2,1)}, bf16[9,32,1024]{2,1,0:T(8,128)(2,1)}, f32[1,448]{1,0:T(1,128)}, /*index=5*/s32[1]{0:T(128)}) custom-call(s32[3]{0:T(128)} %pad_add_fusion.place_ref, bf16[448,8192]{1,0:T(8,128)(2,1)} %hidden_ref.5, bf16[64,128]{1,0:T(8,128)(2,1)} %bitcast.10, ...), custom_call_target="tpu_custom_call" | custom-call | flops 1056964608 | bytes 4000000 | tf_op jit(solution)/shard_map/pallas_call | solution.py:138
  11.7 2.9 %collective-permute-start.1 = (bf16[9,32,1024]{2,1,0:T(8,128)(2,1)}, bf16[9,32,1024]{2,1,0:T(8,128)(2,1)S(1)}, u32[]{:S(2)}, u32[]{:S(2)}) collective-permute-start(bf16[9,32,1024]{2,1,0:T(8,128)(2,1)} %get-tuple-element.37), channel_id=1, source_target_pairs={{0,16},{8,24},{16,0},{24,8},{1,17},{9,25},{17,1},{25,9},{2,18},{10... | collective-permute-start | bytes 1769480 | tf_op jit(solution)/shard_map/ppermute | solution.py:472
  14.6 4.0 %collective-permute-start.6 = (bf16[1152,128]{1,0:T(8,128)(2,1)S(1)}, bf16[1152,128]{1,0:T(8,128)(2,1)S(1)}, u32[]{:S(2)}, u32[]{:S(2)}) collective-permute-start(bf16[1152,128]{1,0:T(8,128)(2,1)S(1)} %copy-done.3), channel_id=1, source_target_pairs={{0,7},{1,0},{2,1},{3,2},{4,3},{5,4},{6,5},{7,6},{8,15},{9,8},{10,9... | collective-permute-start | bytes 884744 | tf_op jit(solution)/shard_map/ppermute | solution.py:472
  18.6 3.2 %collective-permute-start.5 = (bf16[1152,128]{1,0:T(8,128)(2,1)S(1)}, bf16[1152,128]{1,0:T(8,128)(2,1)S(1)}, u32[]{:S(2)}, u32[]{:S(2)}) collective-permute-start(bf16[1152,128]{1,0:T(8,128)(2,1)S(1)} %copy-done.2), channel_id=1, source_target_pairs={{0,7},{1,0},{2,1},{3,2},{4,3},{5,4},{6,5},{7,6},{8,15},{9,8},{10,9... | collective-permute-start | bytes 884744 | tf_op jit(solution)/shard_map/ppermute | solution.py:472
  21.8 4.2 %collective-permute-done.6.refs_9_ = bf16[1152,128]{1,0:T(8,128)(2,1)S(1)} collective-permute-done((bf16[1152,128]{1,0:T(8,128)(2,1)S(1)}, bf16[1152,128]{1,0:T(8,128)(2,1)S(1)}, u32[]{:S(2)}, u32[]{:S(2)}) %collective-permute-start.6) | collective-permute-done | bytes 294944 | tf_op jit(solution)/shard_map/ppermute | solution.py:472
  29.8 2.5 %collective-permute-done.5.refs_8_ = bf16[1152,128]{1,0:T(8,128)(2,1)S(1)} collective-permute-done((bf16[1152,128]{1,0:T(8,128)(2,1)S(1)}, bf16[1152,128]{1,0:T(8,128)(2,1)S(1)}, u32[]{:S(2)}, u32[]{:S(2)}) %collective-permute-start.5) | collective-permute-done | bytes 294944 | tf_op jit(solution)/shard_map/ppermute | solution.py:472
  33.8 6.4 %collective-permute-done.1.refs_2_ = bf16[9,32,1024]{2,1,0:T(8,128)(2,1)S(1)} collective-permute-done((bf16[9,32,1024]{2,1,0:T(8,128)(2,1)}, bf16[9,32,1024]{2,1,0:T(8,128)(2,1)S(1)}, u32[]{:S(2)}, u32[]{:S(2)}) %collective-permute-start.1) | collective-permute-done | bytes 589856 | tf_op jit(solution)/shard_map/ppermute | solution.py:472
  40.2 4.2 %collective-permute-start.9 = (bf16[1152,128]{1,0:T(8,128)(2,1)S(1)}, bf16[1152,128]{1,0:T(8,128)(2,1)}, u32[]{:S(2)}, u32[]{:S(2)}) collective-permute-start(bf16[1152,128]{1,0:T(8,128)(2,1)S(1)} %collective-permute-done.5.refs_8_), channel_id=1, source_target_pairs={{0,7},{1,0},{2,1},{3,2},{4,3},{5,4},{6,5},{7,6},{8,15},{9,8},{10,9... | collective-permute-start | bytes 884744 | tf_op jit(solution)/shard_map/ppermute | solution.py:472
  44.5 3.2 %collective-permute-start.20 = (bf16[1152,128]{1,0:T(8,128)(2,1)S(1)}, bf16[1152,128]{1,0:T(8,128)(2,1)}, u32[]{:S(2)}, u32[]{:S(2)}) collective-permute-start(bf16[1152,128]{1,0:T(8,128)(2,1)S(1)} %collective-permute-done.10.refs_13_), channel_id=1, source_target_pairs={{0,7},{1,0},{2,1},{3,2},{4,3},{5,4},{6,5},{7,6},{8,15},{9,8},{10,9... | collective-permute-start | bytes 884744 | tf_op jit(solution)/shard_map/ppermute | solution.py:472
  47.7 4.1 %collective-permute-done.9.refs_12_ = bf16[1152,128]{1,0:T(8,128)(2,1)} collective-permute-done((bf16[1152,128]{1,0:T(8,128)(2,1)S(1)}, bf16[1152,128]{1,0:T(8,128)(2,1)}, u32[]{:S(2)}, u32[]{:S(2)}) %collective-permute-start.9) | collective-permute-done | bytes 294944 | tf_op jit(solution)/shard_map/ppermute | solution.py:472
  51.9 3.8 %collective-permute-start.19 = (bf16[1152,128]{1,0:T(8,128)(2,1)}, bf16[1152,128]{1,0:T(8,128)(2,1)}, u32[]{:S(2)}, u32[]{:S(2)}) collective-permute-start(bf16[1152,128]{1,0:T(8,128)(2,1)} %collective-permute-done.9.refs_12_), channel_id=1, source_target_pairs={{0,7},{1,0},{2,1},{3,2},{4,3},{5,4},{6,5},{7,6},{8,15},{9,8},{10,9... | collective-permute-start | bytes 884744 | tf_op jit(solution)/shard_map/ppermute | solution.py:472
  55.7 2.5 %collective-permute-done.20.refs_7_.refs_17_ = bf16[1152,128]{1,0:T(8,128)(2,1)} collective-permute-done((bf16[1152,128]{1,0:T(8,128)(2,1)S(1)}, bf16[1152,128]{1,0:T(8,128)(2,1)}, u32[]{:S(2)}, u32[]{:S(2)}) %collective-permute-start.20) | collective-permute-done | bytes 294944 | tf_op jit(solution)/shard_map/ppermute | solution.py:472
  58.2 3.8 %collective-permute-start.22 = (bf16[1152,128]{1,0:T(8,128)(2,1)}, bf16[1152,128]{1,0:T(8,128)(2,1)}, u32[]{:S(2)}, u32[]{:S(2)}) collective-permute-start(bf16[1152,128]{1,0:T(8,128)(2,1)} %collective-permute-done.20.refs_7_.refs_17_), channel_id=1, source_target_pairs={{0,7},{1,0},{2,1},{3,2},{4,3},{5,4},{6,5},{7,6},{8,15},{9,8},{10,9... | collective-permute-start | bytes 884744 | tf_op jit(solution)/shard_map/ppermute | solution.py:472
  63.1 3.9 %shard_map.78 = (bf16[5,128,128]{2,1,0:T(8,128)(2,1)}, bf16[128,128]{1,0:T(8,128)(2,1)S(1)}) custom-call(s32[1]{0:T(128)} %get-tuple-element.34.hot_ref, bf16[9,32,1024]{2,1,0:T(8,128)(2,1)S(1)} %copy-done, bf16[9,32,1024]{2,1,0:T(8,128)(2,1)S(1)} %collective-permute-done.refs_1_, bf16[9,32,1024]{2,1,0:T(8,128)(2,1)S(1)} %collective-permute-done.1.refs_2_, ...), custom_call_target="tpu_custom_call" | custom-call | flops 335544320 | bytes 6000000 | tf_op jit(solution)/shard_map/pallas_call | solution.py:286
  67.6 5.2 %shard_map.73 = (f32[448,256]{1,0:T(8,128)}, f32[448,128]{1,0:T(8,128)}) custom-call(bf16[448,8192]{1,0:T(8,128)(2,1)} %hidden_ref.5, bf16[64,128]{1,0:T(8,128)(2,1)} %bitcast.11, bf16[16384,128]{1,0:T(8,128)(2,1)} %bitcast.8), custom_call_target="tpu_custom_call" | custom-call | flops 939524096 | bytes 6000000 | tf_op jit(solution)/shard_map/pallas_call | solution.py:231
  73.7 2.8 %shard_map.81 = bf16[4,128,128]{2,1,0:T(8,128)(2,1)S(1)} custom-call(s32[1]{0:T(128)} %get-tuple-element.34.hot_ref, bf16[9,32,1024]{2,1,0:T(8,128)(2,1)S(1)} %copy-done.1, bf16[9,32,1024]{2,1,0:T(8,128)(2,1)S(1)} %collective-permute-done.refs_1_, bf16[9,32,1024]{2,1,0:T(8,128)(2,1)S(1)} %collective-permute-done.1.refs_2_, ...), custom_call_target="tpu_custom_call" | custom-call | flops 268435456 | bytes 2000000 | tf_op jit(solution)/shard_map/pallas_call | solution.py:318
  82.9 2.4 %shard_map.82 = (bf16[3,256,256]{2,1,0:T(8,128)(2,1)S(1)}, bf16[4,128,256]{2,1,0:T(8,128)(2,1)S(1)}) custom-call(s32[1]{0:T(128)} %get-tuple-element.34.hot_ref, bf16[9,32,1024]{2,1,0:T(8,128)(2,1)S(1)} %copy-done.1, bf16[9,32,1024]{2,1,0:T(8,128)(2,1)S(1)} %collective-permute-done.refs_1_, bf16[9,32,1024]{2,1,0:T(8,128)(2,1)S(1)} %collective-permute-done.1.refs_2_, ...), custom_call_target="tpu_custom_call" | custom-call | flops 4000000 | bytes 1500000 | tf_op jit(solution)/shard_map/pallas_call | solution.py:394
  87.2 3.3 %collective-permute-done.24 = bf16[4,128,128]{2,1,0:T(8,128)(2,1)S(1)} collective-permute-done((bf16[4,128,128]{2,1,0:T(8,128)(2,1)S(1)}, bf16[4,128,128]{2,1,0:T(8,128)(2,1)S(1)}, u32[]{:S(2)}, u32[]{:S(2)}) %collective-permute-start.24) | collective-permute-done | bytes 131104 | tf_op jit(solution)/shard_map/ppermute | solution.py:476
  93.8 2.2 %shard_map.79 = (bf16[5,32,256]{2,1,0:T(8,128)(2,1)S(1)}, bf16[5,32,256]{2,1,0:T(8,128)(2,1)S(1)}, bf16[5,32,256]{2,1,0:T(8,128)(2,1)}, bf16[5,32,256]{2,1,0:T(8,128)(2,1)}) custom-call(bf16[5,128,128]{2,1,0:T(8,128)(2,1)S(1)} %add_convert_fusion.low_ref, bf16[9,32,1024]{2,1,0:T(8,128)(2,1)S(1)} %copy-done.1, ...), custom_call_target="tpu_custom_call" | custom-call | flops 83886080 | bytes 1500000 | tf_op jit(solution)/shard_map/pallas_call | solution.py:364
  98.2 1.9 %shard_map.83 = (bf16[4,32,256]{2,1,0:T(8,128)(2,1)S(1)}, bf16[4,32,256]{2,1,0:T(8,128)(2,1)S(1)}, bf16[4,32,256]{2,1,0:T(8,128)(2,1)S(1)}, bf16[4,32,256]{2,1,0:T(8,128)(2,1)S(1)}) custom-call(s32[1]{0:T(128)} %get-tuple-element.34.hot_ref, bf16[4,128,128]{2,1,0:T(8,128)(2,1)S(1)} %add_convert_fusion.3.low_ref, ...), custom_call_target="tpu_custom_call" | custom-call | flops 67108864 | bytes 1000000 | tf_op jit(solution)/shard_map/pallas_call | solution.py:424
  100.1 2.6 %collective-permute-start.26 = (bf16[4,32,256]{2,1,0:T(8,128)(2,1)S(1)}, bf16[4,32,256]{2,1,0:T(8,128)(2,1)S(1)}, u32[]{:S(2)}, u32[]{:S(2)}) collective-permute-start(bf16[4,32,256]{2,1,0:T(8,128)(2,1)S(1)} %get-tuple-element.50), channel_id=1, source_target_pairs={{0,24},{8,0},{16,8},{24,16},{1,25},{9,1},{17,9},{25,17},{2,26},{10... | collective-permute-start | bytes 196616 | tf_op jit(solution)/shard_map/ppermute | solution.py:472
  105.6 5.6 %shard_map.74 = (f32[448,256]{1,0:T(8,128)}, f32[448,128]{1,0:T(8,128)}) custom-call(bf16[448,8192]{1,0:T(8,128)(2,1)} %hidden_ref.5, bf16[64,128]{1,0:T(8,128)(2,1)} %bitcast.12, bf16[16384,128]{1,0:T(8,128)(2,1)} %bitcast.9, f32[448,256]{1,0:T(8,128)} %get-tuple-element.29.refs_0_, f32[448,128]{1,0:T(8,128)} %get-tuple-element.30.refs_1_), custom_call_target="tpu_custom_call" | custom-call | flops 939524096 | bytes 6000000 | tf_op jit(solution)/shard_map/pallas_call | solution.py:231
  (98 shorter events, 30.6 us)
Async XLA Ops:
  1.9 16.7 %collective-permute-start.3 = (bf16[1152,128]{1,0:T(8,128)(2,1)}, bf16[1152,128]{1,0:T(8,128)(2,1)S(1)}, u32[]{:S(2)}, u32[]{:S(2)}) collective-permute-start(bf16[1152,128]{1,0:T(8,128)(2,1)} %get-tuple-element.39.refs_4_), channel_id=1, source_target_pairs={{0,1},{1,2},{2,3},{3,4},{4,5},{5,6},{6,7},{7,0},{8,9},{9,10},{10,1... | collective-permute-start | bytes 884744 | tf_op jit(solution)/shard_map/ppermute | solution.py:472
  10.1 23.6 %collective-permute-start = (bf16[9,32,1024]{2,1,0:T(8,128)(2,1)}, bf16[9,32,1024]{2,1,0:T(8,128)(2,1)S(1)}, u32[]{:S(2)}, u32[]{:S(2)}) collective-permute-start(bf16[9,32,1024]{2,1,0:T(8,128)(2,1)} %get-tuple-element.36), channel_id=1, source_target_pairs={{0,8},{8,16},{16,24},{24,0},{1,9},{9,17},{17,25},{25,1},{2,10},{10... | collective-permute-start | bytes 1769480 | tf_op jit(solution)/shard_map/ppermute | solution.py:472
  11.7 28.5 %collective-permute-start.1 = (bf16[9,32,1024]{2,1,0:T(8,128)(2,1)}, bf16[9,32,1024]{2,1,0:T(8,128)(2,1)S(1)}, u32[]{:S(2)}, u32[]{:S(2)}) collective-permute-start(bf16[9,32,1024]{2,1,0:T(8,128)(2,1)} %get-tuple-element.37), channel_id=1, source_target_pairs={{0,16},{8,24},{16,0},{24,8},{1,17},{9,25},{17,1},{25,9},{2,18},{10... | collective-permute-start | bytes 1769480 | tf_op jit(solution)/shard_map/ppermute | solution.py:472
  14.6 11.4 %collective-permute-start.6 = (bf16[1152,128]{1,0:T(8,128)(2,1)S(1)}, bf16[1152,128]{1,0:T(8,128)(2,1)S(1)}, u32[]{:S(2)}, u32[]{:S(2)}) collective-permute-start(bf16[1152,128]{1,0:T(8,128)(2,1)S(1)} %copy-done.3), channel_id=1, source_target_pairs={{0,7},{1,0},{2,1},{3,2},{4,3},{5,4},{6,5},{7,6},{8,15},{9,8},{10,9... | collective-permute-start | bytes 884744 | tf_op jit(solution)/shard_map/ppermute | solution.py:472
  18.6 9.6 %collective-permute-start.4 = (bf16[1152,128]{1,0:T(8,128)(2,1)S(1)}, bf16[1152,128]{1,0:T(8,128)(2,1)S(1)}, u32[]{:S(2)}, u32[]{:S(2)}) collective-permute-start(bf16[1152,128]{1,0:T(8,128)(2,1)S(1)} %copy-done.3), channel_id=1, source_target_pairs={{0,1},{1,2},{2,3},{3,4},{4,5},{5,6},{6,7},{7,0},{8,9},{9,10},{10,1... | collective-permute-start | bytes 884744 | tf_op jit(solution)/shard_map/ppermute | solution.py:472
  18.6 13.7 %collective-permute-start.5 = (bf16[1152,128]{1,0:T(8,128)(2,1)S(1)}, bf16[1152,128]{1,0:T(8,128)(2,1)S(1)}, u32[]{:S(2)}, u32[]{:S(2)}) collective-permute-start(bf16[1152,128]{1,0:T(8,128)(2,1)S(1)} %copy-done.2), channel_id=1, source_target_pairs={{0,7},{1,0},{2,1},{3,2},{4,3},{5,4},{6,5},{7,6},{8,15},{9,8},{10,9... | collective-permute-start | bytes 884744 | tf_op jit(solution)/shard_map/ppermute | solution.py:472
  26.0 18.5 %collective-permute-start.7 = (bf16[1152,128]{1,0:T(8,128)(2,1)S(1)}, bf16[1152,128]{1,0:T(8,128)(2,1)S(1)}, u32[]{:S(2)}, u32[]{:S(2)}) collective-permute-start(bf16[1152,128]{1,0:T(8,128)(2,1)S(1)} %collective-permute-done.3.refs_6_), channel_id=1, source_target_pairs={{0,1},{1,2},{2,3},{3,4},{4,5},{5,6},{6,7},{7,0},{8,9},{9,10},{10,1... | collective-permute-start | bytes 884744 | tf_op jit(solution)/shard_map/ppermute | solution.py:472
  28.2 16.3 %collective-permute-start.10 = (bf16[1152,128]{1,0:T(8,128)(2,1)S(1)}, bf16[1152,128]{1,0:T(8,128)(2,1)S(1)}, u32[]{:S(2)}, u32[]{:S(2)}) collective-permute-start(bf16[1152,128]{1,0:T(8,128)(2,1)S(1)} %collective-permute-done.6.refs_9_), channel_id=1, source_target_pairs={{0,7},{1,0},{2,1},{3,2},{4,3},{5,4},{6,5},{7,6},{8,15},{9,8},{10,9... | collective-permute-start | bytes 884744 | tf_op jit(solution)/shard_map/ppermute | solution.py:472
  32.3 29.7 %collective-permute-start.2 = (bf16[9,32,1024]{2,1,0:T(8,128)(2,1)}, bf16[9,32,1024]{2,1,0:T(8,128)(2,1)S(1)}, u32[]{:S(2)}, u32[]{:S(2)}) collective-permute-start(bf16[9,32,1024]{2,1,0:T(8,128)(2,1)} %get-tuple-element.38), channel_id=1, source_target_pairs={{0,24},{8,0},{16,8},{24,16},{1,25},{9,1},{17,9},{25,17},{2,26},{10... | collective-permute-start | bytes 1769480 | tf_op jit(solution)/shard_map/ppermute | solution.py:472
  33.7 14.1 %collective-permute-start.8 = (bf16[1152,128]{1,0:T(8,128)(2,1)S(1)}, bf16[1152,128]{1,0:T(8,128)(2,1)}, u32[]{:S(2)}, u32[]{:S(2)}) collective-permute-start(bf16[1152,128]{1,0:T(8,128)(2,1)S(1)} %collective-permute-done.4.refs_7_), channel_id=1, source_target_pairs={{0,1},{1,2},{2,3},{3,4},{4,5},{5,6},{6,7},{7,0},{8,9},{9,10},{10,1... | collective-permute-start | bytes 884744 | tf_op jit(solution)/shard_map/ppermute | solution.py:472
  40.2 11.6 %collective-permute-start.9 = (bf16[1152,128]{1,0:T(8,128)(2,1)S(1)}, bf16[1152,128]{1,0:T(8,128)(2,1)}, u32[]{:S(2)}, u32[]{:S(2)}) collective-permute-start(bf16[1152,128]{1,0:T(8,128)(2,1)S(1)} %collective-permute-done.5.refs_8_), channel_id=1, source_target_pairs={{0,7},{1,0},{2,1},{3,2},{4,3},{5,4},{6,5},{7,6},{8,15},{9,8},{10,9... | collective-permute-start | bytes 884744 | tf_op jit(solution)/shard_map/ppermute | solution.py:472
  44.5 11.2 %collective-permute-start.17 = (bf16[1152,128]{1,0:T(8,128)(2,1)S(1)}, bf16[1152,128]{1,0:T(8,128)(2,1)}, u32[]{:S(2)}, u32[]{:S(2)}) collective-permute-start(bf16[1152,128]{1,0:T(8,128)(2,1)S(1)} %collective-permute-done.7.refs_10_), channel_id=1, source_target_pairs={{0,1},{1,2},{2,3},{3,4},{4,5},{5,6},{6,7},{7,0},{8,9},{9,10},{10,1... | collective-permute-start | bytes 884744 | tf_op jit(solution)/shard_map/ppermute | solution.py:472
  44.5 13.7 %collective-permute-start.20 = (bf16[1152,128]{1,0:T(8,128)(2,1)S(1)}, bf16[1152,128]{1,0:T(8,128)(2,1)}, u32[]{:S(2)}, u32[]{:S(2)}) collective-permute-start(bf16[1152,128]{1,0:T(8,128)(2,1)S(1)} %collective-permute-done.10.refs_13_), channel_id=1, source_target_pairs={{0,7},{1,0},{2,1},{3,2},{4,3},{5,4},{6,5},{7,6},{8,15},{9,8},{10,9... | collective-permute-start | bytes 884744 | tf_op jit(solution)/shard_map/ppermute | solution.py:472
  47.7 25.1 %collective-permute-start.18 = (bf16[1152,128]{1,0:T(8,128)(2,1)}, bf16[1152,128]{1,0:T(8,128)(2,1)}, u32[]{:S(2)}, u32[]{:S(2)}) collective-permute-start(bf16[1152,128]{1,0:T(8,128)(2,1)} %collective-permute-done.8.refs_11_), channel_id=1, source_target_pairs={{0,1},{1,2},{2,3},{3,4},{4,5},{5,6},{6,7},{7,0},{8,9},{9,10},{10,1... | collective-permute-start | bytes 884744 | tf_op jit(solution)/shard_map/ppermute | solution.py:472
  51.9 20.9 %collective-permute-start.19 = (bf16[1152,128]{1,0:T(8,128)(2,1)}, bf16[1152,128]{1,0:T(8,128)(2,1)}, u32[]{:S(2)}, u32[]{:S(2)}) collective-permute-start(bf16[1152,128]{1,0:T(8,128)(2,1)} %collective-permute-done.9.refs_12_), channel_id=1, source_target_pairs={{0,7},{1,0},{2,1},{3,2},{4,3},{5,4},{6,5},{7,6},{8,15},{9,8},{10,9... | collective-permute-start | bytes 884744 | tf_op jit(solution)/shard_map/ppermute | solution.py:472
  55.7 17.1 %collective-permute-start.21 = (bf16[1152,128]{1,0:T(8,128)(2,1)}, bf16[1152,128]{1,0:T(8,128)(2,1)}, u32[]{:S(2)}, u32[]{:S(2)}) collective-permute-start(bf16[1152,128]{1,0:T(8,128)(2,1)} %collective-permute-done.17.refs_4_.refs_14_), channel_id=1, source_target_pairs={{0,1},{1,2},{2,3},{3,4},{4,5},{5,6},{6,7},{7,0},{8,9},{9,10},{10,1... | collective-permute-start | bytes 884744 | tf_op jit(solution)/shard_map/ppermute | solution.py:472
  58.2 14.6 %collective-permute-start.22 = (bf16[1152,128]{1,0:T(8,128)(2,1)}, bf16[1152,128]{1,0:T(8,128)(2,1)}, u32[]{:S(2)}, u32[]{:S(2)}) collective-permute-start(bf16[1152,128]{1,0:T(8,128)(2,1)} %collective-permute-done.20.refs_7_.refs_17_), channel_id=1, source_target_pairs={{0,7},{1,0},{2,1},{3,2},{4,3},{5,4},{6,5},{7,6},{8,15},{9,8},{10,9... | collective-permute-start | bytes 884744 | tf_op jit(solution)/shard_map/ppermute | solution.py:472
  67.6 9.5 %collective-permute-start.11 = (bf16[5,128,128]{2,1,0:T(8,128)(2,1)}, bf16[5,128,128]{2,1,0:T(8,128)(2,1)}, u32[]{:S(2)}, u32[]{:S(2)}) collective-permute-start(bf16[5,128,128]{2,1,0:T(8,128)(2,1)} %get-tuple-element.41), channel_id=1, source_target_pairs={{0,32},{32,0},{1,33},{33,1},{2,34},{34,2},{3,35},{35,3},{4,36},{36... | collective-permute-start | bytes 491528 | tf_op jit(solution)/shard_map/ppermute | solution.py:476
  76.5 8.8 %collective-permute-start.23 = (bf16[4,128,128]{2,1,0:T(8,128)(2,1)S(1)}, bf16[4,128,128]{2,1,0:T(8,128)(2,1)S(1)}, u32[]{:S(2)}, u32[]{:S(2)}) collective-permute-start(bf16[4,128,128]{2,1,0:T(8,128)(2,1)S(1)} %shard_map.81), channel_id=1, source_target_pairs={{0,32},{32,0},{1,33},{33,1},{2,34},{34,2},{3,35},{35,3},{4,36},{36... | collective-permute-start | bytes 393224 | tf_op jit(solution)/shard_map/ppermute | solution.py:476
  95.9 15.4 %collective-permute-start.15 = (bf16[5,32,256]{2,1,0:T(8,128)(2,1)}, bf16[5,32,256]{2,1,0:T(8,128)(2,1)S(1)}, u32[]{:S(2)}, u32[]{:S(2)}) collective-permute-start(bf16[5,32,256]{2,1,0:T(8,128)(2,1)} %get-tuple-element.44), channel_id=1, source_target_pairs={{0,16},{8,24},{16,0},{24,8},{1,17},{9,25},{17,1},{25,9},{2,18},{10... | collective-permute-start | bytes 245768 | tf_op jit(solution)/shard_map/ppermute | solution.py:472
  96.8 14.6 %collective-permute-start.16 = (bf16[5,32,256]{2,1,0:T(8,128)(2,1)}, bf16[5,32,256]{2,1,0:T(8,128)(2,1)S(1)}, u32[]{:S(2)}, u32[]{:S(2)}) collective-permute-start(bf16[5,32,256]{2,1,0:T(8,128)(2,1)} %get-tuple-element.45), channel_id=1, source_target_pairs={{0,8},{8,16},{16,24},{24,0},{1,9},{9,17},{17,25},{25,1},{2,10},{10... | collective-permute-start | bytes 245768 | tf_op jit(solution)/shard_map/ppermute | solution.py:472
  100.1 13.7 %collective-permute-start.26 = (bf16[4,32,256]{2,1,0:T(8,128)(2,1)S(1)}, bf16[4,32,256]{2,1,0:T(8,128)(2,1)S(1)}, u32[]{:S(2)}, u32[]{:S(2)}) collective-permute-start(bf16[4,32,256]{2,1,0:T(8,128)(2,1)S(1)} %get-tuple-element.50), channel_id=1, source_target_pairs={{0,24},{8,0},{16,8},{24,16},{1,25},{9,1},{17,9},{25,17},{2,26},{10... | collective-permute-start | bytes 196616 | tf_op jit(solution)/shard_map/ppermute | solution.py:472
  102.7 11.1 %collective-permute-start.27 = (bf16[4,32,256]{2,1,0:T(8,128)(2,1)S(1)}, bf16[4,32,256]{2,1,0:T(8,128)(2,1)S(1)}, u32[]{:S(2)}, u32[]{:S(2)}) collective-permute-start(bf16[4,32,256]{2,1,0:T(8,128)(2,1)S(1)} %get-tuple-element.51), channel_id=1, source_target_pairs={{0,16},{8,24},{16,0},{24,8},{1,17},{9,25},{17,1},{25,9},{2,18},{10... | collective-permute-start | bytes 196616 | tf_op jit(solution)/shard_map/ppermute | solution.py:472
  104.3 9.6 %collective-permute-start.28 = (bf16[4,32,256]{2,1,0:T(8,128)(2,1)S(1)}, bf16[4,32,256]{2,1,0:T(8,128)(2,1)S(1)}, u32[]{:S(2)}, u32[]{:S(2)}) collective-permute-start(bf16[4,32,256]{2,1,0:T(8,128)(2,1)S(1)} %get-tuple-element.52), channel_id=1, source_target_pairs={{0,8},{8,16},{16,24},{24,0},{1,9},{9,17},{17,25},{25,1},{2,10},{10... | collective-permute-start | bytes 196616 | tf_op jit(solution)/shard_map/ppermute | solution.py:472
  (27 other events, 297.9 us)

commit v7 on v5

--- a/solution.py
+++ b/solution.py
@@ -85,7 +85,7 @@
 
 def gain_row(gain):
     wide = gain.astype(F32)
-    return jnp.concatenate([wide[i : i + 1] for i in range(8)], axis=1)
+    return jnp.concatenate([wide[i : i + 1] for i in range(gain.shape[0])], axis=1)
 
 
 def dispatch_kernel(place_ref, hidden_ref, gain_ref, pair_ref, table_ref, *outs):
@@ -146,7 +146,6 @@
         ),
         out_shape=[message] * NY
         + [jax.ShapeDtypeStruct((1, TOK), F32), jax.ShapeDtypeStruct((1,), jnp.int32)],
-        compiler_params=pltpu.CompilerParams(vmem_limit_bytes=WIDE_LIMIT),
         cost_estimate=pl.CostEstimate(
             flops=2 * NY * SLOTS * TOK * COLS, bytes_accessed=4_000_000, transcendentals=0
         ),
@@ -193,11 +192,9 @@
     part_rows = jnp.where(
         lax.broadcasted_iota(jnp.int32, (256, 256), 1) == source, 1.0, 0.0
     ).astype(BF16)
-    first = (part * pl.num_programs(0) + step) * (2 * tile)
     for b in range(0, 2 * tile, 512):
-        at = pl.multiple_of(first + b, 512)
         pair = jnp.concatenate(
-            [mixed_ref[pl.ds(at, 256), :], mixed_ref[pl.ds(at + 256, 256), :]], axis=1
+            [mixed_ref[b : b + 256], mixed_ref[b + 256 : b + 512]], axis=1
         )
         parted = jnp.dot(part_rows, pair, preferred_element_type=F32).astype(BF16)
         d = b // 2
@@ -218,19 +215,20 @@
 
 
 def base_projection(part, hidden, gain, weight, *begun):
-    tile = 1024
+    tile = 2048
     steps = DIM // tile // 2
     first = part * steps
+    sums = [pl.BlockSpec((TOK, 256), lambda k: (0, 0)), pl.BlockSpec((TOK, 128), lambda k: (0, 0))]
     return pl.pallas_call(
         functools.partial(base_kernel, part),
         grid=(steps,),
         in_specs=[
             pl.BlockSpec((TOK, tile), lambda k: (0, first + k)),
-            pl.BlockSpec((8, 128), lambda k: (first + k, 0)),
-            whole(),
+            pl.BlockSpec((tile // 128, 128), lambda k: (first + k, 0)),
+            pl.BlockSpec((2 * tile, 128), lambda k: (first + k, 0)),
         ]
-        + [whole()] * len(begun),
-        out_specs=[whole()] * 2,
+        + sums[: len(begun)],
+        out_specs=sums,
         out_shape=[
             jax.ShapeDtypeStruct((TOK, 256), F32),
             jax.ShapeDtypeStruct((TOK, 128), F32),

time: 115 us -> 111 us (0.965)
  Pallas kernels: 31.6 us -> 28.3 us
    pallas_call x2, Pallas kernels: 14.1 us -> 10.8 us  [base_projection(): pl.pallas_call(functools.partial(base_kernel, part), grid=(steps,), in_sp...]
  transfers between devices with their start and end apart: 29 -> 29, of which waited for: 9 -> 9; matrix products, arithmetic and copies ran while one was open for 2% -> 2% of each run, Pallas kernels for 26% -> 23%
where the time goes in v7:
time: 111 us
  starting transfers between devices  44.3 us (40%)
  waiting for transfers between devices  31 us (28%)
  Pallas kernels  28.3 us (25%)
  local copies, waits for them, and re-layouts  5.13 us (5%)
  other arithmetic  1.9 us (2%)
    ppermute x23, starting transfers between devices, shift(): return lax.ppermute(x, axis, [(i, (i + by) % size) for i in range(size)])  39.8 us
    ppermute x23, waiting for transfers between devices, shift(): return lax.ppermute(x, axis, [(i, (i + by) % size) for i in range(size)])  21.7 us
    pallas_call x2, Pallas kernels, base_projection(): pl.pallas_call(functools.partial(base_kernel, part), grid=(steps,), in_sp...  10.8 us
    ppermute x6, waiting for transfers between devices, pair_sum(): other = lax.ppermute(x, axis, [(i, i ^ flip) for i in range(size)])  9.26 us
    pallas_call x1, Pallas kernels, dispatch(): pl.pallas_call(dispatch_kernel, grid_spec=pltpu.PrefetchScalarGridSpec(nu...  4.84 us
    ppermute x6, starting transfers between devices, pair_sum(): other = lax.ppermute(x, axis, [(i, i ^ flip) for i in range(size)])  4.44 us
    unnamed x18, local copies, waits for them, and re-layouts  4.38 us
    pallas_call x1, Pallas kernels, down_early(): pl.pallas_call(down_early_kernel, in_specs=[scalars()] + [whole()] * (NY...  2.88 us
  transfers between devices with their start and end apart: 29, of which 9 were waited for; matrix products, arithmetic and copies ran while one was open for 2% of the time, Pallas kernels for 23%

profile of v7, /device:TPU:6, one launch (start us, length us, event | category | flops | bytes accessed | tf_op | source)
XLA Modules:
  0.0 110.8 jit_solution(12407805796742067127)
XLA Ops:
  0.0 1.9 %shard_map.77 = (bf16[1152,128]{1,0:T(8,128)(2,1)}, bf16[1152,128]{1,0:T(8,128)(2,1)}) custom-call(bf16[2,1024,128]{2,1,0:T(8,128)(2,1)} %down_ref.1, bf16[2,128,128]{2,1,0:T(8,128)(2,1)} %bitcast.13), custom_call_target="tpu_custom_call" | custom-call | bytes 1200000 | tf_op jit(solution)/shard_map/pallas_call | solution.py:75
  1.9 2.0 %collective-permute-start.3 = (bf16[1152,128]{1,0:T(8,128)(2,1)}, bf16[1152,128]{1,0:T(8,128)(2,1)S(1)}, u32[]{:S(2)}, u32[]{:S(2)}) collective-permute-start(bf16[1152,128]{1,0:T(8,128)(2,1)} %get-tuple-element.39.refs_4_), channel_id=1, source_target_pairs={{0,1},{1,2},{2,3},{3,4},{4,5},{5,6},{6,7},{7,0},{8,9},{9,10},{10,1... | collective-permute-start | bytes 884744 | tf_op jit(solution)/shard_map/ppermute | solution.py:464
  4.6 4.8 %shard_map.75 = (bf16[9,32,1024]{2,1,0:T(8,128)(2,1)}, bf16[9,32,1024]{2,1,0:T(8,128)(2,1)}, bf16[9,32,1024]{2,1,0:T(8,128)(2,1)}, bf16[9,32,1024]{2,1,0:T(8,128)(2,1)}, f32[1,448]{1,0:T(1,128)}, /*index=5*/s32[1]{0:T(128)}) custom-call(s32[3]{0:T(128)} %pad_add_fusion.place_ref, bf16[448,8192]{1,0:T(8,128)(2,1)} %hidden_ref.5, bf16[64,128]{1,0:T(8,128)(2,1)} %bitcast.10, ...), custom_call_target="tpu_custom_call" | custom-call | flops 1056964608 | bytes 4000000 | tf_op jit(solution)/shard_map/pallas_call | solution.py:133
  11.1 2.9 %collective-permute-start.1 = (bf16[9,32,1024]{2,1,0:T(8,128)(2,1)}, bf16[9,32,1024]{2,1,0:T(8,128)(2,1)S(1)}, u32[]{:S(2)}, u32[]{:S(2)}) collective-permute-start(bf16[9,32,1024]{2,1,0:T(8,128)(2,1)} %get-tuple-element.37), channel_id=1, source_target_pairs={{0,16},{8,24},{16,0},{24,8},{1,17},{9,25},{17,1},{25,9},{2,18},{10... | collective-permute-start | bytes 1769480 | tf_op jit(solution)/shard_map/ppermute | solution.py:464
  14.0 4.0 %collective-permute-start.6 = (bf16[1152,128]{1,0:T(8,128)(2,1)S(1)}, bf16[1152,128]{1,0:T(8,128)(2,1)S(1)}, u32[]{:S(2)}, u32[]{:S(2)}) collective-permute-start(bf16[1152,128]{1,0:T(8,128)(2,1)S(1)} %copy-done.3), channel_id=1, source_target_pairs={{0,7},{1,0},{2,1},{3,2},{4,3},{5,4},{6,5},{7,6},{8,15},{9,8},{10,9... | collective-permute-start | bytes 884744 | tf_op jit(solution)/shard_map/ppermute | solution.py:464
  17.9 3.2 %collective-permute-start.5 = (bf16[1152,128]{1,0:T(8,128)(2,1)S(1)}, bf16[1152,128]{1,0:T(8,128)(2,1)S(1)}, u32[]{:S(2)}, u32[]{:S(2)}) collective-permute-start(bf16[1152,128]{1,0:T(8,128)(2,1)S(1)} %copy-done.2), channel_id=1, source_target_pairs={{0,7},{1,0},{2,1},{3,2},{4,3},{5,4},{6,5},{7,6},{8,15},{9,8},{10,9... | collective-permute-start | bytes 884744 | tf_op jit(solution)/shard_map/ppermute | solution.py:464
  21.2 4.2 %collective-permute-done.6.refs_9_ = bf16[1152,128]{1,0:T(8,128)(2,1)S(1)} collective-permute-done((bf16[1152,128]{1,0:T(8,128)(2,1)S(1)}, bf16[1152,128]{1,0:T(8,128)(2,1)S(1)}, u32[]{:S(2)}, u32[]{:S(2)}) %collective-permute-start.6) | collective-permute-done | bytes 294944 | tf_op jit(solution)/shard_map/ppermute | solution.py:464
  29.0 2.6 %collective-permute-done.5.refs_8_ = bf16[1152,128]{1,0:T(8,128)(2,1)S(1)} collective-permute-done((bf16[1152,128]{1,0:T(8,128)(2,1)S(1)}, bf16[1152,128]{1,0:T(8,128)(2,1)S(1)}, u32[]{:S(2)}, u32[]{:S(2)}) %collective-permute-start.5) | collective-permute-done | bytes 294944 | tf_op jit(solution)/shard_map/ppermute | solution.py:464
  33.2 6.4 %collective-permute-done.1.refs_2_ = bf16[9,32,1024]{2,1,0:T(8,128)(2,1)S(1)} collective-permute-done((bf16[9,32,1024]{2,1,0:T(8,128)(2,1)}, bf16[9,32,1024]{2,1,0:T(8,128)(2,1)S(1)}, u32[]{:S(2)}, u32[]{:S(2)}) %collective-permute-start.1) | collective-permute-done | bytes 589856 | tf_op jit(solution)/shard_map/ppermute | solution.py:464
  39.6 4.2 %collective-permute-start.9 = (bf16[1152,128]{1,0:T(8,128)(2,1)S(1)}, bf16[1152,128]{1,0:T(8,128)(2,1)S(1)}, u32[]{:S(2)}, u32[]{:S(2)}) collective-permute-start(bf16[1152,128]{1,0:T(8,128)(2,1)S(1)} %collective-permute-done.5.refs_8_), channel_id=1, source_target_pairs={{0,7},{1,0},{2,1},{3,2},{4,3},{5,4},{6,5},{7,6},{8,15},{9,8},{10,9... | collective-permute-start | bytes 884744 | tf_op jit(solution)/shard_map/ppermute | solution.py:464
  43.8 3.2 %collective-permute-start.20 = (bf16[1152,128]{1,0:T(8,128)(2,1)S(1)}, bf16[1152,128]{1,0:T(8,128)(2,1)S(1)}, u32[]{:S(2)}, u32[]{:S(2)}) collective-permute-start(bf16[1152,128]{1,0:T(8,128)(2,1)S(1)} %collective-permute-done.10.refs_13_), channel_id=1, source_target_pairs={{0,7},{1,0},{2,1},{3,2},{4,3},{5,4},{6,5},{7,6},{8,15},{9,8},{10,9... | collective-permute-start | bytes 884744 | tf_op jit(solution)/shard_map/ppermute | solution.py:464
  47.1 4.1 %collective-permute-done.9.refs_12_ = bf16[1152,128]{1,0:T(8,128)(2,1)S(1)} collective-permute-done((bf16[1152,128]{1,0:T(8,128)(2,1)S(1)}, bf16[1152,128]{1,0:T(8,128)(2,1)S(1)}, u32[]{:S(2)}, u32[]{:S(2)}) %collective-permute-start.9) | collective-permute-done | bytes 294944 | tf_op jit(solution)/shard_map/ppermute | solution.py:464
  51.2 3.7 %collective-permute-start.19 = (bf16[1152,128]{1,0:T(8,128)(2,1)S(1)}, bf16[1152,128]{1,0:T(8,128)(2,1)}, u32[]{:S(2)}, u32[]{:S(2)}) collective-permute-start(bf16[1152,128]{1,0:T(8,128)(2,1)S(1)} %collective-permute-done.9.refs_12_), channel_id=1, source_target_pairs={{0,7},{1,0},{2,1},{3,2},{4,3},{5,4},{6,5},{7,6},{8,15},{9,8},{10,9... | collective-permute-start | bytes 884744 | tf_op jit(solution)/shard_map/ppermute | solution.py:464
  54.9 2.6 %collective-permute-done.20.refs_7_.refs_17_ = bf16[1152,128]{1,0:T(8,128)(2,1)S(1)} collective-permute-done((bf16[1152,128]{1,0:T(8,128)(2,1)S(1)}, bf16[1152,128]{1,0:T(8,128)(2,1)S(1)}, u32[]{:S(2)}, u32[]{:S(2)}) %collective-permute-start.20) | collective-permute-done | bytes 294944 | tf_op jit(solution)/shard_map/ppermute | solution.py:464
  57.5 3.7 %collective-permute-start.22 = (bf16[1152,128]{1,0:T(8,128)(2,1)S(1)}, bf16[1152,128]{1,0:T(8,128)(2,1)}, u32[]{:S(2)}, u32[]{:S(2)}) collective-permute-start(bf16[1152,128]{1,0:T(8,128)(2,1)S(1)} %collective-permute-done.20.refs_7_.refs_17_), channel_id=1, source_target_pairs={{0,7},{1,0},{2,1},{3,2},{4,3},{5,4},{6,5},{7,6},{8,15},{9,8},{10,9... | collective-permute-start | bytes 884744 | tf_op jit(solution)/shard_map/ppermute | solution.py:464
  62.3 2.9 %shard_map.78 = (bf16[5,128,128]{2,1,0:T(8,128)(2,1)}, bf16[128,128]{1,0:T(8,128)(2,1)S(1)}) custom-call(s32[1]{0:T(128)} %get-tuple-element.34.hot_ref, bf16[9,32,1024]{2,1,0:T(8,128)(2,1)S(1)} %copy-done, bf16[9,32,1024]{2,1,0:T(8,128)(2,1)S(1)} %collective-permute-done.refs_1_, bf16[9,32,1024]{2,1,0:T(8,128)(2,1)S(1)} %collective-permute-done.1.refs_2_, ...), custom_call_target="tpu_custom_call" | custom-call | flops 335544320 | bytes 6000000 | tf_op jit(solution)/shard_map/pallas_call | solution.py:278
  65.8 5.2 %shard_map.73 = (f32[448,256]{1,0:T(8,128)}, f32[448,128]{1,0:T(8,128)}) custom-call(bf16[448,8192]{1,0:T(8,128)(2,1)} %hidden_ref.5, bf16[64,128]{1,0:T(8,128)(2,1)} %bitcast.11, bf16[16384,128]{1,0:T(8,128)(2,1)} %bitcast.8), custom_call_target="tpu_custom_call" | custom-call | flops 939524096 | bytes 6000000 | tf_op jit(solution)/shard_map/pallas_call | solution.py:222
  71.8 2.5 %shard_map.81 = bf16[4,128,128]{2,1,0:T(8,128)(2,1)S(1)} custom-call(s32[1]{0:T(128)} %get-tuple-element.34.hot_ref, bf16[9,32,1024]{2,1,0:T(8,128)(2,1)S(1)} %copy-done.1, bf16[9,32,1024]{2,1,0:T(8,128)(2,1)S(1)} %collective-permute-done.refs_1_, bf16[9,32,1024]{2,1,0:T(8,128)(2,1)S(1)} %collective-permute-done.1.refs_2_, ...), custom_call_target="tpu_custom_call" | custom-call | flops 268435456 | bytes 2000000 | tf_op jit(solution)/shard_map/pallas_call | solution.py:310
  76.9 1.9 %shard_map.82 = (bf16[3,256,256]{2,1,0:T(8,128)(2,1)S(1)}, bf16[4,128,256]{2,1,0:T(8,128)(2,1)S(1)}) custom-call(s32[1]{0:T(128)} %get-tuple-element.34.hot_ref, bf16[9,32,1024]{2,1,0:T(8,128)(2,1)S(1)} %copy-done.1, bf16[9,32,1024]{2,1,0:T(8,128)(2,1)S(1)} %collective-permute-done.refs_1_, bf16[9,32,1024]{2,1,0:T(8,128)(2,1)S(1)} %collective-permute-done.1.refs_2_, ...), custom_call_target="tpu_custom_call" | custom-call | flops 4000000 | bytes 1500000 | tf_op jit(solution)/shard_map/pallas_call | solution.py:386
  80.1 2.9 %collective-permute-done.12 = bf16[5,128,128]{2,1,0:T(8,128)(2,1)S(1)} collective-permute-done((bf16[5,128,128]{2,1,0:T(8,128)(2,1)S(1)}, bf16[5,128,128]{2,1,0:T(8,128)(2,1)S(1)}, u32[]{:S(2)}, u32[]{:S(2)}) %collective-permute-start.12) | collective-permute-done | bytes 163872 | tf_op jit(solution)/shard_map/ppermute | solution.py:468
  86.6 4.6 %collective-permute-done.13 = bf16[5,128,128]{2,1,0:T(8,128)(2,1)S(1)} collective-permute-done((bf16[5,128,128]{2,1,0:T(8,128)(2,1)S(1)}, bf16[5,128,128]{2,1,0:T(8,128)(2,1)S(1)}, u32[]{:S(2)}, u32[]{:S(2)}) %collective-permute-start.13) | collective-permute-done | bytes 163872 | tf_op jit(solution)/shard_map/ppermute | solution.py:468
  94.0 1.9 %shard_map.83 = (bf16[4,32,256]{2,1,0:T(8,128)(2,1)S(1)}, bf16[4,32,256]{2,1,0:T(8,128)(2,1)S(1)}, bf16[4,32,256]{2,1,0:T(8,128)(2,1)S(1)}, bf16[4,32,256]{2,1,0:T(8,128)(2,1)S(1)}) custom-call(s32[1]{0:T(128)} %get-tuple-element.34.hot_ref, bf16[4,128,128]{2,1,0:T(8,128)(2,1)S(1)} %add_convert_fusion.3.low_ref, ...), custom_call_target="tpu_custom_call" | custom-call | flops 67108864 | bytes 1000000 | tf_op jit(solution)/shard_map/pallas_call | solution.py:416
  95.9 2.6 %collective-permute-start.26 = (bf16[4,32,256]{2,1,0:T(8,128)(2,1)S(1)}, bf16[4,32,256]{2,1,0:T(8,128)(2,1)S(1)}, u32[]{:S(2)}, u32[]{:S(2)}) collective-permute-start(bf16[4,32,256]{2,1,0:T(8,128)(2,1)S(1)} %get-tuple-element.50), channel_id=1, source_target_pairs={{0,24},{8,0},{16,8},{24,16},{1,25},{9,1},{17,9},{25,17},{2,26},{10... | collective-permute-start | bytes 196616 | tf_op jit(solution)/shard_map/ppermute | solution.py:464
  101.4 5.6 %shard_map.74 = (f32[448,256]{1,0:T(8,128)}, f32[448,128]{1,0:T(8,128)}) custom-call(bf16[448,8192]{1,0:T(8,128)(2,1)} %hidden_ref.5, bf16[64,128]{1,0:T(8,128)(2,1)} %bitcast.12, bf16[16384,128]{1,0:T(8,128)(2,1)} %bitcast.9, f32[448,256]{1,0:T(8,128)} %get-tuple-element.29.refs_0_, f32[448,128]{1,0:T(8,128)} %get-tuple-element.30.refs_1_), custom_call_target="tpu_custom_call" | custom-call | flops 939524096 | bytes 6000000 | tf_op jit(solution)/shard_map/pallas_call | solution.py:222
  (72 shorter events, 26.8 us)
Async XLA Ops:
  1.9 16.0 %collective-permute-start.3 = (bf16[1152,128]{1,0:T(8,128)(2,1)}, bf16[1152,128]{1,0:T(8,128)(2,1)S(1)}, u32[]{:S(2)}, u32[]{:S(2)}) collective-permute-start(bf16[1152,128]{1,0:T(8,128)(2,1)} %get-tuple-element.39.refs_4_), channel_id=1, source_target_pairs={{0,1},{1,2},{2,3},{3,4},{4,5},{5,6},{6,7},{7,0},{8,9},{9,10},{10,1... | collective-permute-start | bytes 884744 | tf_op jit(solution)/shard_map/ppermute | solution.py:464
  9.4 23.6 %collective-permute-start = (bf16[9,32,1024]{2,1,0:T(8,128)(2,1)}, bf16[9,32,1024]{2,1,0:T(8,128)(2,1)S(1)}, u32[]{:S(2)}, u32[]{:S(2)}) collective-permute-start(bf16[9,32,1024]{2,1,0:T(8,128)(2,1)} %get-tuple-element.36), channel_id=1, source_target_pairs={{0,8},{8,16},{16,24},{24,0},{1,9},{9,17},{17,25},{25,1},{2,10},{10... | collective-permute-start | bytes 1769480 | tf_op jit(solution)/shard_map/ppermute | solution.py:464
  11.1 28.5 %collective-permute-start.1 = (bf16[9,32,1024]{2,1,0:T(8,128)(2,1)}, bf16[9,32,1024]{2,1,0:T(8,128)(2,1)S(1)}, u32[]{:S(2)}, u32[]{:S(2)}) collective-permute-start(bf16[9,32,1024]{2,1,0:T(8,128)(2,1)} %get-tuple-element.37), channel_id=1, source_target_pairs={{0,16},{8,24},{16,0},{24,8},{1,17},{9,25},{17,1},{25,9},{2,18},{10... | collective-permute-start | bytes 1769480 | tf_op jit(solution)/shard_map/ppermute | solution.py:464
  14.0 11.4 %collective-permute-start.6 = (bf16[1152,128]{1,0:T(8,128)(2,1)S(1)}, bf16[1152,128]{1,0:T(8,128)(2,1)S(1)}, u32[]{:S(2)}, u32[]{:S(2)}) collective-permute-start(bf16[1152,128]{1,0:T(8,128)(2,1)S(1)} %copy-done.3), channel_id=1, source_target_pairs={{0,7},{1,0},{2,1},{3,2},{4,3},{5,4},{6,5},{7,6},{8,15},{9,8},{10,9... | collective-permute-start | bytes 884744 | tf_op jit(solution)/shard_map/ppermute | solution.py:464
  17.9 9.6 %collective-permute-start.4 = (bf16[1152,128]{1,0:T(8,128)(2,1)S(1)}, bf16[1152,128]{1,0:T(8,128)(2,1)S(1)}, u32[]{:S(2)}, u32[]{:S(2)}) collective-permute-start(bf16[1152,128]{1,0:T(8,128)(2,1)S(1)} %copy-done.3), channel_id=1, source_target_pairs={{0,1},{1,2},{2,3},{3,4},{4,5},{5,6},{6,7},{7,0},{8,9},{9,10},{10,1... | collective-permute-start | bytes 884744 | tf_op jit(solution)/shard_map/ppermute | solution.py:464
  17.9 13.7 %collective-permute-start.5 = (bf16[1152,128]{1,0:T(8,128)(2,1)S(1)}, bf16[1152,128]{1,0:T(8,128)(2,1)S(1)}, u32[]{:S(2)}, u32[]{:S(2)}) collective-permute-start(bf16[1152,128]{1,0:T(8,128)(2,1)S(1)} %copy-done.2), channel_id=1, source_target_pairs={{0,7},{1,0},{2,1},{3,2},{4,3},{5,4},{6,5},{7,6},{8,15},{9,8},{10,9... | collective-permute-start | bytes 884744 | tf_op jit(solution)/shard_map/ppermute | solution.py:464
  25.3 18.5 %collective-permute-start.7 = (bf16[1152,128]{1,0:T(8,128)(2,1)S(1)}, bf16[1152,128]{1,0:T(8,128)(2,1)S(1)}, u32[]{:S(2)}, u32[]{:S(2)}) collective-permute-start(bf16[1152,128]{1,0:T(8,128)(2,1)S(1)} %collective-permute-done.3.refs_6_), channel_id=1, source_target_pairs={{0,1},{1,2},{2,3},{3,4},{4,5},{5,6},{6,7},{7,0},{8,9},{9,10},{10,1... | collective-permute-start | bytes 884744 | tf_op jit(solution)/shard_map/ppermute | solution.py:464
  27.5 16.3 %collective-permute-start.10 = (bf16[1152,128]{1,0:T(8,128)(2,1)S(1)}, bf16[1152,128]{1,0:T(8,128)(2,1)S(1)}, u32[]{:S(2)}, u32[]{:S(2)}) collective-permute-start(bf16[1152,128]{1,0:T(8,128)(2,1)S(1)} %collective-permute-done.6.refs_9_), channel_id=1, source_target_pairs={{0,7},{1,0},{2,1},{3,2},{4,3},{5,4},{6,5},{7,6},{8,15},{9,8},{10,9... | collective-permute-start | bytes 884744 | tf_op jit(solution)/shard_map/ppermute | solution.py:464
  31.7 29.6 %collective-permute-start.2 = (bf16[9,32,1024]{2,1,0:T(8,128)(2,1)}, bf16[9,32,1024]{2,1,0:T(8,128)(2,1)S(1)}, u32[]{:S(2)}, u32[]{:S(2)}) collective-permute-start(bf16[9,32,1024]{2,1,0:T(8,128)(2,1)} %get-tuple-element.38), channel_id=1, source_target_pairs={{0,24},{8,0},{16,8},{24,16},{1,25},{9,1},{17,9},{25,17},{2,26},{10... | collective-permute-start | bytes 1769480 | tf_op jit(solution)/shard_map/ppermute | solution.py:464
  33.0 14.1 %collective-permute-start.8 = (bf16[1152,128]{1,0:T(8,128)(2,1)S(1)}, bf16[1152,128]{1,0:T(8,128)(2,1)S(1)}, u32[]{:S(2)}, u32[]{:S(2)}) collective-permute-start(bf16[1152,128]{1,0:T(8,128)(2,1)S(1)} %collective-permute-done.4.refs_7_), channel_id=1, source_target_pairs={{0,1},{1,2},{2,3},{3,4},{4,5},{5,6},{6,7},{7,0},{8,9},{9,10},{10,1... | collective-permute-start | bytes 884744 | tf_op jit(solution)/shard_map/ppermute | solution.py:464
  39.6 11.6 %collective-permute-start.9 = (bf16[1152,128]{1,0:T(8,128)(2,1)S(1)}, bf16[1152,128]{1,0:T(8,128)(2,1)S(1)}, u32[]{:S(2)}, u32[]{:S(2)}) collective-permute-start(bf16[1152,128]{1,0:T(8,128)(2,1)S(1)} %collective-permute-done.5.refs_8_), channel_id=1, source_target_pairs={{0,7},{1,0},{2,1},{3,2},{4,3},{5,4},{6,5},{7,6},{8,15},{9,8},{10,9... | collective-permute-start | bytes 884744 | tf_op jit(solution)/shard_map/ppermute | solution.py:464
  43.8 11.1 %collective-permute-start.17 = (bf16[1152,128]{1,0:T(8,128)(2,1)S(1)}, bf16[1152,128]{1,0:T(8,128)(2,1)S(1)}, u32[]{:S(2)}, u32[]{:S(2)}) collective-permute-start(bf16[1152,128]{1,0:T(8,128)(2,1)S(1)} %collective-permute-done.7.refs_10_), channel_id=1, source_target_pairs={{0,1},{1,2},{2,3},{3,4},{4,5},{5,6},{6,7},{7,0},{8,9},{9,10},{10,1... | collective-permute-start | bytes 884744 | tf_op jit(solution)/shard_map/ppermute | solution.py:464
  43.8 13.7 %collective-permute-start.20 = (bf16[1152,128]{1,0:T(8,128)(2,1)S(1)}, bf16[1152,128]{1,0:T(8,128)(2,1)S(1)}, u32[]{:S(2)}, u32[]{:S(2)}) collective-permute-start(bf16[1152,128]{1,0:T(8,128)(2,1)S(1)} %collective-permute-done.10.refs_13_), channel_id=1, source_target_pairs={{0,7},{1,0},{2,1},{3,2},{4,3},{5,4},{6,5},{7,6},{8,15},{9,8},{10,9... | collective-permute-start | bytes 884744 | tf_op jit(solution)/shard_map/ppermute | solution.py:464
  47.1 23.9 %collective-permute-start.18 = (bf16[1152,128]{1,0:T(8,128)(2,1)S(1)}, bf16[1152,128]{1,0:T(8,128)(2,1)S(1)}, u32[]{:S(2)}, u32[]{:S(2)}) collective-permute-start(bf16[1152,128]{1,0:T(8,128)(2,1)S(1)} %collective-permute-done.8.refs_11_), channel_id=1, source_target_pairs={{0,1},{1,2},{2,3},{3,4},{4,5},{5,6},{6,7},{7,0},{8,9},{9,10},{10,1... | collective-permute-start | bytes 884744 | tf_op jit(solution)/shard_map/ppermute | solution.py:464
  51.2 19.8 %collective-permute-start.19 = (bf16[1152,128]{1,0:T(8,128)(2,1)S(1)}, bf16[1152,128]{1,0:T(8,128)(2,1)}, u32[]{:S(2)}, u32[]{:S(2)}) collective-permute-start(bf16[1152,128]{1,0:T(8,128)(2,1)S(1)} %collective-permute-done.9.refs_12_), channel_id=1, source_target_pairs={{0,7},{1,0},{2,1},{3,2},{4,3},{5,4},{6,5},{7,6},{8,15},{9,8},{10,9... | collective-permute-start | bytes 884744 | tf_op jit(solution)/shard_map/ppermute | solution.py:464
  54.9 16.1 %collective-permute-start.21 = (bf16[1152,128]{1,0:T(8,128)(2,1)S(1)}, bf16[1152,128]{1,0:T(8,128)(2,1)}, u32[]{:S(2)}, u32[]{:S(2)}) collective-permute-start(bf16[1152,128]{1,0:T(8,128)(2,1)S(1)} %collective-permute-done.17.refs_4_.refs_14_), channel_id=1, source_target_pairs={{0,1},{1,2},{2,3},{3,4},{4,5},{5,6},{6,7},{7,0},{8,9},{9,10},{10,1... | collective-permute-start | bytes 884744 | tf_op jit(solution)/shard_map/ppermute | solution.py:464
  57.5 13.5 %collective-permute-start.22 = (bf16[1152,128]{1,0:T(8,128)(2,1)S(1)}, bf16[1152,128]{1,0:T(8,128)(2,1)}, u32[]{:S(2)}, u32[]{:S(2)}) collective-permute-start(bf16[1152,128]{1,0:T(8,128)(2,1)S(1)} %collective-permute-done.20.refs_7_.refs_17_), channel_id=1, source_target_pairs={{0,7},{1,0},{2,1},{3,2},{4,3},{5,4},{6,5},{7,6},{8,15},{9,8},{10,9... | collective-permute-start | bytes 884744 | tf_op jit(solution)/shard_map/ppermute | solution.py:464
  65.8 9.1 %collective-permute-start.11 = (bf16[5,128,128]{2,1,0:T(8,128)(2,1)}, bf16[5,128,128]{2,1,0:T(8,128)(2,1)}, u32[]{:S(2)}, u32[]{:S(2)}) collective-permute-start(bf16[5,128,128]{2,1,0:T(8,128)(2,1)} %get-tuple-element.41), channel_id=1, source_target_pairs={{0,32},{32,0},{1,33},{33,1},{2,34},{34,2},{3,35},{35,3},{4,36},{36... | collective-permute-start | bytes 491528 | tf_op jit(solution)/shard_map/ppermute | solution.py:468
  85.0 8.9 %collective-permute-start.25 = (bf16[4,128,128]{2,1,0:T(8,128)(2,1)S(1)}, bf16[4,128,128]{2,1,0:T(8,128)(2,1)S(1)}, u32[]{:S(2)}, u32[]{:S(2)}) collective-permute-start(bf16[4,128,128]{2,1,0:T(8,128)(2,1)S(1)} %add_convert_fusion.4), channel_id=1, source_target_pairs={{0,192},{64,128},{128,64},{192,0},{1,193},{65,129},{129,65},{193,1... | collective-permute-start | bytes 393224 | tf_op jit(solution)/shard_map/ppermute | solution.py:468
  91.8 15.4 %collective-permute-start.15 = (bf16[5,32,256]{2,1,0:T(8,128)(2,1)S(1)}, bf16[5,32,256]{2,1,0:T(8,128)(2,1)S(1)}, u32[]{:S(2)}, u32[]{:S(2)}) collective-permute-start(bf16[5,32,256]{2,1,0:T(8,128)(2,1)S(1)} %get-tuple-element.44), channel_id=1, source_target_pairs={{0,16},{8,24},{16,0},{24,8},{1,17},{9,25},{17,1},{25,9},{2,18},{10... | collective-permute-start | bytes 245768 | tf_op jit(solution)/shard_map/ppermute | solution.py:464
  92.6 14.5 %collective-permute-start.16 = (bf16[5,32,256]{2,1,0:T(8,128)(2,1)S(1)}, bf16[5,32,256]{2,1,0:T(8,128)(2,1)S(1)}, u32[]{:S(2)}, u32[]{:S(2)}) collective-permute-start(bf16[5,32,256]{2,1,0:T(8,128)(2,1)S(1)} %get-tuple-element.45), channel_id=1, source_target_pairs={{0,8},{8,16},{16,24},{24,0},{1,9},{9,17},{17,25},{25,1},{2,10},{10... | collective-permute-start | bytes 245768 | tf_op jit(solution)/shard_map/ppermute | solution.py:464
  95.9 13.7 %collective-permute-start.26 = (bf16[4,32,256]{2,1,0:T(8,128)(2,1)S(1)}, bf16[4,32,256]{2,1,0:T(8,128)(2,1)S(1)}, u32[]{:S(2)}, u32[]{:S(2)}) collective-permute-start(bf16[4,32,256]{2,1,0:T(8,128)(2,1)S(1)} %get-tuple-element.50), channel_id=1, source_target_pairs={{0,24},{8,0},{16,8},{24,16},{1,25},{9,1},{17,9},{25,17},{2,26},{10... | collective-permute-start | bytes 196616 | tf_op jit(solution)/shard_map/ppermute | solution.py:464
  98.5 11.1 %collective-permute-start.27 = (bf16[4,32,256]{2,1,0:T(8,128)(2,1)S(1)}, bf16[4,32,256]{2,1,0:T(8,128)(2,1)S(1)}, u32[]{:S(2)}, u32[]{:S(2)}) collective-permute-start(bf16[4,32,256]{2,1,0:T(8,128)(2,1)S(1)} %get-tuple-element.51), channel_id=1, source_target_pairs={{0,16},{8,24},{16,0},{24,8},{1,17},{9,25},{17,1},{25,9},{2,18},{10... | collective-permute-start | bytes 196616 | tf_op jit(solution)/shard_map/ppermute | solution.py:464
  100.0 9.5 %collective-permute-start.28 = (bf16[4,32,256]{2,1,0:T(8,128)(2,1)S(1)}, bf16[4,32,256]{2,1,0:T(8,128)(2,1)S(1)}, u32[]{:S(2)}, u32[]{:S(2)}) collective-permute-start(bf16[4,32,256]{2,1,0:T(8,128)(2,1)S(1)} %get-tuple-element.52), channel_id=1, source_target_pairs={{0,8},{8,16},{16,24},{24,0},{1,9},{9,17},{17,25},{25,1},{2,10},{10... | collective-permute-start | bytes 196616 | tf_op jit(solution)/shard_map/ppermute | solution.py:464
  (14 other events, 90.6 us)

commit v8 on v7

--- a/solution.py
+++ b/solution.py
@@ -28,7 +28,7 @@
 RANK2 = 128
 CHUNK = COLS + RANK2
 VMEM_LIMIT = 20 * 1024 * 1024
-WIDE_LIMIT = 58 * 1024 * 1024
+WIDE_LIMIT = 56 * 1024 * 1024
 PACK_LIMIT = 66_200_000
 
 
@@ -57,27 +57,39 @@
     return pl.BlockSpec(memory_space=pltpu.HBM)
 
 
-def pack_kernel(down_ref, up_ref, zero_ref, one_ref, sems):
-    copies = []
+def pack_kernel(down_ref, up_ref, zero_ref, one_ref, stage_ref, sems):
+    moves = []
+    half = COLS // 2
     for a, out_ref in enumerate((zero_ref, one_ref)):
-        for src, dst in (
-            (down_ref.at[a], out_ref.at[pl.ds(0, COLS)]),
-            (up_ref.at[a], out_ref.at[pl.ds(COLS, RANK2)]),
+        for src, first, size in (
+            (down_ref.at[a, pl.ds(0, half)], 0, half),
+            (down_ref.at[a, pl.ds(half, half)], half, half),
+            (up_ref.at[a], COLS, RANK2),
         ):
-            copies.append(pltpu.make_async_copy(src, dst, sems.at[len(copies)]))
-    for copy in copies:
-        copy.start()
-    for copy in copies:
-        copy.wait()
+            n = len(moves)
+            stage = stage_ref.at[a, pl.ds(first, size)]
+            moves.append(
+                (
+                    pltpu.make_async_copy(src, stage, sems.at[0, n]),
+                    pltpu.make_async_copy(stage, out_ref.at[pl.ds(first, size)], sems.at[1, n]),
+                )
+            )
+    for fetch, _ in moves:
+        fetch.start()
+    for fetch, store in moves:
+        fetch.wait()
+        store.start()
+    for _, store in moves:
+        store.wait()
 
 
 def pack(down_weight, up_planes):
     return pl.pallas_call(
         pack_kernel,
         in_specs=[in_hbm()] * 2,
-        out_specs=[whole()] * 2,
+        out_specs=[in_hbm()] * 2,
         out_shape=[jax.ShapeDtypeStruct((CHUNK, 128), BF16)] * 2,
-        scratch_shapes=[pltpu.SemaphoreType.DMA((4,))],
+        scratch_shapes=[pltpu.VMEM((2, CHUNK, 128), BF16), pltpu.SemaphoreType.DMA((2, 6))],
         compiler_params=pltpu.CompilerParams(vmem_limit_bytes=PACK_LIMIT),
         cost_estimate=pl.CostEstimate(flops=0, bytes_accessed=1_200_000, transcendentals=0),
     )(down_weight, up_planes)
@@ -258,65 +270,66 @@
     return jnp.where(local < 0.5, both[:, :RANK2], both[:, RANK2:])
 
 
-def down_early_kernel(hot_ref, *refs):
+def down_kernel(first, count, hot_ref, *refs):
     received = refs[:NY]
-    chunks = refs[NY:-2]
+    chunks = refs[NY : NY + 2 * count]
+    begun = refs[NY + 2 * count : -2]
     low_ref, more_ref = refs[-2:]
-    more_ref[...] = jnp.zeros_like(more_ref)
-    for k in range(EARLY):
+    more_ref[...] = begun[0][...] if begun else jnp.zeros_like(more_ref)
+    for k in range(count):
         weight = jnp.concatenate([chunks[2 * k][:COLS], chunks[2 * k + 1][:COLS]], axis=1)
-        rows, local = bucket_rows(received, k)
+        rows, local = bucket_rows(received, first + k)
         low_ref[k] = project(rows, local, weight).astype(BF16)
 
-        @pl.when(hot_ref[0] == k)
+        @pl.when(hot_ref[0] == first + k)
         def _():
             rows, local = bucket_rows(received, NZ)
             more_ref[...] = project(rows, local, weight).astype(BF16)
 
 
-def down_early(hot, received, chunks):
-    return pl.pallas_call(
-        down_early_kernel,
-        in_specs=[scalars()] + [whole()] * (NY + len(chunks)),
+def down(first, hot, received, chunks, *begun):
+    count = len(chunks) // 2
+    return pl.pallas_call(
+        functools.partial(down_kernel, first, count),
+        in_specs=[scalars()] + [whole()] * (NY + len(chunks) + len(begun)),
         out_specs=[whole()] * 2,
         out_shape=[
-            jax.ShapeDtypeStruct((EARLY, NY * BLOCK, RANK2), BF16),
+            jax.ShapeDtypeStruct((count, NY * BLOCK, RANK2), BF16),
             jax.ShapeDtypeStruct((NY * BLOCK, RANK2), BF16),
         ],
         compiler_params=params(),
         cost_estimate=pl.CostEstimate(
-            flops=2 * EARLY * 128 * 1024 * 256, bytes_accessed=6_000_000, transcendentals=0
-        ),
-    )(hot, *received, *chunks)
-
-
-def down_late_kernel(hot_ref, *refs):
+            flops=2 * count * 128 * 1024 * 256, bytes_accessed=count * 1_000_000, transcendentals=0
+        ),
+    )(hot, *received, *chunks, *begun)
+
+
+def down_last_kernel(hot_ref, *refs):
     received = refs[:NY]
-    chunks = refs[NY:-2]
-    more_ref, low_ref = refs[-2:]
+    zero_ref, one_ref, before_ref, more_ref, low_ref = refs[NY:]
+    low_ref[: LATE - 2] = before_ref[...]
     low_ref[LATE - 1] = more_ref[...]
-    for at in range(LATE - 1):
-        weight = jnp.concatenate([chunks[2 * at][:COLS], chunks[2 * at + 1][:COLS]], axis=1)
-        rows, local = bucket_rows(received, EARLY + at)
-        low_ref[at] = project(rows, local, weight).astype(BF16)
-
-        @pl.when(hot_ref[0] == EARLY + at)
-        def _():
-            rows, local = bucket_rows(received, NZ)
-            low_ref[LATE - 1] = project(rows, local, weight).astype(BF16)
-
-
-def down_late(hot, received, chunks, more):
-    return pl.pallas_call(
-        down_late_kernel,
-        in_specs=[scalars()] + [whole()] * (NY + len(chunks) + 1),
+    weight = jnp.concatenate([zero_ref[:COLS], one_ref[:COLS]], axis=1)
+    rows, local = bucket_rows(received, NZ - 1)
+    low_ref[LATE - 2] = project(rows, local, weight).astype(BF16)
+
+    @pl.when(hot_ref[0] == NZ - 1)
+    def _():
+        rows, local = bucket_rows(received, NZ)
+        low_ref[LATE - 1] = project(rows, local, weight).astype(BF16)
+
+
+def down_last(hot, received, chunks, before, more):
+    return pl.pallas_call(
+        down_last_kernel,
+        in_specs=[scalars()] + [whole()] * (NY + 4),
         out_specs=whole(),
         out_shape=jax.ShapeDtypeStruct((LATE, NY * BLOCK, RANK2), BF16),
         compiler_params=params(),
         cost_estimate=pl.CostEstimate(
-            flops=2 * 512 * 1024 * 256, bytes_accessed=2_000_000, transcendentals=0
-        ),
-    )(hot, *received, *chunks, more)
+            flops=2 * 256 * 1024 * 256, bytes_accessed=1_000_000, transcendentals=0
+        ),
+    )(hot, *received, *chunks, before, more)
 
 
 def spread(low, local):
@@ -503,13 +516,14 @@
     base, inv = base_projection(0, hidden, gains, mixed)
     base, inv = base_projection(1, hidden, gains, mixed, base, inv)
 
-    low, more = down_early(hot, received, early)
+    low, more = down(0, hot, received, early)
     low = sum_over_tp(low)
     delta = up_early(low, received, early)
     back = [delta[0]] + [shift(delta[dy], "y", NY, -dy) for dy in range(1, NY)]
     summed = finish(finish_early_kernel, base, inv, dst, back, F32)
 
-    low = down_late(hot, received, late, more)
+    before, more = down(EARLY, hot, received, late[:-2], more)
+    low = down_last(hot, received, last, before, more)
     matrix, mask = up_prepare(hot, received, early + late[:-2])
     low = sum_over_tp(low)
     delta = up_late(hot, low, matrix, mask, last)

time: 111 us -> 107 us (0.964)
  Pallas kernels: 28.3 us -> 25.1 us
  local copies, waits for them, and re-layouts: 5.13 us -> 3.78 us
    unnamed x18 -> x14, local copies, waits for them, and re-layouts: 4.38 us -> 3.03 us
    pallas_call x3 -> x4, Pallas kernels: 7.3 us -> 6.17 us  [the longest x2 3.37 us: down(): pl.pallas_call(functools.partial(down_kernel, first, count), in_specs=[sc...]
  transfers between devices with their start and end apart: 29 -> 29, of which waited for: 9 -> 9; matrix products, arithmetic and copies ran while one was open for 2% -> 1% of each run, Pallas kernels for 23% -> 21%
where the time goes in v8:
time: 107 us
  starting transfers between devices  45.1 us (42%)
  waiting for transfers between devices  31.5 us (29%)
  Pallas kernels  25.1 us (23%)
  local copies, waits for them, and re-layouts  3.78 us (4%)
    ppermute x23, starting transfers between devices, shift(): return lax.ppermute(x, axis, [(i, (i + by) % size) for i in range(size)])  40 us
    ppermute x23, waiting for transfers between devices, shift(): return lax.ppermute(x, axis, [(i, (i + by) % size) for i in range(size)])  21.7 us
    pallas_call x2, Pallas kernels, base_projection(): pl.pallas_call(functools.partial(base_kernel, part), grid=(steps,), in_sp...  10.8 us
    ppermute x6, waiting for transfers between devices, pair_sum(): other = lax.ppermute(x, axis, [(i, i ^ flip) for i in range(size)])  9.78 us
    ppermute x6, starting transfers between devices, pair_sum(): other = lax.ppermute(x, axis, [(i, i ^ flip) for i in range(size)])  5.02 us
    pallas_call x1, Pallas kernels, dispatch(): pl.pallas_call(dispatch_kernel, grid_spec=pltpu.PrefetchScalarGridSpec(nu...  4.83 us
    pallas_call x2, Pallas kernels, down(): pl.pallas_call(functools.partial(down_kernel, first, count), in_specs=[sc...  3.37 us
    unnamed x14, local copies, waits for them, and re-layouts  3.03 us
  transfers between devices with their start and end apart: 29, of which 9 were waited for; matrix products, arithmetic and copies ran while one was open for 1% of the time, Pallas kernels for 21%

profile of v8, /device:TPU:6, one launch (start us, length us, event | category | flops | bytes accessed | tf_op | source)
XLA Modules:
  0.0 106.6 jit_solution(15833784548275990745)
XLA Ops:
  0.0 1.9 %shard_map.77 = (bf16[1152,128]{1,0:T(8,128)(2,1)}, bf16[1152,128]{1,0:T(8,128)(2,1)}) custom-call(bf16[2,1024,128]{2,1,0:T(8,128)(2,1)} %down_ref.1, bf16[2,128,128]{2,1,0:T(8,128)(2,1)} %bitcast.13), custom_call_target="tpu_custom_call" | custom-call | bytes 1200000 | tf_op jit(solution)/shard_map/pallas_call | solution.py:87
  1.9 2.0 %collective-permute-start.3 = (bf16[1152,128]{1,0:T(8,128)(2,1)}, bf16[1152,128]{1,0:T(8,128)(2,1)S(1)}, u32[]{:S(2)}, u32[]{:S(2)}) collective-permute-start(bf16[1152,128]{1,0:T(8,128)(2,1)} %get-tuple-element.41.refs_4_), channel_id=1, source_target_pairs={{0,1},{1,2},{2,3},{3,4},{4,5},{5,6},{6,7},{7,0},{8,9},{9,10},{10,1... | collective-permute-start | bytes 884744 | tf_op jit(solution)/shard_map/ppermute | solution.py:477
  4.5 4.8 %shard_map.75 = (bf16[9,32,1024]{2,1,0:T(8,128)(2,1)}, bf16[9,32,1024]{2,1,0:T(8,128)(2,1)}, bf16[9,32,1024]{2,1,0:T(8,128)(2,1)}, bf16[9,32,1024]{2,1,0:T(8,128)(2,1)}, f32[1,448]{1,0:T(1,128)}, /*index=5*/s32[1]{0:T(128)}) custom-call(s32[3]{0:T(128)} %pad_add_fusion.place_ref, bf16[448,8192]{1,0:T(8,128)(2,1)} %hidden_ref.5, bf16[64,128]{1,0:T(8,128)(2,1)} %bitcast.10, ...), custom_call_target="tpu_custom_call" | custom-call | flops 1056964608 | bytes 4000000 | tf_op jit(solution)/shard_map/pallas_call | solution.py:145
  9.3 1.7 %collective-permute-start = (bf16[9,32,1024]{2,1,0:T(8,128)(2,1)}, bf16[9,32,1024]{2,1,0:T(8,128)(2,1)S(1)}, u32[]{:S(2)}, u32[]{:S(2)}) collective-permute-start(bf16[9,32,1024]{2,1,0:T(8,128)(2,1)} %get-tuple-element.38), channel_id=1, source_target_pairs={{0,8},{8,16},{16,24},{24,0},{1,9},{9,17},{17,25},{25,1},{2,10},{10... | collective-permute-start | bytes 1769480 | tf_op jit(solution)/shard_map/ppermute | solution.py:477
  11.0 2.9 %collective-permute-start.1 = (bf16[9,32,1024]{2,1,0:T(8,128)(2,1)}, bf16[9,32,1024]{2,1,0:T(8,128)(2,1)S(1)}, u32[]{:S(2)}, u32[]{:S(2)}) collective-permute-start(bf16[9,32,1024]{2,1,0:T(8,128)(2,1)} %get-tuple-element.39), channel_id=1, source_target_pairs={{0,16},{8,24},{16,0},{24,8},{1,17},{9,25},{17,1},{25,9},{2,18},{10... | collective-permute-start | bytes 1769480 | tf_op jit(solution)/shard_map/ppermute | solution.py:477
  13.9 4.0 %collective-permute-start.6 = (bf16[1152,128]{1,0:T(8,128)(2,1)S(1)}, bf16[1152,128]{1,0:T(8,128)(2,1)S(1)}, u32[]{:S(2)}, u32[]{:S(2)}) collective-permute-start(bf16[1152,128]{1,0:T(8,128)(2,1)S(1)} %copy-done.3), channel_id=1, source_target_pairs={{0,7},{1,0},{2,1},{3,2},{4,3},{5,4},{6,5},{7,6},{8,15},{9,8},{10,9... | collective-permute-start | bytes 884744 | tf_op jit(solution)/shard_map/ppermute | solution.py:477
  17.9 3.2 %collective-permute-start.5 = (bf16[1152,128]{1,0:T(8,128)(2,1)S(1)}, bf16[1152,128]{1,0:T(8,128)(2,1)S(1)}, u32[]{:S(2)}, u32[]{:S(2)}) collective-permute-start(bf16[1152,128]{1,0:T(8,128)(2,1)S(1)} %copy-done.2), channel_id=1, source_target_pairs={{0,7},{1,0},{2,1},{3,2},{4,3},{5,4},{6,5},{7,6},{8,15},{9,8},{10,9... | collective-permute-start | bytes 884744 | tf_op jit(solution)/shard_map/ppermute | solution.py:477
  21.1 4.2 %collective-permute-done.6.refs_9_ = bf16[1152,128]{1,0:T(8,128)(2,1)S(1)} collective-permute-done((bf16[1152,128]{1,0:T(8,128)(2,1)S(1)}, bf16[1152,128]{1,0:T(8,128)(2,1)S(1)}, u32[]{:S(2)}, u32[]{:S(2)}) %collective-permute-start.6) | collective-permute-done | bytes 294944 | tf_op jit(solution)/shard_map/ppermute | solution.py:477
  25.7 1.7 %collective-permute-done.4.refs_7_ = bf16[1152,128]{1,0:T(8,128)(2,1)S(1)} collective-permute-done((bf16[1152,128]{1,0:T(8,128)(2,1)S(1)}, bf16[1152,128]{1,0:T(8,128)(2,1)S(1)}, u32[]{:S(2)}, u32[]{:S(2)}) %collective-permute-start.4) | collective-permute-done | bytes 294944 | tf_op jit(solution)/shard_map/ppermute | solution.py:477
  28.9 2.6 %collective-permute-done.5.refs_8_ = bf16[1152,128]{1,0:T(8,128)(2,1)S(1)} collective-permute-done((bf16[1152,128]{1,0:T(8,128)(2,1)S(1)}, bf16[1152,128]{1,0:T(8,128)(2,1)S(1)}, u32[]{:S(2)}, u32[]{:S(2)}) %collective-permute-start.5) | collective-permute-done | bytes 294944 | tf_op jit(solution)/shard_map/ppermute | solution.py:477
  33.1 6.4 %collective-permute-done.1.refs_2_ = bf16[9,32,1024]{2,1,0:T(8,128)(2,1)S(1)} collective-permute-done((bf16[9,32,1024]{2,1,0:T(8,128)(2,1)}, bf16[9,32,1024]{2,1,0:T(8,128)(2,1)S(1)}, u32[]{:S(2)}, u32[]{:S(2)}) %collective-permute-start.1) | collective-permute-done | bytes 589856 | tf_op jit(solution)/shard_map/ppermute | solution.py:477
  39.5 4.2 %collective-permute-start.9 = (bf16[1152,128]{1,0:T(8,128)(2,1)S(1)}, bf16[1152,128]{1,0:T(8,128)(2,1)S(1)}, u32[]{:S(2)}, u32[]{:S(2)}) collective-permute-start(bf16[1152,128]{1,0:T(8,128)(2,1)S(1)} %collective-permute-done.5.refs_8_), channel_id=1, source_target_pairs={{0,7},{1,0},{2,1},{3,2},{4,3},{5,4},{6,5},{7,6},{8,15},{9,8},{10,9... | collective-permute-start | bytes 884744 | tf_op jit(solution)/shard_map/ppermute | solution.py:477
  43.7 3.2 %collective-permute-start.19 = (bf16[1152,128]{1,0:T(8,128)(2,1)S(1)}, bf16[1152,128]{1,0:T(8,128)(2,1)S(1)}, u32[]{:S(2)}, u32[]{:S(2)}) collective-permute-start(bf16[1152,128]{1,0:T(8,128)(2,1)S(1)} %collective-permute-done.10.refs_13_), channel_id=1, source_target_pairs={{0,7},{1,0},{2,1},{3,2},{4,3},{5,4},{6,5},{7,6},{8,15},{9,8},{10,9... | collective-permute-start | bytes 884744 | tf_op jit(solution)/shard_map/ppermute | solution.py:477
  47.0 4.1 %collective-permute-done.9.refs_12_ = bf16[1152,128]{1,0:T(8,128)(2,1)S(1)} collective-permute-done((bf16[1152,128]{1,0:T(8,128)(2,1)S(1)}, bf16[1152,128]{1,0:T(8,128)(2,1)S(1)}, u32[]{:S(2)}, u32[]{:S(2)}) %collective-permute-start.9) | collective-permute-done | bytes 294944 | tf_op jit(solution)/shard_map/ppermute | solution.py:477
  51.1 3.7 %collective-permute-start.22 = (bf16[1152,128]{1,0:T(8,128)(2,1)S(1)}, bf16[1152,128]{1,0:T(8,128)(2,1)S(1)}, u32[]{:S(2)}, u32[]{:S(2)}) collective-permute-start(bf16[1152,128]{1,0:T(8,128)(2,1)S(1)} %collective-permute-done.9.refs_12_), channel_id=1, source_target_pairs={{0,7},{1,0},{2,1},{3,2},{4,3},{5,4},{6,5},{7,6},{8,15},{9,8},{10,9... | collective-permute-start | bytes 884744 | tf_op jit(solution)/shard_map/ppermute | solution.py:477
  54.8 2.6 %collective-permute-done.19.refs_7_.refs_17_ = bf16[1152,128]{1,0:T(8,128)(2,1)S(1)} collective-permute-done((bf16[1152,128]{1,0:T(8,128)(2,1)S(1)}, bf16[1152,128]{1,0:T(8,128)(2,1)S(1)}, u32[]{:S(2)}, u32[]{:S(2)}) %collective-permute-start.19) | collective-permute-done | bytes 294944 | tf_op jit(solution)/shard_map/ppermute | solution.py:477
  57.5 3.7 %collective-permute-start.20 = (bf16[1152,128]{1,0:T(8,128)(2,1)S(1)}, bf16[1152,128]{1,0:T(8,128)(2,1)S(1)}, u32[]{:S(2)}, u32[]{:S(2)}) collective-permute-start(bf16[1152,128]{1,0:T(8,128)(2,1)S(1)} %collective-permute-done.19.refs_7_.refs_17_), channel_id=1, source_target_pairs={{0,7},{1,0},{2,1},{3,2},{4,3},{5,4},{6,5},{7,6},{8,15},{9,8},{10,9... | collective-permute-start | bytes 884744 | tf_op jit(solution)/shard_map/ppermute | solution.py:477
  62.2 2.2 %shard_map.78 = (bf16[5,128,128]{2,1,0:T(8,128)(2,1)S(1)}, bf16[128,128]{1,0:T(8,128)(2,1)S(1)}) custom-call(s32[1]{0:T(128)} %get-tuple-element.36.hot_ref, bf16[9,32,1024]{2,1,0:T(8,128)(2,1)S(1)} %copy-done, bf16[9,32,1024]{2,1,0:T(8,128)(2,1)S(1)} %collective-permute-done.refs_1_, bf16[9,32,1024]{2,1,0:T(8,128)(2,1)S(1)} %collective-permute-done.1.refs_2_, ...), custom_call_target="tpu_custom_call" | custom-call | flops 335544320 | bytes 5000000 | tf_op jit(solution)/shard_map/pallas_call | solution.py:292
  64.5 5.2 %shard_map.73 = (f32[448,256]{1,0:T(8,128)}, f32[448,128]{1,0:T(8,128)}) custom-call(bf16[448,8192]{1,0:T(8,128)(2,1)} %hidden_ref.5, bf16[64,128]{1,0:T(8,128)(2,1)} %bitcast.11, bf16[16384,128]{1,0:T(8,128)(2,1)} %bitcast.8), custom_call_target="tpu_custom_call" | custom-call | flops 939524096 | bytes 6000000 | tf_op jit(solution)/shard_map/pallas_call | solution.py:234
  75.7 4.0 %collective-permute-done.12 = bf16[5,128,128]{2,1,0:T(8,128)(2,1)S(1)} collective-permute-done((bf16[5,128,128]{2,1,0:T(8,128)(2,1)S(1)}, bf16[5,128,128]{2,1,0:T(8,128)(2,1)S(1)}, u32[]{:S(2)}, u32[]{:S(2)}) %collective-permute-start.12) | collective-permute-done | bytes 163872 | tf_op jit(solution)/shard_map/ppermute | solution.py:481
  81.6 1.6 %collective-permute-start.25 = (bf16[4,128,128]{2,1,0:T(8,128)(2,1)S(1)}, bf16[4,128,128]{2,1,0:T(8,128)(2,1)S(1)}, u32[]{:S(2)}, u32[]{:S(2)}) collective-permute-start(bf16[4,128,128]{2,1,0:T(8,128)(2,1)S(1)} %add_convert_fusion.4), channel_id=1, source_target_pairs={{0,192},{64,128},{128,64},{192,0},{1,193},{65,129},{129,65},{193,1... | collective-permute-start | bytes 393224 | tf_op jit(solution)/shard_map/ppermute | solution.py:481
  83.1 4.6 %collective-permute-done.13 = bf16[5,128,128]{2,1,0:T(8,128)(2,1)S(1)} collective-permute-done((bf16[5,128,128]{2,1,0:T(8,128)(2,1)S(1)}, bf16[5,128,128]{2,1,0:T(8,128)(2,1)S(1)}, u32[]{:S(2)}, u32[]{:S(2)}) %collective-permute-start.13) | collective-permute-done | bytes 163872 | tf_op jit(solution)/shard_map/ppermute | solution.py:481
  91.4 2.8 %collective-permute-start.26 = (bf16[4,32,256]{2,1,0:T(8,128)(2,1)S(1)}, bf16[4,32,256]{2,1,0:T(8,128)(2,1)S(1)}, u32[]{:S(2)}, u32[]{:S(2)}) collective-permute-start(bf16[4,32,256]{2,1,0:T(8,128)(2,1)S(1)} %get-tuple-element.54), channel_id=1, source_target_pairs={{0,24},{8,0},{16,8},{24,16},{1,25},{9,1},{17,9},{25,17},{2,26},{10... | collective-permute-start | bytes 196616 | tf_op jit(solution)/shard_map/ppermute | solution.py:477
  97.1 5.6 %shard_map.74 = (f32[448,256]{1,0:T(8,128)}, f32[448,128]{1,0:T(8,128)}) custom-call(bf16[448,8192]{1,0:T(8,128)(2,1)} %hidden_ref.5, bf16[64,128]{1,0:T(8,128)(2,1)} %bitcast.12, bf16[16384,128]{1,0:T(8,128)(2,1)} %bitcast.9, f32[448,256]{1,0:T(8,128)} %get-tuple-element.31.refs_0_, f32[448,128]{1,0:T(8,128)} %get-tuple-element.32.refs_1_), custom_call_target="tpu_custom_call" | custom-call | flops 939524096 | bytes 6000000 | tf_op jit(solution)/shard_map/pallas_call | solution.py:234
  (69 shorter events, 23.4 us)
Async XLA Ops:
  1.9 15.9 %collective-permute-start.3 = (bf16[1152,128]{1,0:T(8,128)(2,1)}, bf16[1152,128]{1,0:T(8,128)(2,1)S(1)}, u32[]{:S(2)}, u32[]{:S(2)}) collective-permute-start(bf16[1152,128]{1,0:T(8,128)(2,1)} %get-tuple-element.41.refs_4_), channel_id=1, source_target_pairs={{0,1},{1,2},{2,3},{3,4},{4,5},{5,6},{6,7},{7,0},{8,9},{9,10},{10,1... | collective-permute-start | bytes 884744 | tf_op jit(solution)/shard_map/ppermute | solution.py:477
  9.3 23.6 %collective-permute-start = (bf16[9,32,1024]{2,1,0:T(8,128)(2,1)}, bf16[9,32,1024]{2,1,0:T(8,128)(2,1)S(1)}, u32[]{:S(2)}, u32[]{:S(2)}) collective-permute-start(bf16[9,32,1024]{2,1,0:T(8,128)(2,1)} %get-tuple-element.38), channel_id=1, source_target_pairs={{0,8},{8,16},{16,24},{24,0},{1,9},{9,17},{17,25},{25,1},{2,10},{10... | collective-permute-start | bytes 1769480 | tf_op jit(solution)/shard_map/ppermute | solution.py:477
  11.0 28.5 %collective-permute-start.1 = (bf16[9,32,1024]{2,1,0:T(8,128)(2,1)}, bf16[9,32,1024]{2,1,0:T(8,128)(2,1)S(1)}, u32[]{:S(2)}, u32[]{:S(2)}) collective-permute-start(bf16[9,32,1024]{2,1,0:T(8,128)(2,1)} %get-tuple-element.39), channel_id=1, source_target_pairs={{0,16},{8,24},{16,0},{24,8},{1,17},{9,25},{17,1},{25,9},{2,18},{10... | collective-permute-start | bytes 1769480 | tf_op jit(solution)/shard_map/ppermute | solution.py:477
  13.9 11.4 %collective-permute-start.6 = (bf16[1152,128]{1,0:T(8,128)(2,1)S(1)}, bf16[1152,128]{1,0:T(8,128)(2,1)S(1)}, u32[]{:S(2)}, u32[]{:S(2)}) collective-permute-start(bf16[1152,128]{1,0:T(8,128)(2,1)S(1)} %copy-done.3), channel_id=1, source_target_pairs={{0,7},{1,0},{2,1},{3,2},{4,3},{5,4},{6,5},{7,6},{8,15},{9,8},{10,9... | collective-permute-start | bytes 884744 | tf_op jit(solution)/shard_map/ppermute | solution.py:477
  17.8 9.6 %collective-permute-start.4 = (bf16[1152,128]{1,0:T(8,128)(2,1)S(1)}, bf16[1152,128]{1,0:T(8,128)(2,1)S(1)}, u32[]{:S(2)}, u32[]{:S(2)}) collective-permute-start(bf16[1152,128]{1,0:T(8,128)(2,1)S(1)} %copy-done.3), channel_id=1, source_target_pairs={{0,1},{1,2},{2,3},{3,4},{4,5},{5,6},{6,7},{7,0},{8,9},{9,10},{10,1... | collective-permute-start | bytes 884744 | tf_op jit(solution)/shard_map/ppermute | solution.py:477
  17.9 13.7 %collective-permute-start.5 = (bf16[1152,128]{1,0:T(8,128)(2,1)S(1)}, bf16[1152,128]{1,0:T(8,128)(2,1)S(1)}, u32[]{:S(2)}, u32[]{:S(2)}) collective-permute-start(bf16[1152,128]{1,0:T(8,128)(2,1)S(1)} %copy-done.2), channel_id=1, source_target_pairs={{0,7},{1,0},{2,1},{3,2},{4,3},{5,4},{6,5},{7,6},{8,15},{9,8},{10,9... | collective-permute-start | bytes 884744 | tf_op jit(solution)/shard_map/ppermute | solution.py:477
  25.2 18.5 %collective-permute-start.7 = (bf16[1152,128]{1,0:T(8,128)(2,1)S(1)}, bf16[1152,128]{1,0:T(8,128)(2,1)S(1)}, u32[]{:S(2)}, u32[]{:S(2)}) collective-permute-start(bf16[1152,128]{1,0:T(8,128)(2,1)S(1)} %collective-permute-done.3.refs_6_), channel_id=1, source_target_pairs={{0,1},{1,2},{2,3},{3,4},{4,5},{5,6},{6,7},{7,0},{8,9},{9,10},{10,1... | collective-permute-start | bytes 884744 | tf_op jit(solution)/shard_map/ppermute | solution.py:477
  27.4 16.3 %collective-permute-start.10 = (bf16[1152,128]{1,0:T(8,128)(2,1)S(1)}, bf16[1152,128]{1,0:T(8,128)(2,1)S(1)}, u32[]{:S(2)}, u32[]{:S(2)}) collective-permute-start(bf16[1152,128]{1,0:T(8,128)(2,1)S(1)} %collective-permute-done.6.refs_9_), channel_id=1, source_target_pairs={{0,7},{1,0},{2,1},{3,2},{4,3},{5,4},{6,5},{7,6},{8,15},{9,8},{10,9... | collective-permute-start | bytes 884744 | tf_op jit(solution)/shard_map/ppermute | solution.py:477
  31.6 29.6 %collective-permute-start.2 = (bf16[9,32,1024]{2,1,0:T(8,128)(2,1)}, bf16[9,32,1024]{2,1,0:T(8,128)(2,1)S(1)}, u32[]{:S(2)}, u32[]{:S(2)}) collective-permute-start(bf16[9,32,1024]{2,1,0:T(8,128)(2,1)} %get-tuple-element.40), channel_id=1, source_target_pairs={{0,24},{8,0},{16,8},{24,16},{1,25},{9,1},{17,9},{25,17},{2,26},{10... | collective-permute-start | bytes 1769480 | tf_op jit(solution)/shard_map/ppermute | solution.py:477
  32.9 14.1 %collective-permute-start.8 = (bf16[1152,128]{1,0:T(8,128)(2,1)S(1)}, bf16[1152,128]{1,0:T(8,128)(2,1)S(1)}, u32[]{:S(2)}, u32[]{:S(2)}) collective-permute-start(bf16[1152,128]{1,0:T(8,128)(2,1)S(1)} %collective-permute-done.4.refs_7_), channel_id=1, source_target_pairs={{0,1},{1,2},{2,3},{3,4},{4,5},{5,6},{6,7},{7,0},{8,9},{9,10},{10,1... | collective-permute-start | bytes 884744 | tf_op jit(solution)/shard_map/ppermute | solution.py:477
  39.5 11.6 %collective-permute-start.9 = (bf16[1152,128]{1,0:T(8,128)(2,1)S(1)}, bf16[1152,128]{1,0:T(8,128)(2,1)S(1)}, u32[]{:S(2)}, u32[]{:S(2)}) collective-permute-start(bf16[1152,128]{1,0:T(8,128)(2,1)S(1)} %collective-permute-done.5.refs_8_), channel_id=1, source_target_pairs={{0,7},{1,0},{2,1},{3,2},{4,3},{5,4},{6,5},{7,6},{8,15},{9,8},{10,9... | collective-permute-start | bytes 884744 | tf_op jit(solution)/shard_map/ppermute | solution.py:477
  43.7 11.1 %collective-permute-start.17 = (bf16[1152,128]{1,0:T(8,128)(2,1)S(1)}, bf16[1152,128]{1,0:T(8,128)(2,1)S(1)}, u32[]{:S(2)}, u32[]{:S(2)}) collective-permute-start(bf16[1152,128]{1,0:T(8,128)(2,1)S(1)} %collective-permute-done.7.refs_10_), channel_id=1, source_target_pairs={{0,1},{1,2},{2,3},{3,4},{4,5},{5,6},{6,7},{7,0},{8,9},{9,10},{10,1... | collective-permute-start | bytes 884744 | tf_op jit(solution)/shard_map/ppermute | solution.py:477
  43.7 13.7 %collective-permute-start.19 = (bf16[1152,128]{1,0:T(8,128)(2,1)S(1)}, bf16[1152,128]{1,0:T(8,128)(2,1)S(1)}, u32[]{:S(2)}, u32[]{:S(2)}) collective-permute-start(bf16[1152,128]{1,0:T(8,128)(2,1)S(1)} %collective-permute-done.10.refs_13_), channel_id=1, source_target_pairs={{0,7},{1,0},{2,1},{3,2},{4,3},{5,4},{6,5},{7,6},{8,15},{9,8},{10,9... | collective-permute-start | bytes 884744 | tf_op jit(solution)/shard_map/ppermute | solution.py:477
  47.0 22.7 %collective-permute-start.21 = (bf16[1152,128]{1,0:T(8,128)(2,1)S(1)}, bf16[1152,128]{1,0:T(8,128)(2,1)S(1)}, u32[]{:S(2)}, u32[]{:S(2)}) collective-permute-start(bf16[1152,128]{1,0:T(8,128)(2,1)S(1)} %collective-permute-done.8.refs_11_), channel_id=1, source_target_pairs={{0,1},{1,2},{2,3},{3,4},{4,5},{5,6},{6,7},{7,0},{8,9},{9,10},{10,1... | collective-permute-start | bytes 884744 | tf_op jit(solution)/shard_map/ppermute | solution.py:477
  51.1 18.6 %collective-permute-start.22 = (bf16[1152,128]{1,0:T(8,128)(2,1)S(1)}, bf16[1152,128]{1,0:T(8,128)(2,1)S(1)}, u32[]{:S(2)}, u32[]{:S(2)}) collective-permute-start(bf16[1152,128]{1,0:T(8,128)(2,1)S(1)} %collective-permute-done.9.refs_12_), channel_id=1, source_target_pairs={{0,7},{1,0},{2,1},{3,2},{4,3},{5,4},{6,5},{7,6},{8,15},{9,8},{10,9... | collective-permute-start | bytes 884744 | tf_op jit(solution)/shard_map/ppermute | solution.py:477
  54.8 16.1 %collective-permute-start.18 = (bf16[1152,128]{1,0:T(8,128)(2,1)S(1)}, bf16[1152,128]{1,0:T(8,128)(2,1)S(1)}, u32[]{:S(2)}, u32[]{:S(2)}) collective-permute-start(bf16[1152,128]{1,0:T(8,128)(2,1)S(1)} %collective-permute-done.17.refs_4_.refs_14_), channel_id=1, source_target_pairs={{0,1},{1,2},{2,3},{3,4},{4,5},{5,6},{6,7},{7,0},{8,9},{9,10},{10,1... | collective-permute-start | bytes 884744 | tf_op jit(solution)/shard_map/ppermute | solution.py:477
  57.5 13.5 %collective-permute-start.20 = (bf16[1152,128]{1,0:T(8,128)(2,1)S(1)}, bf16[1152,128]{1,0:T(8,128)(2,1)S(1)}, u32[]{:S(2)}, u32[]{:S(2)}) collective-permute-start(bf16[1152,128]{1,0:T(8,128)(2,1)S(1)} %collective-permute-done.19.refs_7_.refs_17_), channel_id=1, source_target_pairs={{0,7},{1,0},{2,1},{3,2},{4,3},{5,4},{6,5},{7,6},{8,15},{9,8},{10,9... | collective-permute-start | bytes 884744 | tf_op jit(solution)/shard_map/ppermute | solution.py:477
  79.7 8.0 %collective-permute-start.13 = (bf16[5,128,128]{2,1,0:T(8,128)(2,1)S(1)}, bf16[5,128,128]{2,1,0:T(8,128)(2,1)S(1)}, u32[]{:S(2)}, u32[]{:S(2)}) collective-permute-start(bf16[5,128,128]{2,1,0:T(8,128)(2,1)S(1)} %add_convert_fusion.1), channel_id=1, source_target_pairs={{0,192},{64,128},{128,64},{192,0},{1,193},{65,129},{129,65},{193,1... | collective-permute-start | bytes 491528 | tf_op jit(solution)/shard_map/ppermute | solution.py:481
  81.6 8.9 %collective-permute-start.25 = (bf16[4,128,128]{2,1,0:T(8,128)(2,1)S(1)}, bf16[4,128,128]{2,1,0:T(8,128)(2,1)S(1)}, u32[]{:S(2)}, u32[]{:S(2)}) collective-permute-start(bf16[4,128,128]{2,1,0:T(8,128)(2,1)S(1)} %add_convert_fusion.4), channel_id=1, source_target_pairs={{0,192},{64,128},{128,64},{192,0},{1,193},{65,129},{129,65},{193,1... | collective-permute-start | bytes 393224 | tf_op jit(solution)/shard_map/ppermute | solution.py:481
  88.3 14.6 %collective-permute-start.15 = (bf16[5,32,256]{2,1,0:T(8,128)(2,1)S(1)}, bf16[5,32,256]{2,1,0:T(8,128)(2,1)S(1)}, u32[]{:S(2)}, u32[]{:S(2)}) collective-permute-start(bf16[5,32,256]{2,1,0:T(8,128)(2,1)S(1)} %get-tuple-element.46), channel_id=1, source_target_pairs={{0,16},{8,24},{16,0},{24,8},{1,17},{9,25},{17,1},{25,9},{2,18},{10... | collective-permute-start | bytes 245768 | tf_op jit(solution)/shard_map/ppermute | solution.py:477
  89.2 13.8 %collective-permute-start.16 = (bf16[5,32,256]{2,1,0:T(8,128)(2,1)S(1)}, bf16[5,32,256]{2,1,0:T(8,128)(2,1)S(1)}, u32[]{:S(2)}, u32[]{:S(2)}) collective-permute-start(bf16[5,32,256]{2,1,0:T(8,128)(2,1)S(1)} %get-tuple-element.47), channel_id=1, source_target_pairs={{0,8},{8,16},{16,24},{24,0},{1,9},{9,17},{17,25},{25,1},{2,10},{10... | collective-permute-start | bytes 245768 | tf_op jit(solution)/shard_map/ppermute | solution.py:477
  91.4 13.9 %collective-permute-start.26 = (bf16[4,32,256]{2,1,0:T(8,128)(2,1)S(1)}, bf16[4,32,256]{2,1,0:T(8,128)(2,1)S(1)}, u32[]{:S(2)}, u32[]{:S(2)}) collective-permute-start(bf16[4,32,256]{2,1,0:T(8,128)(2,1)S(1)} %get-tuple-element.54), channel_id=1, source_target_pairs={{0,24},{8,0},{16,8},{24,16},{1,25},{9,1},{17,9},{25,17},{2,26},{10... | collective-permute-start | bytes 196616 | tf_op jit(solution)/shard_map/ppermute | solution.py:477
  94.2 11.1 %collective-permute-start.27 = (bf16[4,32,256]{2,1,0:T(8,128)(2,1)S(1)}, bf16[4,32,256]{2,1,0:T(8,128)(2,1)S(1)}, u32[]{:S(2)}, u32[]{:S(2)}) collective-permute-start(bf16[4,32,256]{2,1,0:T(8,128)(2,1)S(1)} %get-tuple-element.55), channel_id=1, source_target_pairs={{0,16},{8,24},{16,0},{24,8},{1,17},{9,25},{17,1},{25,9},{2,18},{10... | collective-permute-start | bytes 196616 | tf_op jit(solution)/shard_map/ppermute | solution.py:477
  95.8 9.6 %collective-permute-start.28 = (bf16[4,32,256]{2,1,0:T(8,128)(2,1)S(1)}, bf16[4,32,256]{2,1,0:T(8,128)(2,1)S(1)}, u32[]{:S(2)}, u32[]{:S(2)}) collective-permute-start(bf16[4,32,256]{2,1,0:T(8,128)(2,1)S(1)} %get-tuple-element.56), channel_id=1, source_target_pairs={{0,8},{8,16},{16,24},{24,0},{1,9},{9,17},{17,25},{25,1},{2,10},{10... | collective-permute-start | bytes 196616 | tf_op jit(solution)/shard_map/ppermute | solution.py:477
  (12 other events, 85.3 us)
